TPU v7x, 32 devices: a whole 2x2x4 slice. The times are simulated.
32 devices in a mesh: batch: 16 (over z, y, x), mp: 2 (over core).
Axes of the slice: x: 2, y: 2, z: 4, core: 2. Of those that a mesh axis runs over, the one named last changes fastest.
Arguments:
- block_input_slots: bfloat16 [32768, 512], P('batch'), may hold values from -6 to 6
- memory: bfloat16 [16384, 512], P('batch'), may hold values from -6 to 6
- target_sentence_lengths: int32 [16, 32], P('batch'), may hold values from 1 to 1024, 2048 in all within a row
- source_lengths: int32 [16, 32], P('batch'), may hold values from 1 to 512, 1024 in all within a row
- self_qkv: bfloat16 [3, 512, 512], P(None, None, 'mp'), may hold values from -0.25 to 0.25
- self_out: bfloat16 [512, 512], P('mp'), may hold values from -0.75 to 0.75
- cross_query: bfloat16 [512, 512], P(None, 'mp'), may hold values from -0.25 to 0.25
- cross_kv: bfloat16 [2, 512, 512], P(None, None, 'mp'), may hold values from -0.25 to 0.25
- cross_out: bfloat16 [512, 512], P('mp'), may hold values from -0.75 to 0.75
- up_proj: bfloat16 [2048, 512], P('mp'), may hold values from -0.25 to 0.25
- down_proj: bfloat16 [2048, 512], P('mp'), may hold values from -0.125 to 0.125
- norm_gains: float32 [512, 3], replicated, may hold values from 0.1 to 1.9
- norm_biases: float32 [512, 3], replicated, may hold values from -3 to 3
- cotangent: bfloat16 [32768, 512], P(('batch', 'mp')), may hold values from -6 to 6
Outputs:
- layer_output: bfloat16 [32768, 512], P(('batch', 'mp'))
- input_grad: float32 [32768, 512], P(('batch', 'mp'))
- memory_grad: float32 [16384, 512], P(('batch', 'mp'))
- self_qkv_grad: float32 [3, 512, 512], P(None, None, 'mp')
- self_out_grad: float32 [512, 512], P('mp')
- cross_query_grad: float32 [512, 512], P(None, 'mp')
- cross_kv_grad: float32 [2, 512, 512], P(None, None, 'mp')
- cross_out_grad: float32 [512, 512], P('mp')
- up_proj_grad: float32 [2048, 512], P('mp')
- down_proj_grad: float32 [2048, 512], P('mp')
- gain_grad: float32 [512, 3], P('mp')
- bias_grad: float32 [512, 3], P('mp')
Inputs may be any that keep to these rules, and one draw needn't show every extreme that they name: `target_sentence_lengths`: in every row the 32 target lengths add up to 2048 and the longest is exactly 1024; sentence j of a row fills the slots right after those of sentences 0 to j-1. `source_lengths`: in every row the 32 source lengths add up to 1024 and the longest is exactly 512; source sentence j of a row pairs with target sentence j and fills the memory slots right after those of sentences 0 to j-1.
All inputs are finite; a program needn't handle non-finite values.
Results may differ from a plain program's by a relative error of at most 0.023.
Values may be sent and summed in bfloat16 or wider, within the bound.
A program may use at most 192 MiB of HBM per device.

v0:
```python
import jax
import jax.numpy as jnp
from jax import lax
from jax.sharding import PartitionSpec as P

DH = 64


def segment_labels(lengths, span_len):
    ends_at = jnp.cumsum(lengths, axis=-1)
    places = jnp.arange(span_len, dtype=jnp.int32)
    return jnp.sum((places[None, :, None] >= ends_at[:, None, :]).astype(jnp.int32), axis=-1)


def layer_norm(values, gain_vec, shift_vec):
    centre = values - jnp.mean(values, axis=-1, keepdims=True)
    spread = jnp.mean(centre * centre, axis=-1, keepdims=True)
    return centre * lax.rsqrt(spread + 1e-05) * gain_vec + shift_vec


def block_mask(query_seg, key_seg, first_row, causal):
    same_seg = query_seg[:, None] == key_seg[None, :]
    if causal:
        query_place = first_row + jnp.arange(query_seg.shape[0], dtype=jnp.int32)
        key_place = jnp.arange(key_seg.shape[0], dtype=jnp.int32)
        same_seg = jnp.logical_and(same_seg, query_place[:, None] >= key_place[None, :])
    return same_seg


def attend_forward(query, keys, values, query_seg, key_seg, causal):
    row_count, length, head_count, head_size = query.shape
    block_len = min(512, length)
    score_scale = head_size ** (-0.5)

    def per_row(row_items):
        query_row, keys_row, values_row, qseg_row, kseg_row = row_items

        def per_block(block_index):
            first_row = block_index * block_len
            query_blk = lax.dynamic_slice_in_dim(query_row, first_row, block_len, 0)
            seg_blk = lax.dynamic_slice_in_dim(qseg_row, first_row, block_len, 0)
            key_mask = block_mask(seg_blk, kseg_row, first_row, causal)
            scores = (
                jnp.einsum("qhe,khe->hqk", query_blk, keys_row, preferred_element_type=jnp.float32)
                * score_scale
            )
            scores = jnp.where(key_mask[None], scores, -1e30)
            row_top = jnp.max(scores, axis=-1, keepdims=True)
            exp_scores = jnp.exp(scores - row_top)
            row_total = jnp.sum(exp_scores, axis=-1, keepdims=True)
            prob_low = (exp_scores / row_total).astype(jnp.bfloat16)
            context = jnp.einsum(
                "hqk,khe->qhe", prob_low, values_row, preferred_element_type=jnp.float32
            )
            return (context.astype(jnp.bfloat16), (row_top + jnp.log(row_total))[..., 0])

        context, log_total = lax.map(per_block, jnp.arange(length // block_len, dtype=jnp.int32))
        return (context.reshape(length, head_count, head_size), log_total)

    return lax.map(per_row, (query, keys, values, query_seg, key_seg))


def attend_backward(query, keys, values, query_seg, key_seg, causal, log_total, grad_ctx):
    row_count, length, head_count, head_size = query.shape
    block_len = min(512, length)
    score_scale = head_size ** (-0.5)

    def per_row(row_items):
        query_row, keys_row, values_row, qseg_row, kseg_row, total_row, grad_row = row_items

        def per_block(sums_kv, block_index):
            grad_keys, grad_values = sums_kv
            first_row = block_index * block_len
            query_blk = lax.dynamic_slice_in_dim(query_row, first_row, block_len, 0)
            seg_blk = lax.dynamic_slice_in_dim(qseg_row, first_row, block_len, 0)
            grad_blk = lax.dynamic_slice_in_dim(grad_row, first_row, block_len, 0)
            total_blk = total_row[block_index]
            key_mask = block_mask(seg_blk, kseg_row, first_row, causal)
            scores = (
                jnp.einsum("qhe,khe->hqk", query_blk, keys_row, preferred_element_type=jnp.float32)
                * score_scale
            )
            scores = jnp.where(key_mask[None], scores, -1e30)
            probs_full = jnp.exp(scores - total_blk[..., None])
            grad_prob = jnp.einsum(
                "qhe,khe->hqk", grad_blk, values_row, preferred_element_type=jnp.float32
            )
            delta_row = jnp.sum(probs_full * grad_prob, axis=-1, keepdims=True)
            grad_score = (probs_full * (grad_prob - delta_row)).astype(jnp.bfloat16)
            grad_query = (
                jnp.einsum("hqk,khe->qhe", grad_score, keys_row, preferred_element_type=jnp.float32)
                * score_scale
            )
            grad_keys = (
                grad_keys
                + jnp.einsum(
                    "hqk,qhe->khe", grad_score, query_blk, preferred_element_type=jnp.float32
                )
                * score_scale
            )
            grad_values = grad_values + jnp.einsum(
                "hqk,qhe->khe",
                probs_full.astype(jnp.bfloat16),
                grad_blk,
                preferred_element_type=jnp.float32,
            )
            return ((grad_keys, grad_values), grad_query)

        empty_kv = jnp.zeros(keys_row.shape, jnp.float32)
        (grad_keys, grad_values), grad_query = lax.scan(
            per_block, (empty_kv, empty_kv), jnp.arange(length // block_len, dtype=jnp.int32)
        )
        return (grad_query.reshape(length, head_count, head_size), grad_keys, grad_values)

    return lax.map(per_row, (query, keys, values, query_seg, key_seg, log_total, grad_ctx))


def shards(
    block_input_slots,
    memory,
    target_sentence_lengths,
    source_lengths,
    self_qkv,
    self_out,
    cross_query,
    cross_kv,
    cross_out,
    up_proj,
    down_proj,
    norm_gains,
    norm_biases,
    cotangent,
):
    row_count = target_sentence_lengths.shape[0]
    tokens = block_input_slots.shape[0]
    row_len = tokens // row_count
    mem_tokens = memory.shape[0]
    mem_len = mem_tokens // row_count
    share_len = cotangent.shape[0]
    first_row = lax.axis_index("mp") * share_len
    local_width = self_qkv.shape[2]
    head_count = local_width // DH
    target_segment = segment_labels(target_sentence_lengths, row_len)
    source_seg = segment_labels(source_lengths, mem_len)
    input_share = lax.dynamic_slice_in_dim(block_input_slots, first_row, share_len, 0).astype(
        jnp.float32
    )
    self_proj = jnp.einsum(
        "td,cdh->cth", block_input_slots, self_qkv, preferred_element_type=jnp.float32
    ).astype(jnp.bfloat16)
    self_rows = self_proj.reshape(3, row_count, row_len, head_count, DH)
    self_ctx, self_total = attend_forward(
        self_rows[0], self_rows[1], self_rows[2], target_segment, target_segment, True
    )
    self_ctx = self_ctx.reshape(tokens, local_width)
    sum_one = input_share + lax.psum_scatter(
        jnp.dot(self_ctx, self_out, preferred_element_type=jnp.float32),
        "mp",
        scatter_dimension=0,
        tiled=True,
    )
    normed_one_f, norm_back_one = jax.vjp(layer_norm, sum_one, norm_gains[:, 0], norm_biases[:, 0])
    normed_one = normed_one_f.astype(jnp.bfloat16)
    full_one = lax.all_gather(normed_one, "mp", axis=0, tiled=True)
    cross_q = jnp.dot(full_one, cross_query, preferred_element_type=jnp.float32).astype(
        jnp.bfloat16
    )
    cross_pair = jnp.einsum(
        "md,cdh->cmh", memory, cross_kv, preferred_element_type=jnp.float32
    ).astype(jnp.bfloat16)
    pair_rows = cross_pair.reshape(2, row_count, mem_len, head_count, DH)
    query_rows = cross_q.reshape(row_count, row_len, head_count, DH)
    cross_ctx, cross_total = attend_forward(
        query_rows, pair_rows[0], pair_rows[1], target_segment, source_seg, False
    )
    cross_ctx = cross_ctx.reshape(tokens, local_width)
    sum_two = normed_one.astype(jnp.float32) + lax.psum_scatter(
        jnp.dot(cross_ctx, cross_out, preferred_element_type=jnp.float32),
        "mp",
        scatter_dimension=0,
        tiled=True,
    )
    normed_two_f, norm_back_two = jax.vjp(layer_norm, sum_two, norm_gains[:, 1], norm_biases[:, 1])
    normed_two = normed_two_f.astype(jnp.bfloat16)
    full_two = lax.all_gather(normed_two, "mp", axis=0, tiled=True)
    pre_act = jnp.einsum("td,fd->tf", full_two, up_proj, preferred_element_type=jnp.float32)
    hidden_f, silu_back = jax.vjp(jax.nn.silu, pre_act)
    hidden = hidden_f.astype(jnp.bfloat16)
    ffn_sum = lax.psum_scatter(
        jnp.einsum("tf,fd->td", hidden, down_proj, preferred_element_type=jnp.float32).astype(
            jnp.bfloat16
        ),
        "mp",
        scatter_dimension=0,
        tiled=True,
    ).astype(jnp.float32)
    sum_three = normed_two.astype(jnp.float32) + ffn_sum
    out_value, norm_back_three = jax.vjp(layer_norm, sum_three, norm_gains[:, 2], norm_biases[:, 2])
    layer_output = out_value.astype(jnp.bfloat16)
    grad_three, gain_three, shift_three = norm_back_three(cotangent.astype(jnp.float32))
    grad_three_low = grad_three.astype(jnp.bfloat16)
    grad_three_full = lax.all_gather(grad_three_low, "mp", axis=0, tiled=True)
    grad_hidden = jnp.einsum(
        "td,fd->tf", grad_three_full, down_proj, preferred_element_type=jnp.float32
    )
    down_grad = jnp.einsum("tf,td->fd", hidden, grad_three_full, preferred_element_type=jnp.float32)
    grad_pre = silu_back(grad_hidden)[0].astype(jnp.bfloat16)
    up_grad = jnp.einsum("tf,td->fd", grad_pre, full_two, preferred_element_type=jnp.float32)
    grad_two_out = grad_three + lax.psum_scatter(
        jnp.einsum("tf,fd->td", grad_pre, up_proj, preferred_element_type=jnp.float32),
        "mp",
        scatter_dimension=0,
        tiled=True,
    )
    grad_two, gain_two, shift_two = norm_back_two(grad_two_out)
    grad_two_full = lax.all_gather(grad_two.astype(jnp.bfloat16), "mp", axis=0, tiled=True)
    grad_cross_ctx = jnp.einsum(
        "td,ed->te", grad_two_full, cross_out, preferred_element_type=jnp.float32
    ).astype(jnp.bfloat16)
    cross_out_grad = jnp.einsum(
        "te,td->ed", cross_ctx, grad_two_full, preferred_element_type=jnp.float32
    )
    grad_cq, grad_ck, grad_cv = attend_backward(
        query_rows,
        pair_rows[0],
        pair_rows[1],
        target_segment,
        source_seg,
        False,
        cross_total,
        grad_cross_ctx.reshape(row_count, row_len, head_count, DH),
    )
    grad_cq = grad_cq.reshape(tokens, local_width).astype(jnp.bfloat16)
    grad_pair = jnp.stack(
        [grad_ck.reshape(mem_tokens, local_width), grad_cv.reshape(mem_tokens, local_width)]
    ).astype(jnp.bfloat16)
    cross_query_grad = jnp.einsum(
        "td,te->de", full_one, grad_cq, preferred_element_type=jnp.float32
    )
    cross_kv_grad = jnp.einsum("md,cme->cde", memory, grad_pair, preferred_element_type=jnp.float32)
    memory_part = jnp.einsum("cme,cde->md", grad_pair, cross_kv, preferred_element_type=jnp.float32)
    grad_one_out = grad_two + lax.psum_scatter(
        jnp.einsum("te,de->td", grad_cq, cross_query, preferred_element_type=jnp.float32).astype(
            jnp.bfloat16
        ),
        "mp",
        scatter_dimension=0,
        tiled=True,
    ).astype(jnp.float32)
    grad_one, gain_one, shift_one = norm_back_one(grad_one_out)
    grad_one_full = lax.all_gather(grad_one.astype(jnp.bfloat16), "mp", axis=0, tiled=True)
    grad_self_ctx = jnp.einsum(
        "td,ed->te", grad_one_full, self_out, preferred_element_type=jnp.float32
    ).astype(jnp.bfloat16)
    self_out_grad = jnp.einsum(
        "te,td->ed", self_ctx, grad_one_full, preferred_element_type=jnp.float32
    )
    grad_sq, grad_sk, grad_sv = attend_backward(
        self_rows[0],
        self_rows[1],
        self_rows[2],
        target_segment,
        target_segment,
        True,
        self_total,
        grad_self_ctx.reshape(row_count, row_len, head_count, DH),
    )
    grad_proj = jnp.stack(
        [
            grad_sq.reshape(tokens, local_width),
            grad_sk.reshape(tokens, local_width),
            grad_sv.reshape(tokens, local_width),
        ]
    ).astype(jnp.bfloat16)
    self_qkv_grad = jnp.einsum(
        "td,cte->cde", block_input_slots, grad_proj, preferred_element_type=jnp.float32
    )
    input_part = jnp.einsum("cte,cde->td", grad_proj, self_qkv, preferred_element_type=jnp.float32)
    gain_part = jnp.stack([gain_one, gain_two, gain_three], axis=1)
    shift_part = jnp.stack([shift_one, shift_two, shift_three], axis=1)
    input_sum, memory_grad, gain_share, shift_share = (
        lax.psum_scatter(
            input_part.astype(jnp.bfloat16), "mp", scatter_dimension=0, tiled=True
        ).astype(jnp.float32),
        lax.psum_scatter(
            memory_part.astype(jnp.bfloat16), "mp", scatter_dimension=0, tiled=True
        ).astype(jnp.float32),
        lax.psum_scatter(
            gain_part.astype(jnp.bfloat16), "mp", scatter_dimension=0, tiled=True
        ).astype(jnp.float32),
        lax.psum_scatter(
            shift_part.astype(jnp.bfloat16), "mp", scatter_dimension=0, tiled=True
        ).astype(jnp.float32),
    )
    input_grad = input_sum + grad_one
    summed = (
        lax.psum(self_qkv_grad.astype(jnp.bfloat16), "batch").astype(jnp.float32),
        lax.psum(self_out_grad.astype(jnp.bfloat16), "batch").astype(jnp.float32),
        lax.psum(cross_query_grad.astype(jnp.bfloat16), "batch").astype(jnp.float32),
        lax.psum(cross_kv_grad.astype(jnp.bfloat16), "batch").astype(jnp.float32),
        lax.psum(cross_out_grad.astype(jnp.bfloat16), "batch").astype(jnp.float32),
        lax.psum(up_grad.astype(jnp.bfloat16), "batch").astype(jnp.float32),
        lax.psum(down_grad.astype(jnp.bfloat16), "batch").astype(jnp.float32),
        lax.psum(gain_share.astype(jnp.bfloat16), "batch").astype(jnp.float32),
        lax.psum(shift_share.astype(jnp.bfloat16), "batch").astype(jnp.float32),
    )
    return (
        layer_output,
        input_grad,
        memory_grad,
        summed[0],
        summed[1],
        summed[2],
        summed[3],
        summed[4],
        summed[5],
        summed[6],
        summed[7],
        summed[8],
    )


def solution(mesh):
    placed = (
        P("batch", None),
        P("batch", None),
        P("batch", None),
        P("batch", None),
        P(None, None, "mp"),
        P("mp", None),
        P(None, "mp"),
        P(None, None, "mp"),
        P("mp", None),
        P("mp", None),
        P("mp", None),
        P(),
        P(),
        P(("batch", "mp"), None),
    )
    return jax.shard_map(
        shards,
        mesh=mesh,
        in_specs=placed,
        out_specs=(
            P(("batch", "mp"), None),
            P(("batch", "mp"), None),
            P(("batch", "mp"), None),
            P(None, None, "mp"),
            P("mp", None),
            P(None, "mp"),
            P(None, None, "mp"),
            P("mp", None),
            P("mp", None),
            P("mp", None),
            P("mp", None),
            P("mp", None),
        ),
        check_vma=False,
    )
```

profile of v0, /device:TPU:0, one launch (start us, length us, event | category | flops | bytes accessed | tf_op | source)
XLA Modules:
  0.0 829.1 jit_solution(15711046235817125379)
XLA Ops:
  14.4 69.1 %while.96 = (s32[]{:T(128)}, bf16[4,512,4,64]{1,3,2,0:T(8,128)(2,1)}, f32[4,4,512]{2,1,0:T(4,128)S(1)}, s32[4]{0:T(128)S(1)}, s32[2048]{0:T(1024)S(1)}, /*index=...) while((s32[]{:T(128)}, ...), condition=%wide.region_5.6_spmd, body=%wide.region_2.0_spmd.sunk | while | flops 1127348736 | bytes 57231560 | solution.py:57
  91.6 14.2 %reduce-scatter.14.cloned.1.call-done = f32[1024,512]{1,0:T(8,128)} async-done(((f32[2048,512]{1,0:T(8,128)}), f32[1024,512]{1,0:T(8,128)}) %reduce-scatter.14.cloned.1.call-update) | async-done | bytes 2097168 | tf_op jit(solution)/shard_map/reduce_scatter | solution.py:156
  113.1 9.3 %all-gather.6.cloned.1.call-done = bf16[2048,512]{1,0:T(8,128)(2,1)} async-done(((bf16[1024,512]{1,0:T(8,128)(2,1)}), bf16[2048,512]{1,0:T(8,128)(2,1)}) %all-gather.6.cloned.1.call-update) | async-done | bytes 2097168 | tf_op jit(solution)/shard_map/all_gather | solution.py:164
  125.9 37.2 %while.97 = (s32[]{:T(128)}, bf16[4,512,4,64]{1,3,2,0:T(8,128)(2,1)}, f32[4,4,512]{2,1,0:T(4,128)S(1)}, s32[4]{0:T(128)S(1)}, s32[2048]{0:T(1024)S(1)}, /*index=...) while((s32[]{:T(128)}, ...), condition=%wide.region_14.15_spmd, body=%wide.region_11.14_spmd.sunk | while | flops 562690048 | bytes 28911824 | solution.py:57
  170.0 13.3 %reduce-scatter.16.cloned.1.call-done = f32[1024,512]{1,0:T(8,128)} async-done(((f32[2048,512]{1,0:T(8,128)}), f32[1024,512]{1,0:T(8,128)}) %reduce-scatter.16.cloned.1.call-update) | async-done | bytes 2097168 | tf_op jit(solution)/shard_map/reduce_scatter | solution.py:177
  188.3 11.8 %all-gather.8.cloned.1.call-done = bf16[2048,512]{1,0:T(8,128)(2,1)} async-done(((bf16[1024,512]{1,0:T(8,128)(2,1)}), bf16[2048,512]{1,0:T(8,128)(2,1)}) %all-gather.8.cloned.1.call-update) | async-done | bytes 2097168 | tf_op jit(solution)/shard_map/all_gather | solution.py:185
  200.1 7.4 multiply_convert_fusion.2
  213.2 10.9 %reduce-scatter.18.cloned.1.call-done = bf16[1024,512]{1,0:T(8,128)(2,1)} async-done(((bf16[2048,512]{1,0:T(8,128)(2,1)}), bf16[1024,512]{1,0:T(8,128)(2,1)}) %reduce-scatter.18.cloned.1.call-update) | async-done | bytes 1048592 | tf_op jit(solution)/shard_map/reduce_scatter | solution.py:189
  234.7 11.5 %all-gather.10.cloned.1.call-done = bf16[2048,512]{1,0:T(8,128)(2,1)} async-done(((bf16[1024,512]{1,0:T(8,128)(2,1)}), bf16[2048,512]{1,0:T(8,128)(2,1)}) %all-gather.10.cloned.1.call-update) | async-done | bytes 2097168 | tf_op jit(solution)/shard_map/all_gather | solution.py:202
  246.2 8.8 %fusion.78 = bf16[2048,1024]{1,0:T(8,128)(2,1)S(1)} fusion(f32[2048,1024]{1,0:T(8,128)} %get-tuple-element.667, bf16[2048,512]{1,0:T(8,128)(2,1)} %all-gather.10.cloned.1.call-done, bf16[1024,512]{1,0:T(8,128)(2,1)} %param.32), kind=kOutput, calls=%fused_computation.95 | convolution fusion | flops 2168455168 | bytes 15728640 | tf_op jit(solution)/shard_map/td,fd->tf/dot_general | solution.py:203
  261.4 13.3 %reduce-scatter.20.cloned.1.call-done = f32[1024,512]{1,0:T(8,128)} async-done(((f32[2048,512]{1,0:T(8,128)}), f32[1024,512]{1,0:T(8,128)}) %reduce-scatter.20.cloned.1.call-update) | async-done | bytes 2097168 | tf_op jit(solution)/shard_map/reduce_scatter | solution.py:209
  281.0 11.9 %all-gather.12.cloned.1.call-done = bf16[2048,512]{1,0:T(8,128)(2,1)} async-done(((bf16[1024,512]{1,0:T(8,128)(2,1)}), bf16[2048,512]{1,0:T(8,128)(2,1)}) %all-gather.12.cloned.1.call-update) | async-done | bytes 2097168 | tf_op jit(solution)/shard_map/all_gather | solution.py:216
  297.4 67.7 %while.98 = (s32[]{:T(128)}, f32[1024,4,64]{0,2,1:T(8,128)S(1)}, f32[1024,4,64]{0,2,1:T(8,128)}, bf16[4,512,4,64]{1,3,2,0:T(8,128)(2,1)}, s32[4]{0:T(128)S(1)}, ...) while((s32[]{:T(128)}, f32[1024,4,64]{0,2,1:T(8,128)S(1)}, ...), condition=%wide.region_28.29_spmd.clone, body=%wide.region_26.28_spmd.clone.sunk | while | flops 1375598592 | bytes 93391288 | solution.py:110
  370.6 10.9 %reduce-scatter.22.cloned.1.call-done = bf16[1024,512]{1,0:T(8,128)(2,1)} async-done(((bf16[2048,512]{1,0:T(8,128)(2,1)}), bf16[1024,512]{1,0:T(8,128)(2,1)}) %reduce-scatter.22.cloned.1.call-update) | async-done | bytes 1048592 | tf_op jit(solution)/shard_map/reduce_scatter | solution.py:242
  414.0 201.5 %while.99 = (s32[]{:T(128)}, f32[2048,4,64]{0,2,1:T(8,128)}, f32[2048,4,64]{0,2,1:T(8,128)}, bf16[4,512,4,64]{1,3,2,0:T(8,128)(2,1)}, s32[4]{0:T(128)S(1)}, /*in...) while((s32[]{:T(128)}, f32[2048,4,64]{0,2,1:T(8,128)}, ...), condition=%wide.region_34.35_spmd.clone, body=%wide.region_32.34_spmd.clone.sunk | while | flops 2753165824 | bytes 180988288 | solution.py:110
  423.1 7.2 fusion.241
  430.3 11.6 %multiply_reduce_fusion.12 = (f32[4,512]{1,0:T(4,128)}, f32[4,512,2048]{2,1,0:T(8,128)}) fusion(f32[4,512,2048]{2,1,0:T(8,128)S(1)} %fusion.238, f32[4,512]{1,0:T(4,128)} %copy-done.34, pred[512,2048]{1,0:T(8,128)(4,1)} %copy-done.5, bf16[2048,4,64]{0,2,1:T(8,128)(2,1)} %get-tuple-element.1096, bf16[2048,4,64]{0,2,1:T(8,128)(2,1)} %get-tuple-element.1095, ...), kind=kOutput, calls=%fused_computation.63.clone.1 | convolution fusion | flops 557840384 | bytes 35930116 | tf_op jit(solution)/shard_map/while/body/eval_jaxpr/while/body/eval_jaxpr/qhe,khe->hqk/dot_general | solution.py:85
  441.9 11.0 %multiply_convert_fusion.6 = bf16[4,512,2048]{2,1,0:T(8,128)(2,1)} fusion(f32[4,512,2048]{2,1,0:T(8,128)} %get-tuple-element.926, f32[4,512,2048]{2,1,0:T(8,128)S(1)} %fusion.238, f32[4,512]{1,0:T(4,128)} %get-tuple-element.927, f32[4,512]{1,0:T(4,128)} %copy-done.34, pred[512,2048]{1,0:T(8,128)(4,1)} %copy-done.5), kind=kLoop, calls=%fused_computation.62.clone.1 | loop fusion | flops 25165824 | bytes 43008000 | tf_op jit(solution)/shard_map/while/body/eval_jaxpr/while/body/eval_jaxpr/convert_element_type | solution.py:89
  453.0 6.9 fusion.242
  472.5 7.6 fusion.241
  480.1 11.6 %multiply_reduce_fusion.12 = (f32[4,512]{1,0:T(4,128)}, f32[4,512,2048]{2,1,0:T(8,128)}) fusion(f32[4,512,2048]{2,1,0:T(8,128)S(1)} %fusion.238, f32[4,512]{1,0:T(4,128)} %copy-done.34, pred[512,2048]{1,0:T(8,128)(4,1)} %copy-done.5, bf16[2048,4,64]{0,2,1:T(8,128)(2,1)} %get-tuple-element.1096, bf16[2048,4,64]{0,2,1:T(8,128)(2,1)} %get-tuple-element.1095, ...), kind=kOutput, calls=%fused_computation.63.clone.1 | convolution fusion | flops 557840384 | bytes 35930116 | tf_op jit(solution)/shard_map/while/body/eval_jaxpr/while/body/eval_jaxpr/qhe,khe->hqk/dot_general | solution.py:85
  491.7 11.0 %multiply_convert_fusion.6 = bf16[4,512,2048]{2,1,0:T(8,128)(2,1)} fusion(f32[4,512,2048]{2,1,0:T(8,128)} %get-tuple-element.926, f32[4,512,2048]{2,1,0:T(8,128)S(1)} %fusion.238, f32[4,512]{1,0:T(4,128)} %get-tuple-element.927, f32[4,512]{1,0:T(4,128)} %copy-done.34, pred[512,2048]{1,0:T(8,128)(4,1)} %copy-done.5), kind=kLoop, calls=%fused_computation.62.clone.1 | loop fusion | flops 25165824 | bytes 43008000 | tf_op jit(solution)/shard_map/while/body/eval_jaxpr/while/body/eval_jaxpr/convert_element_type | solution.py:89
  502.7 6.9 fusion.242
  523.0 7.6 fusion.241
  530.6 11.6 %multiply_reduce_fusion.12 = (f32[4,512]{1,0:T(4,128)}, f32[4,512,2048]{2,1,0:T(8,128)}) fusion(f32[4,512,2048]{2,1,0:T(8,128)S(1)} %fusion.238, f32[4,512]{1,0:T(4,128)} %copy-done.34, pred[512,2048]{1,0:T(8,128)(4,1)} %copy-done.5, bf16[2048,4,64]{0,2,1:T(8,128)(2,1)} %get-tuple-element.1096, bf16[2048,4,64]{0,2,1:T(8,128)(2,1)} %get-tuple-element.1095, ...), kind=kOutput, calls=%fused_computation.63.clone.1 | convolution fusion | flops 557840384 | bytes 35930116 | tf_op jit(solution)/shard_map/while/body/eval_jaxpr/while/body/eval_jaxpr/qhe,khe->hqk/dot_general | solution.py:85
  542.3 11.0 %multiply_convert_fusion.6 = bf16[4,512,2048]{2,1,0:T(8,128)(2,1)} fusion(f32[4,512,2048]{2,1,0:T(8,128)} %get-tuple-element.926, f32[4,512,2048]{2,1,0:T(8,128)S(1)} %fusion.238, f32[4,512]{1,0:T(4,128)} %get-tuple-element.927, f32[4,512]{1,0:T(4,128)} %copy-done.34, pred[512,2048]{1,0:T(8,128)(4,1)} %copy-done.5), kind=kLoop, calls=%fused_computation.62.clone.1 | loop fusion | flops 25165824 | bytes 43008000 | tf_op jit(solution)/shard_map/while/body/eval_jaxpr/while/body/eval_jaxpr/convert_element_type | solution.py:89
  553.3 6.9 fusion.242
  573.5 7.6 fusion.241
  581.2 11.6 %multiply_reduce_fusion.12 = (f32[4,512]{1,0:T(4,128)}, f32[4,512,2048]{2,1,0:T(8,128)}) fusion(f32[4,512,2048]{2,1,0:T(8,128)S(1)} %fusion.238, f32[4,512]{1,0:T(4,128)} %copy-done.34, pred[512,2048]{1,0:T(8,128)(4,1)} %copy-done.5, bf16[2048,4,64]{0,2,1:T(8,128)(2,1)} %get-tuple-element.1096, bf16[2048,4,64]{0,2,1:T(8,128)(2,1)} %get-tuple-element.1095, ...), kind=kOutput, calls=%fused_computation.63.clone.1 | convolution fusion | flops 557840384 | bytes 35930116 | tf_op jit(solution)/shard_map/while/body/eval_jaxpr/while/body/eval_jaxpr/qhe,khe->hqk/dot_general | solution.py:85
  592.8 11.0 %multiply_convert_fusion.6 = bf16[4,512,2048]{2,1,0:T(8,128)(2,1)} fusion(f32[4,512,2048]{2,1,0:T(8,128)} %get-tuple-element.926, f32[4,512,2048]{2,1,0:T(8,128)S(1)} %fusion.238, f32[4,512]{1,0:T(4,128)} %get-tuple-element.927, f32[4,512]{1,0:T(4,128)} %copy-done.34, pred[512,2048]{1,0:T(8,128)(4,1)} %copy-done.5), kind=kLoop, calls=%fused_computation.62.clone.1 | loop fusion | flops 25165824 | bytes 43008000 | tf_op jit(solution)/shard_map/while/body/eval_jaxpr/while/body/eval_jaxpr/convert_element_type | solution.py:89
  643.7 44.0 %all-reduce = (bf16[256,3]{0,1:T(4,128)(2,1)S(1)}, bf16[256,3]{0,1:T(4,128)(2,1)S(1)}) all-reduce(bf16[256,3]{0,1:T(4,128)(2,1)S(1)} %copy.88, bf16[256,3]{0,1:T(4,128)(2,1)S(1)} %copy.90), channel_id=1, replica_groups=mesh['batch'=16,'mp'=2] {'batch'}, use_global_device_ids=true, to_apply=%region_48.49 | all-reduce | flops 1536 | bytes 6144 | tf_op jit(solution)/shard_map/psum | solution.py:304
  688.9 118.5 %all-reduce.4.cloned.1.call-done = (bf16[3,512,256]{1,2,0:T(8,128)(2,1)}, bf16[2,512,256]{1,2,0:T(8,128)(2,1)}, bf16[256,512]{1,0:T(8,128)(2,1)}, bf16[512,256]{...) async-done(((bf16[3,512,256]{1,2,0:T(8,128)(2,1)}, bf16[2,512,256]{1,2,0:T(8,128)(2,1)}, ...) | async-done | bytes 4194320 | tf_op jit(solution)/shard_map/psum | solution.py:297
  (474 shorter events, 359.4 us)
Async XLA Ops:
  7.2 192.9 %copy-start = (bf16[1024,512]{1,0:T(8,128)(2,1)S(1)}, bf16[1024,512]{1,0:T(8,128)(2,1)}, u32[]{:S(2)}) copy-start(bf16[1024,512]{1,0:T(8,128)(2,1)} %param.31) | copy-start | bytes 3145732
  7.2 98.7 %reduce-scatter.14.cloned.1.call-start = ((), (), s32[]{:S(2)}) async-start(), calls=%async_computation.9 | async-start | bytes 6291456 | tf_op jit(solution)/shard_map/reduce_scatter | solution.py:156
  90.9 14.9 %copy-start.47 = (bf16[2048,512]{1,0:T(8,128)(2,1)S(1)}, bf16[2048,512]{1,0:T(8,128)(2,1)}, u32[]{:S(2)}) copy-start(bf16[2048,512]{1,0:T(8,128)(2,1)} %param.22) | copy-start | bytes 6291460
  90.9 31.5 %all-gather.6.cloned.1.call-start = ((), (), s32[]{:S(2)}) async-start(), calls=%async_computation.10 | async-start | bytes 3145728 | tf_op jit(solution)/shard_map/all_gather | solution.py:164
  91.6 91.7 %copy-start.56 = (f32[512,1]{0,1:T(1,128)}, f32[512,1]{0,1:T(1,128)S(1)}, u32[]{:S(2)}) copy-start(f32[512,1]{0,1:T(1,128)S(1)} %get-tuple-element.661) | copy-start | bytes 6148
  107.7 75.6 %copy-start.52 = (f32[1024]{0:T(1024)}, f32[1024]{0:T(1024)S(1)}, u32[]{:S(2)}) copy-start(f32[1024]{0:T(1024)S(1)} %broadcast_multiply_fusion.2) | copy-start | bytes 12292
  108.2 75.1 %copy-start.54 = (f32[1024]{0:T(1024)}, f32[1024]{0:T(1024)S(1)}, u32[]{:S(2)}) copy-start(f32[1024]{0:T(1024)S(1)} %fusion.99) | copy-start | bytes 12292
  110.4 72.9 %reduce-scatter.16.cloned.1.call-start = ((), (), s32[]{:S(2)}) async-start(), calls=%async_computation.11 | async-start | bytes 6291456 | tf_op jit(solution)/shard_map/reduce_scatter | solution.py:177
  111.0 11.5 %copy-start.43 = (bf16[512,256]{1,0:T(8,128)(2,1)S(1)}, bf16[512,256]{1,0:T(8,128)(2,1)}, u32[]{:S(2)}) copy-start(bf16[512,256]{1,0:T(8,128)(2,1)} %param.28) | copy-start | bytes 786436
  170.0 30.1 %all-gather.8.cloned.1.call-start = ((), (), s32[]{:S(2)}) async-start(), calls=%async_computation.12 | async-start | bytes 3145728 | tf_op jit(solution)/shard_map/all_gather | solution.py:185
  188.0 36.1 %reduce-scatter.18.cloned.1.call-start = ((), (), s32[]{:S(2)}) async-start(), calls=%async_computation.13 | async-start | bytes 3145728 | tf_op jit(solution)/shard_map/reduce_scatter | solution.py:189
  200.1 9.4 %copy-start.68 = (bf16[1024,512]{1,0:T(8,128)(2,1)S(1)}, bf16[1024,512]{1,0:T(8,128)(2,1)}, u32[]{:S(2)}) copy-start(bf16[1024,512]{1,0:T(8,128)(2,1)} %param.32) | copy-start | bytes 3145732
  213.2 33.0 %all-gather.10.cloned.1.call-start = ((), (), s32[]{:S(2)}) async-start(), calls=%async_computation.14 | async-start | bytes 3145728 | tf_op jit(solution)/shard_map/all_gather | solution.py:202
  234.3 40.5 %reduce-scatter.20.cloned.1.call-start = ((), (), s32[]{:S(2)}) async-start(), calls=%async_computation.15 | async-start | bytes 6291456 | tf_op jit(solution)/shard_map/reduce_scatter | solution.py:209
  261.4 31.6 %all-gather.12.cloned.1.call-start = ((), (), s32[]{:S(2)}) async-start(), calls=%async_computation.16 | async-start | bytes 3145728 | tf_op jit(solution)/shard_map/all_gather | solution.py:216
  280.9 100.6 %reduce-scatter.22.cloned.1.call-start = ((), (), s32[]{:S(2)}) async-start(), calls=%async_computation.17 | async-start | bytes 3145728 | tf_op jit(solution)/shard_map/reduce_scatter | solution.py:242
  281.0 16.4 %copy-start.7 = (bf16[1024,4,64]{0,2,1:T(8,128)(2,1)S(1)}, bf16[1024,4,64]{0,2,1:T(8,128)(2,1)}, u32[]{:S(2)}) copy-start(bf16[1024,4,64]{0,2,1:T(8,128)(2,1)} %copy-done.6) | copy-start | bytes 1572868
  281.0 16.3 %copy-start.15 = (bf16[2048,4,64]{0,2,1:T(8,128)(2,1)S(1)}, bf16[2048,4,64]{0,2,1:T(8,128)(2,1)}, u32[]{:S(2)}) copy-start(bf16[2048,4,64]{0,2,1:T(8,128)(2,1)} %copy-done.14) | copy-start | bytes 3145732
  281.0 16.3 %copy-start.17 = (bf16[1024,4,64]{0,2,1:T(8,128)(2,1)S(1)}, bf16[1024,4,64]{0,2,1:T(8,128)(2,1)}, u32[]{:S(2)}) copy-start(bf16[1024,4,64]{0,2,1:T(8,128)(2,1)} %copy-done.16) | copy-start | bytes 1572868
  368.4 13.1 %copy-start.10 = (f32[1024,512]{1,0:T(8,128)S(1)}, f32[1024,512]{1,0:T(8,128)}, u32[]{:S(2)}) copy-start(f32[1024,512]{1,0:T(8,128)} %copy-done.9) | copy-start | bytes 6291460
  368.4 13.1 %copy-start.53 = (f32[1024]{0:T(1024)S(1)}, f32[1024]{0:T(1024)}, u32[]{:S(2)}) copy-start(f32[1024]{0:T(1024)} %copy-done.52) | copy-start | bytes 12292
  368.4 13.1 %copy-start.55 = (f32[1024]{0:T(1024)S(1)}, f32[1024]{0:T(1024)}, u32[]{:S(2)}) copy-start(f32[1024]{0:T(1024)} %copy-done.54) | copy-start | bytes 12292
  368.4 13.1 %copy-start.57 = (f32[512,1]{0,1:T(1,128)S(1)}, f32[512,1]{0,1:T(1,128)}, u32[]{:S(2)}) copy-start(f32[512,1]{0,1:T(1,128)} %copy-done.56) | copy-start | bytes 6148
  370.6 14.0 %copy-start.59 = (f32[1024]{0:T(1024)S(1)}, f32[1024]{0:T(1024)}, u32[]{:S(2)}) copy-start(f32[1024]{0:T(1024)} %copy-done.58) | copy-start | bytes 12292
  370.6 38.7 %all-gather.14.cloned.1.call-start = ((), (), s32[]{:S(2)}) async-start(), calls=%async_computation.18 | async-start | bytes 3145728 | tf_op jit(solution)/shard_map/all_gather | solution.py:251
  388.6 251.1 %reduce-scatter.26.cloned.1.call-start = ((), (), s32[]{:S(2)}) async-start(), calls=%async_computation.20 | async-start | bytes 1572864 | tf_op jit(solution)/shard_map/reduce_scatter | solution.py:285
  392.0 249.8 %reduce-scatter.30.cloned.1.call-start = ((), (), s32[]{:S(2)}) async-start(), calls=%async_computation.22 | async-start | bytes 196608
  408.3 234.4 %reduce-scatter.28.cloned.1.call-start = ((), (), s32[]{:S(2)}) async-start(), calls=%async_computation.21 | async-start | bytes 196608
  409.2 398.2 %all-reduce.4.cloned.1.call-start = ((), (), s32[]{:S(2)}) async-start(), calls=%async_computation.23 | async-start | bytes 8388608 | tf_op jit(solution)/shard_map/psum | solution.py:297
  452.9 6.9 copy-start.2
  502.7 6.9 copy-start.2
  634.1 184.7 %reduce-scatter.24.cloned.1.call-start = ((), (), s32[]{:S(2)}) async-start(), calls=%async_computation.19 | async-start | bytes 3145728 | tf_op jit(solution)/shard_map/reduce_scatter | solution.py:282
  (83 other events, 219.4 us)
Sparse Core Ops, SparseCore 0:
  91.1 14.7 reduce-scatter.13
  110.6 11.8 all-gather.5
  170.1 13.1 reduce-scatter.15
  188.1 11.8 all-gather.7
  213.3 10.7 reduce-scatter.17
  234.4 11.7 all-gather.9
  261.5 13.1 reduce-scatter.19
  281.1 11.8 all-gather.11
  370.7 10.7 reduce-scatter.21
  388.7 11.7 all-gather.13
  402.8 9.6 reduce-scatter.25
  414.6 8.6 reduce-scatter.29
  425.5 8.6 reduce-scatter.27
  634.2 173.1 all-reduce.3
  810.1 8.4 reduce-scatter.23
where the time goes:
time: 839 us; the launch traced here: 829 us
  matrix products  309 us (37%)
  waiting for transfers between devices  226 us (27%)
  other arithmetic  138 us (16%)
  local copies, waits for them, and re-layouts  67.5 us (8%)
  blocking collectives  44 us (5%)
  loops' own time  27.5 us (3%)
  between operations  15 us (2%)
    psum x1, waiting for transfers between devices, shards(): lax.psum(self_qkv_grad.astype(jnp.bfloat16), 'batch').astype(jnp.float32)  119 us
    dot_general x8, matrix products, per_block(): jnp.einsum('qhe,khe->hqk', grad_blk, values_row, preferred_element_type=j...  59.1 us
    convert_element_type x8, other arithmetic, per_block(): grad_score = (probs_full * (grad_prob - delta_row)).astype(jnp.bfloat16)  53.6 us
    psum x1, blocking collectives, shards(): lax.psum(gain_share.astype(jnp.bfloat16), 'batch').astype(jnp.float32)  44 us
    dot_general x16, matrix products, per_block(): jnp.einsum('qhe,khe->hqk', query_blk, keys_row, preferred_element_type=jn...  43.9 us
    dot_general x8, matrix products, per_block(): jnp.einsum('hqk,qhe->khe', probs_full.astype(jnp.bfloat16), grad_blk, pre...  40.3 us
    dot_general x8, matrix products, per_block(): jnp.einsum('hqk,khe->qhe', prob_low, values_row, preferred_element_type=j...  38 us
    dot_general x8, matrix products, per_block(): jnp.einsum('hqk,khe->qhe', grad_score, keys_row, preferred_element_type=j...  33.2 us
  transfers between devices with their start and end apart: 15, of which 10 were waited for; matrix products, arithmetic and copies ran while one was open for 31% of the time, Pallas kernels for 0%

commit v1 on v0

v1 whole, which is shorter than its diff:
```python
import functools
import math

import jax
import jax.numpy as jnp
from jax import lax
from jax.experimental import pallas as pl
from jax.experimental.pallas import tpu as pltpu
from jax.sharding import PartitionSpec as P

DH = 64
NEG = -1e30
F32 = jnp.float32
BF16 = jnp.bfloat16
SCALE = DH**-0.5
SCALE2 = SCALE * math.log2(math.e)
NT = (((1,), (1,)), ((), ()))
NN = (((1,), (0,)), ((), ()))
TN = (((0,), (0,)), ((), ()))
VMEM_BYTES = 50 << 20


def mm(a, b, dims=NN):
    return lax.dot_general(a, b, dims, preferred_element_type=F32)


def params(semantics=("arbitrary",)):
    return pltpu.CompilerParams(dimension_semantics=semantics, vmem_limit_bytes=VMEM_BYTES)


def cost(flops, nbytes, exps=0):
    return pl.CostEstimate(flops=int(flops), bytes_accessed=int(nbytes), transcendentals=int(exps))


def pick(i, per_part, refs):
    value = refs[0][...]
    for r in range(1, len(refs)):
        value = jnp.where(i >= r * per_part, refs[r][...], value)
    return value


def part_map(r, per_part):
    return lambda i, sc: (jnp.clip(i - r * per_part, 0, per_part - 1), 0)


def attend_kernel(nblk, per_part, n_q, n_out, heads, bq, bk, sc, *refs):
    q_refs, refs = refs[:n_q], refs[n_q:]
    k_ref, v_ref, lo_ref, hi_ref = refs[:4]
    out_refs, (lse_ref, m_ref, l_ref, acc_ref) = refs[4 : 4 + n_out], refs[4 + n_out :]
    i = pl.program_id(0)
    q = pick(i, per_part, q_refs)
    lo = lo_ref[...]
    hi = hi_ref[...]
    m_ref[...] = jnp.full_like(m_ref, NEG)
    l_ref[...] = jnp.zeros_like(l_ref)
    acc_ref[...] = jnp.zeros_like(acc_ref)
    place = lax.broadcasted_iota(jnp.int32, (bk, bq), 0)

    def step(kb, carry):
        start = pl.multiple_of(kb * bk, bk)
        k = k_ref[pl.ds(start, bk), :]
        v = v_ref[pl.ds(start, bk), :]
        keep = jnp.logical_and(place >= lo - start, place < hi - start)
        for h in range(heads):
            cols = slice(h * DH, (h + 1) * DH)
            s = mm(k[:, cols], q[:, cols], NT) * SCALE2
            s = jnp.where(keep, s, NEG)
            m_old = m_ref[h : h + 1, :]
            m_new = jnp.maximum(m_old, jnp.max(s, axis=0, keepdims=True))
            p = jnp.exp2(s - m_new)
            decay = jnp.exp2(m_old - m_new)
            m_ref[h : h + 1, :] = m_new
            l_ref[h : h + 1, :] = l_ref[h : h + 1, :] * decay + jnp.sum(p, axis=0, keepdims=True)
            acc_ref[cols, :] = acc_ref[cols, :] * decay + mm(v[:, cols], p.astype(BF16), TN)
        return carry

    lax.fori_loop(sc[i], sc[nblk + i], step, 0)
    for h in range(heads):
        cols = slice(h * DH, (h + 1) * DH)
        acc_ref[cols, :] = acc_ref[cols, :] / l_ref[h : h + 1, :]
    ctx = acc_ref[...].T.astype(BF16)
    for r in range(n_out):

        @pl.when(jnp.logical_and(i >= r * per_part, i < (r + 1) * per_part))
        def _():
            out_refs[r][...] = ctx

    lse_ref[0, :, :] = m_ref[...] + jnp.log2(l_ref[...])


def attend(sc, q_parts, keys, values, lo, hi, mp, bq, bk):
    tokens, width = sum(q.shape[0] for q in q_parts), keys.shape[1]
    heads = width // DH
    nblk, per_part = tokens // bq, tokens // bq // mp
    if len(q_parts) == 1 and mp > 1:
        q_specs = [pl.BlockSpec((bq, width), lambda i, sc: (sc[2 * nblk + i], 0))]
    else:
        q_specs = [pl.BlockSpec((bq, width), part_map(r, per_part)) for r in range(mp)]
    full = pl.BlockSpec(keys.shape, lambda i, sc: (0, 0))
    row = pl.BlockSpec((1, bq), lambda i, sc: (0, i))
    per_pick = per_part if len(q_parts) > 1 else nblk
    outs = pl.pallas_call(
        functools.partial(attend_kernel, nblk, per_part, len(q_parts), mp, heads, bq, bk),
        grid_spec=pltpu.PrefetchScalarGridSpec(
            num_scalar_prefetch=1,
            grid=(nblk,),
            in_specs=q_specs + [full, full, row, row],
            out_specs=[pl.BlockSpec((bq, width), part_map(r, per_part)) for r in range(mp)]
            + [pl.BlockSpec((1, heads, bq), lambda i, sc: (i, 0, 0))],
            scratch_shapes=[
                pltpu.VMEM((heads, bq), F32),
                pltpu.VMEM((heads, bq), F32),
                pltpu.VMEM((width, bq), F32),
            ],
        ),
        out_shape=[jax.ShapeDtypeStruct((tokens // mp, width), BF16)] * mp
        + [jax.ShapeDtypeStruct((nblk, heads, bq), F32)],
        compiler_params=params(),
        cost_estimate=cost(4 * tokens * 512 * width, 8 * tokens * width, tokens * 512 * heads),
    )(sc, *q_parts, keys, values, lo, hi)
    return outs[:mp], outs[mp]


def attend_back_kernel(nblk, per_part, n_q, n_part, heads, bq, bk, sc, *refs):
    q_refs, refs = refs[:n_q], refs[n_q:]
    do_refs, refs = refs[:n_part], refs[n_part:]
    o_refs, refs = refs[:n_part], refs[n_part:]
    k_ref, v_ref, lo_ref, hi_ref, lse_ref = refs[:5]
    dq_refs, refs = refs[5 : 5 + n_q], refs[5 + n_q :]
    dk_ref, dv_ref, dk_acc, dv_acc, dq_acc, delta_ref = refs
    i = pl.program_id(0)

    @pl.when(i == 0)
    def _():
        dk_acc[...] = jnp.zeros_like(dk_acc)
        dv_acc[...] = jnp.zeros_like(dv_acc)

    q = pick(i, per_part, q_refs)
    do = pick(i, per_part, do_refs)
    o = pick(i, per_part, o_refs)
    lo = lo_ref[...]
    hi = hi_ref[...]
    prod = (do.astype(F32) * o.astype(F32)).T
    for h in range(heads):
        delta_ref[h : h + 1, :] = jnp.sum(prod[h * DH : (h + 1) * DH, :], axis=0, keepdims=True)
    dq_acc[...] = jnp.zeros_like(dq_acc)
    place = lax.broadcasted_iota(jnp.int32, (bk, bq), 0)

    def step(kb, carry):
        start = pl.multiple_of(kb * bk, bk)
        k = k_ref[pl.ds(start, bk), :]
        v = v_ref[pl.ds(start, bk), :]
        keep = jnp.logical_and(place >= lo - start, place < hi - start)
        dks, dvs = [], []
        for h in range(heads):
            cols = slice(h * DH, (h + 1) * DH)
            s = mm(k[:, cols], q[:, cols], NT) * SCALE2 - lse_ref[0, h : h + 1, :]
            p = jnp.where(keep, jnp.exp2(s), 0.0)
            dp = mm(v[:, cols], do[:, cols], NT)
            ds = (p * (dp - delta_ref[h : h + 1, :])).astype(BF16)
            dvs.append(mm(p.astype(BF16), do[:, cols]))
            dks.append(mm(ds, q[:, cols]))
            dq_acc[cols, :] += mm(k[:, cols], ds, TN)
        rows = pl.ds(start, bk)
        dk_acc[rows, :] += jnp.concatenate(dks, axis=1)
        dv_acc[rows, :] += jnp.concatenate(dvs, axis=1)
        return carry

    lax.fori_loop(sc[i], sc[nblk + i], step, 0)
    dq = (dq_acc[...] * SCALE).T.astype(BF16)
    if n_q == 1:
        dq_refs[0][...] = dq
    else:
        for r in range(n_q):

            @pl.when(jnp.logical_and(i >= r * per_part, i < (r + 1) * per_part))
            def _():
                dq_refs[r][...] = dq

    @pl.when(i == nblk - 1)
    def _():
        dk_ref[...] = (dk_acc[...] * SCALE).astype(BF16)
        dv_ref[...] = dv_acc[...].astype(BF16)


def attend_back(sc, q_parts, do_parts, o_parts, keys, values, lo, hi, lse, mp, bq, bk):
    tokens, width = sum(q.shape[0] for q in q_parts), keys.shape[1]
    heads = width // DH
    nblk, per_part = tokens // bq, tokens // bq // mp
    parts = [pl.BlockSpec((bq, width), part_map(r, per_part)) for r in range(mp)]
    if len(q_parts) == 1 and mp > 1:
        q_specs = [pl.BlockSpec((bq, width), lambda i, sc: (sc[2 * nblk + i], 0))]
    else:
        q_specs = parts
    full = pl.BlockSpec(keys.shape, lambda i, sc: (0, 0))
    row = pl.BlockSpec((1, bq), lambda i, sc: (0, i))
    outs = pl.pallas_call(
        functools.partial(attend_back_kernel, nblk, per_part, len(q_parts), mp, heads, bq, bk),
        grid_spec=pltpu.PrefetchScalarGridSpec(
            num_scalar_prefetch=1,
            grid=(nblk,),
            in_specs=q_specs
            + parts
            + parts
            + [full, full, row, row, pl.BlockSpec((1, heads, bq), lambda i, sc: (i, 0, 0))],
            out_specs=q_specs + [full, full],
            scratch_shapes=[
                pltpu.VMEM(keys.shape, F32),
                pltpu.VMEM(keys.shape, F32),
                pltpu.VMEM((width, bq), F32),
                pltpu.VMEM((heads, bq), F32),
            ],
        ),
        out_shape=[jax.ShapeDtypeStruct(q.shape, BF16) for q in q_parts]
        + [jax.ShapeDtypeStruct(keys.shape, BF16)] * 2,
        compiler_params=params(),
        cost_estimate=cost(10 * tokens * 512 * width, 12 * tokens * width, tokens * 512 * heads),
    )(sc, *q_parts, *do_parts, *o_parts, keys, values, lo, hi, lse)
    return outs[: len(q_parts)], outs[-2], outs[-1]


def norm_stats(a):
    centre = a - jnp.mean(a, axis=-1, keepdims=True)
    rstd = lax.rsqrt(jnp.mean(centre * centre, axis=-1, keepdims=True) + 1e-05)
    return centre * rstd, rstd


def norm_back(dy, xhat, rstd, gain):
    t = dy * gain
    mean_t = jnp.mean(t, axis=-1, keepdims=True)
    mean_tx = jnp.mean(t * xhat, axis=-1, keepdims=True)
    return rstd * (t - mean_t - xhat * mean_tx)


def post_self_kernel(mp, sc, *refs):
    x_ref = refs[0]
    ctx, wo, cq = refs[1 : 1 + mp], refs[1 + mp : 1 + 2 * mp], refs[1 + 2 * mp : 1 + 3 * mp]
    gain_ref, shift_ref = refs[1 + 3 * mp : 3 + 3 * mp]
    n1_ref, xhat_ref, rstd_ref = refs[3 + 3 * mp : 6 + 3 * mp]
    qc = refs[6 + 3 * mp :]
    a1 = x_ref[...].astype(F32)
    for r in range(mp):
        a1 += mm(ctx[r][...], wo[r][...])
    xhat, rstd = norm_stats(a1)
    n1 = (xhat * gain_ref[0:1, :] + shift_ref[0:1, :]).astype(BF16)
    n1_ref[...] = n1
    xhat_ref[...] = xhat
    rstd_ref[...] = rstd
    for r in range(mp):
        qc[r][...] = mm(n1, cq[r][...]).astype(BF16)


def whole(a):
    return pl.BlockSpec(a.shape, lambda i, sc: (0,) * a.ndim)


def rows_of(bt, width):
    return pl.BlockSpec((bt, width), lambda i, sc: (i, 0))


def post_self(sc, x, ctx, wo, cq, gain, shift, share, bt):
    mp, d = len(ctx), x.shape[1]
    width = ctx[0].shape[1]
    nb = share // bt
    outs = pl.pallas_call(
        functools.partial(post_self_kernel, mp),
        grid_spec=pltpu.PrefetchScalarGridSpec(
            num_scalar_prefetch=1,
            grid=(nb,),
            in_specs=[pl.BlockSpec((bt, d), lambda i, sc: (sc[0] * nb + i, 0))]
            + [rows_of(bt, width)] * mp
            + [whole(w) for w in (*wo, *cq, gain, shift)],
            out_specs=[rows_of(bt, d), rows_of(bt, d), rows_of(bt, 1)] + [rows_of(bt, width)] * mp,
        ),
        out_shape=[
            jax.ShapeDtypeStruct((share, d), BF16),
            jax.ShapeDtypeStruct((share, d), F32),
            jax.ShapeDtypeStruct((share, 1), F32),
        ]
        + [jax.ShapeDtypeStruct((share, width), BF16)] * mp,
        compiler_params=params(),
        cost_estimate=cost(4 * share * d * d, share * d * 12),
    )(sc, x, *ctx, *wo, *cq, gain, shift)
    return outs[0], outs[1], outs[2], outs[3:]


def middle_kernel(mp, *refs):
    refs = list(refs)

    def take(n):
        got = refs[:n]
        del refs[:n]
        return got

    cctx, (n1_ref, cot_ref) = take(mp), take(2)
    co, up, down = take(mp), take(mp), take(mp)
    gain_ref, shift_ref = take(2)
    out_ref, da2_ref, n2_ref, e3_ref, e2_ref = take(5)
    dcctx, hid, dpre = take(mp), take(mp), take(mp)
    (small_ref,) = take(1)
    (slope_ref,) = take(1)
    ff = up[0].shape[0]
    i = pl.program_id(0)

    a2 = n1_ref[...].astype(F32)
    for r in range(mp):
        a2 += mm(cctx[r][...], co[r][...])
    xhat2, rstd2 = norm_stats(a2)
    n2 = (xhat2 * gain_ref[1:2, :] + shift_ref[1:2, :]).astype(BF16)
    n2_ref[...] = n2
    a3 = n2.astype(F32)
    for r in range(mp):
        u = mm(n2, up[r][...], NT)
        sg = 1.0 / (1.0 + jnp.exp(-u))
        h = u * sg
        hid[r][...] = h.astype(BF16)
        slope_ref[:, r * ff : (r + 1) * ff] = sg + h * (1.0 - sg)
        a3 += mm(hid[r][...], down[r][...])
    xhat3, rstd3 = norm_stats(a3)
    out_ref[...] = (xhat3 * gain_ref[2:3, :] + shift_ref[2:3, :]).astype(BF16)
    g = cot_ref[...].astype(F32)
    da3 = norm_back(g, xhat3, rstd3, gain_ref[2:3, :])
    e3 = da3.astype(BF16)
    e3_ref[...] = e3
    dn2 = da3
    for r in range(mp):
        dh = mm(e3, down[r][...], NT)
        dpre[r][...] = (dh * slope_ref[:, r * ff : (r + 1) * ff]).astype(BF16)
        dn2 += mm(dpre[r][...], up[r][...])
    da2 = norm_back(dn2, xhat2, rstd2, gain_ref[1:2, :])
    da2_ref[...] = da2
    e2 = da2.astype(BF16)
    e2_ref[...] = e2
    for r in range(mp):
        dcctx[r][...] = mm(e2, co[r][...], NT).astype(BF16)
    sums = jnp.concatenate(
        [
            jnp.sum(dn2 * xhat2, axis=0, keepdims=True),
            jnp.sum(g * xhat3, axis=0, keepdims=True),
            jnp.sum(dn2, axis=0, keepdims=True),
            jnp.sum(g, axis=0, keepdims=True),
        ],
        axis=0,
    )

    @pl.when(i == 0)
    def _():
        small_ref[...] = sums

    @pl.when(i > 0)
    def _():
        small_ref[...] += sums


def middle(cctx, n1, cot, co, up, down, gain, shift, bt):
    mp = len(cctx)
    share, d = n1.shape
    width = cctx[0].shape[1]
    ff = up[0].shape[0]
    row = lambda w: pl.BlockSpec((bt, w), lambda i: (i, 0))
    all_of = lambda a: pl.BlockSpec(a.shape, lambda i: (0,) * a.ndim)
    shape = lambda w, t: jax.ShapeDtypeStruct((share, w), t)
    outs = pl.pallas_call(
        functools.partial(middle_kernel, mp),
        grid=(share // bt,),
        in_specs=[row(width)] * mp + [row(d)] * 2 + [all_of(w) for w in (*co, *up, *down, gain, shift)],
        out_specs=[row(d)] * 5
        + [row(width)] * mp
        + [row(ff)] * (2 * mp)
        + [pl.BlockSpec((4, d), lambda i: (0, 0))],
        scratch_shapes=[pltpu.VMEM((bt, ff * mp), F32)],
        out_shape=[shape(d, BF16), shape(d, F32), shape(d, BF16), shape(d, BF16), shape(d, BF16)]
        + [shape(width, BF16)] * mp
        + [shape(ff, BF16)] * (2 * mp)
        + [jax.ShapeDtypeStruct((4, d), F32)],
        compiler_params=params(),
        cost_estimate=cost(8 * share * d * ff * mp + 4 * share * d * d, share * ff * mp * 4, share * ff * mp),
    )(*cctx, n1, cot, *co, *up, *down, gain, shift)
    out, da2, n2, e3, e2 = outs[:5]
    return out, da2, n2, e3, e2, outs[5 : 5 + mp], outs[5 + mp : 5 + 2 * mp], outs[5 + 2 * mp : 5 + 3 * mp], outs[-1]


def pre_self_kernel(mp, *refs):
    dqc, cq, wo = refs[:mp], refs[mp : 2 * mp], refs[2 * mp : 3 * mp]
    da2_ref, xhat_ref, rstd_ref, gain_ref = refs[3 * mp : 3 * mp + 4]
    da1_ref, e1_ref = refs[3 * mp + 4 : 3 * mp + 6]
    dctx = refs[3 * mp + 6 : 4 * mp + 6]
    small_ref = refs[4 * mp + 6]
    i = pl.program_id(0)
    dn1 = da2_ref[...]
    for r in range(mp):
        dn1 += mm(dqc[r][...], cq[r][...], NT)
    xhat = xhat_ref[...]
    da1 = norm_back(dn1, xhat, rstd_ref[...], gain_ref[0:1, :])
    da1_ref[...] = da1
    e1 = da1.astype(BF16)
    e1_ref[...] = e1
    for r in range(mp):
        dctx[r][...] = mm(e1, wo[r][...], NT).astype(BF16)
    sums = jnp.concatenate(
        [jnp.sum(dn1 * xhat, axis=0, keepdims=True), jnp.sum(dn1, axis=0, keepdims=True)], axis=0
    )

    @pl.when(i == 0)
    def _():
        small_ref[...] = sums

    @pl.when(i > 0)
    def _():
        small_ref[...] += sums


def pre_self(dqc, cq, wo, da2, xhat, rstd, gain, bt):
    mp = len(dqc)
    share, d = da2.shape
    width = dqc[0].shape[1]
    row = lambda w: pl.BlockSpec((bt, w), lambda i: (i, 0))
    all_of = lambda a: pl.BlockSpec(a.shape, lambda i: (0,) * a.ndim)
    outs = pl.pallas_call(
        functools.partial(pre_self_kernel, mp),
        grid=(share // bt,),
        in_specs=[row(width)] * mp
        + [all_of(w) for w in (*cq, *wo)]
        + [row(d), row(d), row(1), all_of(gain)],
        out_specs=[row(d), row(d)] + [row(width)] * mp + [pl.BlockSpec((2, d), lambda i: (0, 0))],
        out_shape=[jax.ShapeDtypeStruct((share, d), F32), jax.ShapeDtypeStruct((share, d), BF16)]
        + [jax.ShapeDtypeStruct((share, width), BF16)] * mp
        + [jax.ShapeDtypeStruct((2, d), F32)],
        compiler_params=params(),
        cost_estimate=cost(4 * share * d * d, share * d * 14),
    )(*dqc, *cq, *wo, da2, xhat, rstd, gain)
    return outs[0], outs[1], outs[2 : 2 + mp], outs[-1]


def part_kernel(n_in, n_out, per_part, sc, *refs):
    grads, w_ref, outs = refs[:n_in], refs[n_in], refs[n_in + 1 :]
    i = pl.program_id(0)
    total = mm(grads[0][...], w_ref[0], NT)
    for c in range(1, n_in):
        total += mm(grads[c][...], w_ref[c], NT)
    for r in range(n_out):

        @pl.when(jnp.logical_and(i >= r * per_part, i < (r + 1) * per_part))
        def _():
            outs[r][...] = total.astype(outs[r].dtype)


def input_part(sc, grads, w, mp, bt):
    tokens, width = grads[0].shape
    d = w.shape[1]
    nblk = tokens // bt
    per_part = nblk // mp
    outs = pl.pallas_call(
        functools.partial(part_kernel, len(grads), mp, per_part),
        grid_spec=pltpu.PrefetchScalarGridSpec(
            num_scalar_prefetch=1,
            grid=(nblk,),
            in_specs=[pl.BlockSpec((bt, width), lambda i, sc: (sc[i], 0))] * len(grads) + [whole(w)],
            out_specs=[pl.BlockSpec((bt, d), part_map(r, per_part)) for r in range(mp)],
        ),
        out_shape=[jax.ShapeDtypeStruct((tokens // mp, d), F32)]
        + [jax.ShapeDtypeStruct((tokens // mp, d), BF16)] * (mp - 1),
        compiler_params=params(),
        cost_estimate=cost(2 * tokens * d * width * len(grads), tokens * d * 6),
    )(sc, *grads, w)
    return outs


def shards(
    block_input_slots,
    memory,
    target_sentence_lengths,
    source_lengths,
    self_qkv,
    self_out,
    cross_query,
    cross_kv,
    cross_out,
    up_proj,
    down_proj,
    norm_gains,
    norm_biases,
    cotangent,
    mp,
):
    tokens, d = block_input_slots.shape
    mem_tokens = memory.shape[0]
    share = cotangent.shape[0]
    mem_share = mem_tokens // mp
    width = self_qkv.shape[2]
    me = lax.axis_index("mp")
    bt = min(256, share)
    bq = min(256, share)
    bk = min(256, mem_tokens)

    def spread(own):
        return [own] + [
            lax.ppermute(own, "mp", [(i, (i + r) % mp) for i in range(mp)]) for r in range(1, mp)
        ]

    def exchange(pieces):
        got = [pieces[0]] + [None] * (mp - 1)
        for r in range(1, mp):
            got[mp - r] = lax.ppermute(pieces[r], "mp", [(i, (i - r) % mp) for i in range(mp)])
        return got

    wo, cq, co = spread(self_out), spread(cross_query), spread(cross_out)
    up, down = spread(up_proj), spread(down_proj)
    gain, shift = norm_gains.T, norm_biases.T

    t_len = target_sentence_lengths.reshape(-1)
    s_len = source_lengths.reshape(-1)
    t_end, s_end = jnp.cumsum(t_len), jnp.cumsum(s_len)
    t_start, s_start = t_end - t_len, s_end - s_len
    first = ((me - jnp.arange(mp)) % mp) * share
    place = (first[:, None] + jnp.arange(share)[None, :]).reshape(-1).astype(jnp.int32)
    begun = place[:, None] >= t_start[None, :]
    self_lo = jnp.max(jnp.where(begun, t_start[None, :], 0), axis=1)
    self_hi = place + 1
    cross_lo = jnp.max(jnp.where(begun, s_start[None, :], 0), axis=1)
    cross_hi = jnp.max(jnp.where(begun, s_end[None, :], 0), axis=1)
    nblk = tokens // bq
    q_block = place.reshape(nblk, bq)[:, 0] // bq

    def table(lo, hi):
        return jnp.concatenate(
            [lo.reshape(nblk, bq)[:, 0] // bk, (hi.reshape(nblk, bq)[:, -1] + bk - 1) // bk, q_block]
        ).astype(jnp.int32)

    self_table, cross_table = table(self_lo, self_hi), table(cross_lo, cross_hi)
    as_row = lambda v: v.reshape(1, tokens).astype(jnp.int32)
    self_lo, self_hi, cross_lo, cross_hi = map(as_row, (self_lo, self_hi, cross_lo, cross_hi))

    proj = [
        jnp.dot(block_input_slots, self_qkv[c], preferred_element_type=F32).astype(BF16) for c in range(3)
    ]
    pair = [jnp.dot(memory, cross_kv[c], preferred_element_type=F32).astype(BF16) for c in range(2)]
    ctx_parts, self_lse = attend(
        self_table, proj[:1], proj[1], proj[2], self_lo, self_hi, mp, bq, bk
    )
    ctx = exchange(ctx_parts)
    me_row = me.reshape(1).astype(jnp.int32)
    n1, xhat1, rstd1, qc = post_self(me_row, block_input_slots, ctx, wo, cq, gain, shift, share, bt)
    qc_parts = exchange(qc)
    cctx_parts, cross_lse = attend(
        cross_table, qc_parts, pair[0], pair[1], cross_lo, cross_hi, mp, bq, bk
    )
    cctx = exchange(cctx_parts)
    layer_output, da2, n2, e3, e2, dcctx, hid, dpre, small23 = middle(
        cctx, n1, cotangent, co, up, down, gain, shift, bt
    )
    dcctx_parts = exchange(dcctx)

    def grads(lefts, rights):
        return [mm(a, b, TN).astype(BF16) for a, b in zip(lefts, rights)]

    def collect(pieces):
        got = exchange(pieces)
        total = got[0].astype(F32)
        for g in got[1:]:
            total += g.astype(F32)
        return total

    down_grad = collect(grads(hid, [e3] * mp))
    up_grad = collect(grads(dpre, [n2] * mp))
    cross_out_grad = collect(grads(cctx, [e2] * mp))
    dqc_parts, dkc, dvc = attend_back(
        cross_table, qc_parts, dcctx_parts, cctx_parts, pair[0], pair[1], cross_lo, cross_hi, cross_lse, mp, bq, bk
    )
    dqc = exchange(dqc_parts)
    da1, e1, dctx, small1 = pre_self(dqc, cq, wo, da2, xhat1, rstd1, gain, bt)
    dctx_parts = exchange(dctx)
    mem_bt = min(256, mem_share)
    mem_nb = mem_share // mem_bt
    mem_blocks = ((((me - jnp.arange(mp)) % mp) * mem_nb)[:, None] + jnp.arange(mem_nb)[None, :]).reshape(-1)
    memory_parts = input_part(mem_blocks.astype(jnp.int32), [dkc, dvc], cross_kv, mp, mem_bt)
    memory_grad = collect(memory_parts)
    cross_kv_grad = jnp.stack([mm(memory, g, TN) for g in (dkc, dvc)])
    cross_query_grad = collect(grads([n1] * mp, dqc))
    self_out_grad = collect(grads(ctx, [e1] * mp))
    (dq,), dk, dv = attend_back(
        self_table, proj[:1], dctx_parts, ctx_parts, proj[1], proj[2], self_lo, self_hi, self_lse, mp, bq, bk
    )
    input_parts = input_part(q_block.astype(jnp.int32), [dq, dk, dv], self_qkv, mp, bq)
    input_grad = collect(input_parts) + da1
    self_qkv_grad = jnp.stack([mm(block_input_slots, g, TN) for g in (dq, dk, dv)])

    small = jnp.concatenate([small1[:1], small23[:2], small1[1:], small23[2:]], axis=0)
    part = d // mp
    pieces = [
        lax.dynamic_slice_in_dim(small, ((me - r) % mp) * part, part, 1).astype(BF16) for r in range(mp)
    ]
    small = collect(pieces)
    summed = [
        lax.psum(g.astype(BF16), "batch").astype(F32)
        for g in (
            self_qkv_grad,
            self_out_grad,
            cross_query_grad,
            cross_kv_grad,
            cross_out_grad,
            up_grad,
            down_grad,
            small,
        )
    ]
    small = summed[-1].T
    return (layer_output, input_grad, memory_grad, *summed[:-1], small[:, :3], small[:, 3:])


def solution(mesh):
    mp = mesh.shape["mp"]
    rows = P("batch", None)
    both = P(("batch", "mp"), None)
    first, last, last3 = P("mp", None), P(None, "mp"), P(None, None, "mp")
    return jax.shard_map(
        functools.partial(shards, mp=mp),
        mesh=mesh,
        in_specs=(rows, rows, rows, rows, last3, first, last, last3, first, first, first, P(), P(), both),
        out_specs=(both, both, both, last3, first, last, last3, first, first, first, first, first),
        check_vma=False,
    )
```

time: 839 us -> 385 us (0.46)
  matrix products: 309 us -> 28 us
  Pallas kernels: 0 us -> 138 us
  other arithmetic: 138 us -> 21.1 us
  waiting for transfers between devices: 226 us -> 115 us
  local copies, waits for them, and re-layouts: 67.5 us -> 12.4 us
  loops' own time: 27.5 us -> 0 us
    dot_general x77 -> x20, matrix products: 309 us -> 28 us  [the longest x15 20.4 us: mm(): return lax.dot_general(a, b, dims, preferred_element_type=F32)]
    pallas_call x0 -> x9, Pallas kernels: none -> 138 us  [the longest x2 50.8 us: attend_back(): pl.pallas_call(functools.partial(attend_back_kernel, nblk, per_part, len(...]
    reduce_scatter x7 -> x0, waiting for transfers between devices: 62.6 us -> none  [the longest x1 14.2 us: shards(): lax.psum_scatter(jnp.dot(self_ctx, self_out, preferred_element_type=jnp.f...]
    convert_element_type x21 -> x7, other arithmetic: 71.9 us -> 12.5 us  [the longest x5 8.68 us: shards(): lax.psum(g.astype(BF16), 'batch').astype(F32)]
    reduce_sum x23 -> x0, other arithmetic: 47.9 us -> none  [the longest x8 26.7 us: per_block(): row_total = jnp.sum(exp_scores, axis=-1, keepdims=True)]
    all_gather x5 -> x0, waiting for transfers between devices: 44.5 us -> none  [the longest x1 11.9 us: shards(): lax.all_gather(grad_two.astype(jnp.bfloat16), 'mp', axis=0, tiled=True)]
    another operation x4 -> x0, loops' own time: 27.5 us -> none  [the longest x2 22 us: per_row(): lax.scan(per_block, (empty_kv, empty_kv), jnp.arange(length // block_len,...]
    another operation x18 -> x1, local copies, waits for them, and re-layouts: 15.1 us -> 0.09 us  [the longest x4 10.4 us: shards(): jnp.stack([grad_sq.reshape(tokens, local_width), grad_sk.reshape(tokens,...]
  transfers between devices with their start and end apart: 15 -> 20, of which waited for: 10 -> 6; matrix products, arithmetic and copies ran while one was open for 31% -> 7% of each run, Pallas kernels for 0% -> 15%
where the time goes in v1:
time: 385 us; the launch traced here: 382 us
  Pallas kernels  138 us (36%)
  waiting for transfers between devices  115 us (30%)
  blocking collectives  47.1 us (12%)
  matrix products  28 us (7%)
  other arithmetic  21.1 us (5%)
  between operations  14.5 us (4%)
  local copies, waits for them, and re-layouts  12.4 us (3%)
  starting transfers between devices  5.82 us (2%)
    psum x1, waiting for transfers between devices, shards(): lax.psum(g.astype(BF16), 'batch').astype(F32)  110 us
    pallas_call x2, Pallas kernels, attend_back(): pl.pallas_call(functools.partial(attend_back_kernel, nblk, per_part, len(...  50.8 us
    psum x1, blocking collectives, shards(): lax.psum(g.astype(BF16), 'batch').astype(F32)  47.1 us
    pallas_call x2, Pallas kernels, attend(): pl.pallas_call(functools.partial(attend_kernel, nblk, per_part, len(q_par...  46.9 us
    dot_general x15, matrix products, mm(): return lax.dot_general(a, b, dims, preferred_element_type=F32)  20.4 us
    pallas_call x1, Pallas kernels, middle(): pl.pallas_call(functools.partial(middle_kernel, mp), grid=(share // bt,),...  19.4 us
    unnamed x82, local copies, waits for them, and re-layouts  11.2 us
    pallas_call x2, Pallas kernels, input_part(): pl.pallas_call(functools.partial(part_kernel, len(grads), mp, per_part),...  9.72 us
  transfers between devices with their start and end apart: 20, of which 6 were waited for; matrix products, arithmetic and copies ran while one was open for 7% of the time, Pallas kernels for 15%

profile of v1, /device:TPU:0, one launch (start us, length us, event | category | flops | bytes accessed | tf_op | source)
XLA Modules:
  0.0 382.0 jit_solution(13344481002746140200)
XLA Ops:
  7.3 3.4 convolution_convert_fusion.1.refs_1_.refs_5_
  10.7 1.7 convolution_convert_fusion.2.refs_0_
  12.4 1.7 convolution_convert_fusion.refs_2_.refs_6_
  18.4 30.8 %shard_map.229 = (bf16[1024,256]{1,0:T(8,128)(2,1)S(1)}, bf16[1024,256]{1,0:T(8,128)(2,1)S(1)}, f32[8,4,256]{2,1,0:T(4,128)S(1)}) custom-call(s32[24]{0:T(128)S(1)} %get-tuple-element.158.sc, bf16[2048,256]{1,0:T(8,128)(2,1)S(1)} %copy-done.12, bf16[2048,256]{1,0:T(8,128)(2,1)S(1)} %copy-done.11, bf16[2048,256]{1,0:T(8,128)(2,1)} %convolution_convert_fusion.refs_2_.refs_6_, ...), custom_call_target="tpu_custom_call" | custom-call | flops 1073741824 | bytes 4194304 | tf_op jit(solution)/shard_map/pallas_call | solution.py:102
  50.8 1.3 collective-permute-done.1.refs_4_.refs_5_
  52.8 5.0 %shard_map.230 = (bf16[1024,512]{1,0:T(8,128)(2,1)}, f32[1024,512]{1,0:T(8,128)}, f32[1024,1]{1,0:T(8,128)S(1)}, bf16[1024,256]{1,0:T(8,128)(2,1)S(1)}, bf16[1024,256]{1,0:T(8,128)(2,1)S(1)}) custom-call(s32[1]{0:T(128)} %bitcast.3.sc, bf16[2048,512]{1,0:T(8,128)(2,1)} %refs_0_.1, bf16[1024,256]{1,0:T(8,128)(2,1)S(1)} %get-tuple-element.51.refs_1_.refs_3_, ...), custom_call_target="tpu_custom_call" | custom-call | flops 1073741824 | bytes 6291456 | tf_op jit(solution)/shard_map/pallas_call | solution.py:265
  59.7 16.1 %shard_map.231 = (bf16[1024,256]{1,0:T(8,128)(2,1)S(1)}, bf16[1024,256]{1,0:T(8,128)(2,1)S(1)}, f32[8,4,256]{2,1,0:T(4,128)S(1)}) custom-call(s32[24]{0:T(128)S(1)} %get-tuple-element.159.sc, bf16[1024,256]{1,0:T(8,128)(2,1)S(1)} %get-tuple-element.53.refs_0_, bf16[1024,256]{1,0:T(8,128)(2,1)S(1)} %collective-permute-done.3.refs_1_, ...), custom_call_target="tpu_custom_call" | custom-call | flops 1073741824 | bytes 4194304 | tf_op jit(solution)/shard_map/pallas_call | solution.py:102
  76.5 1.8 collective-permute-done.5.refs_5_
  78.3 19.4 %shard_map.232 = (bf16[1024,512]{1,0:T(8,128)(2,1)}, f32[1024,512]{1,0:T(8,128)}, bf16[1024,512]{1,0:T(8,128)(2,1)S(1)}, bf16[1024,512]{1,0:T(8,128)(2,1)}, bf16...) custom-call(bf16[1024,256]{1,0:T(8,128)(2,1)S(1)} %get-tuple-element, ...), custom_call_target="tpu_custom_call" | custom-call | flops 9663676416 | bytes 8388608 | tf_op jit(solution)/shard_map/pallas_call | solution.py:363
  97.7 1.7 convolution_convert_fusion.9
  100.0 3.0 convolution_convert_fusion.6
  103.0 2.3 convolution_convert_fusion.5
  105.3 2.3 convolution_convert_fusion.3
  108.1 2.3 convolution_convert_fusion.4
  112.4 18.7 %shard_map.233 = (bf16[1024,256]{1,0:T(8,128)(2,1)S(1)}, bf16[1024,256]{1,0:T(8,128)(2,1)S(1)}, bf16[1024,256]{1,0:T(8,128)(2,1)S(1)}, bf16[1024,256]{1,0:T(8,128)(2,1)S(1)}) custom-call(s32[24]{0:T(128)S(1)} %get-tuple-element.159.sc, bf16[1024,256]{1,0:T(8,128)(2,1)S(1)} %get-tuple-element.53.refs_0_, ...), custom_call_target="tpu_custom_call" | custom-call | flops 2684354560 | bytes 6291456 | tf_op jit(solution)/shard_map/pallas_call | solution.py:197
  133.2 6.3 %shard_map.234 = (f32[1024,512]{1,0:T(8,128)}, bf16[1024,512]{1,0:T(8,128)(2,1)}, bf16[1024,256]{1,0:T(8,128)(2,1)S(1)}, bf16[1024,256]{1,0:T(8,128)(2,1)S(1)}, f32[2,512]{1,0:T(2,128)S(1)}) custom-call(bf16[1024,256]{1,0:T(8,128)(2,1)S(1)} %get-tuple-element.62.refs_0_, bf16[1024,256]{1,0:T(8,128)(2,1)S(1)} %collective-permute-done.9.refs_1_, ...), custom_call_target="tpu_custom_call" | custom-call | flops 1073741824 | bytes 7340032 | tf_op jit(solution)/shard_map/pallas_call | solution.py:419
  139.6 1.8 convolution_convert_fusion.15
  142.6 2.5 add_convert_fusion
  145.2 1.3 add_convert_fusion.1
  148.8 32.2 %shard_map.235 = (bf16[2048,256]{1,0:T(8,128)(2,1)S(1)}, bf16[2048,256]{1,0:T(8,128)(2,1)}, bf16[2048,256]{1,0:T(8,128)(2,1)}) custom-call(s32[24]{0:T(128)S(1)} %get-tuple-element.158.sc, bf16[2048,256]{1,0:T(8,128)(2,1)} %convolution_convert_fusion.2.refs_0_, bf16[1024,256]{1,0:T(8,128)(2,1)S(1)} %get-tuple-element.67.refs_1_, ...), custom_call_target="tpu_custom_call" | custom-call | flops 2684354560 | bytes 6291456 | tf_op jit(solution)/shard_map/pallas_call | solution.py:197
  186.1 2.0 shard_map.237
  190.9 7.7 %shard_map.236 = (f32[1024,512]{1,0:T(8,128)}, bf16[1024,512]{1,0:T(8,128)(2,1)S(1)}) custom-call(s32[8]{0:T(128)S(1)} %get-tuple-element.162.sc, bf16[2048,256]{1,0:T(8,128)(2,1)S(1)} %copy-done.17, bf16[2048,256]{1,0:T(8,128)(2,1)S(1)} %copy-done.19, bf16[2048,256]{1,0:T(8,128)(2,1)} %get-tuple-element.72.refs_2_, bf16[3,512,256]{2,1,0:T(8,128)(2,1)S(1)} %copy-done.5), custom_call_target="tpu_custom_call" | custom-call | flops 1610612736 | bytes 6291456 | tf_op jit(solution)/shard_map/pallas_call | solution.py:453
  201.3 47.1 %psum.63 = bf16[256,6]{0,1:T(8,128)(2,1)S(1)} all-reduce(bf16[256,6]{0,1:T(8,128)(2,1)S(1)} %fusion.28), channel_id=1, replica_groups=mesh['batch'=16,'mp'=2] {'batch'}, use_global_device_ids=true, to_apply=%region_12.13 | all-reduce | flops 1536 | bytes 6144 | tf_op jit(solution)/shard_map/psum | solution.py:595
  249.0 4.3 %add_add_fusion = f32[1024,512]{1,0:T(8,128)} fusion(f32[1024,512]{1,0:T(8,128)} %get-tuple-element.75, f32[1024,512]{1,0:T(8,128)} %get-tuple-element.73, bf16[1024,512]{1,0:T(8,128)(2,1)S(1)} %collective-permute-done.11), kind=kLoop, calls=%fused_computation.5 | loop fusion | flops 1572864 | bytes 7340032 | tf_op jit(solution)/shard_map/add | solution.py:585
  253.3 109.5 %all-reduce.3.cloned.1.call-done = (bf16[3,512,256]{1,2,0:T(8,128)(2,1)}, bf16[2,512,256]{1,2,0:T(8,128)(2,1)}, bf16[256,512]{1,0:T(8,128)(2,1)}, bf16[512,256]{...) async-done(((bf16[3,512,256]{1,2,0:T(8,128)(2,1)}, bf16[2,512,256]{1,2,0:T(8,128)(2,1)}, ...) | async-done | bytes 4194320 | tf_op jit(solution)/shard_map/psum | solution.py:595
  362.8 1.9 convert_element_type.148
  364.7 1.8 convert_element_type.154
  366.4 1.8 convert_element_type.161
  368.2 1.4 copy.36
  369.7 2.3 copy.37
  372.0 1.6 convert_element_type.167
  373.6 1.6 convert_element_type.173
  (167 shorter events, 29.1 us)
Async XLA Ops:
  7.2 51.0 %copy-start = (bf16[1024,512]{1,0:T(8,128)(2,1)S(1)}, bf16[1024,512]{1,0:T(8,128)(2,1)}, u32[]{:S(2)}) copy-start(bf16[1024,512]{1,0:T(8,128)(2,1)} %param.15) | copy-start | bytes 3145732
  7.2 355.6 %all-reduce.3.cloned.1.call-start = ((), (), s32[]{:S(2)}) async-start(), calls=%async_computation | async-start | bytes 8388608 | tf_op jit(solution)/shard_map/psum | solution.py:595
  18.4 31.4 %copy-start.1 = (bf16[256,512]{1,0:T(8,128)(2,1)S(1)}, bf16[256,512]{1,0:T(8,128)(2,1)}, u32[]{:S(2)}) copy-start(bf16[256,512]{1,0:T(8,128)(2,1)} %refs_4_.3) | copy-start | bytes 786436
  18.4 31.5 %copy-start.2 = (bf16[512,256]{1,0:T(8,128)(2,1)S(1)}, bf16[512,256]{1,0:T(8,128)(2,1)}, u32[]{:S(2)}) copy-start(bf16[512,256]{1,0:T(8,128)(2,1)} %refs_2_.2) | copy-start | bytes 786436
  18.4 31.9 %copy-start.27 = (bf16[1024,512]{1,0:T(8,128)(2,1)S(1)}, bf16[1024,512]{1,0:T(8,128)(2,1)}, u32[]{:S(2)}) copy-start(bf16[1024,512]{1,0:T(8,128)(2,1)} %refs_6_.1) | copy-start | bytes 3145732
  18.4 32.0 %copy-start.28 = (bf16[1024,512]{1,0:T(8,128)(2,1)S(1)}, bf16[1024,512]{1,0:T(8,128)(2,1)}, u32[]{:S(2)}) copy-start(bf16[1024,512]{1,0:T(8,128)(2,1)} %refs_8_.1) | copy-start | bytes 3145732
  18.4 34.4 %copy-start.3 = (f32[512,3]{0,1:T(4,128)S(1)}, f32[512,3]{0,1:T(4,128)}, u32[]{:S(2)}) copy-start(f32[512,3]{0,1:T(4,128)} %param.25) | copy-start | bytes 18436
  18.4 34.4 %copy-start.4 = (f32[512,3]{0,1:T(4,128)S(1)}, f32[512,3]{0,1:T(4,128)}, u32[]{:S(2)}) copy-start(f32[512,3]{0,1:T(4,128)} %param.26) | copy-start | bytes 18436
  49.2 3.6 collective-permute-start
  49.7 2.3 collective-permute-start.1
  49.8 2.9 collective-permute-start.2
  50.3 28.0 %collective-permute-start.6 = (bf16[1024,512]{1,0:T(8,128)(2,1)S(1)}, bf16[1024,512]{1,0:T(8,128)(2,1)}, u32[]{:S(2)}, u32[]{:S(2)}) collective-permute-start(bf16[1024,512]{1,0:T(8,128)(2,1)S(1)} %copy-done.27), channel_id=1, source_target_pairs={{0,1},{1,0},{2,3},{3,2},{4,5},{5,4},{6,7},{7,6},{8,9},{9,8},{10,11... | collective-permute-start | bytes 3145736 | tf_op jit(solution)/shard_map/ppermute | solution.py:498
  50.3 27.9 %collective-permute-start.7 = (bf16[1024,512]{1,0:T(8,128)(2,1)S(1)}, bf16[1024,512]{1,0:T(8,128)(2,1)}, u32[]{:S(2)}, u32[]{:S(2)}) collective-permute-start(bf16[1024,512]{1,0:T(8,128)(2,1)S(1)} %copy-done.28), channel_id=1, source_target_pairs={{0,1},{1,0},{2,3},{3,2},{4,5},{5,4},{6,7},{7,6},{8,9},{9,8},{10,11... | collective-permute-start | bytes 3145736 | tf_op jit(solution)/shard_map/ppermute | solution.py:498
  57.8 1.9 collective-permute-start.3
  58.6 17.2 %copy-start.9 = (bf16[1024,256]{1,0:T(8,128)(2,1)}, bf16[1024,256]{1,0:T(8,128)(2,1)S(1)}, u32[]{:S(2)}) copy-start(bf16[1024,256]{1,0:T(8,128)(2,1)S(1)} %convolution_convert_fusion.8.refs_2_.refs_6_) | copy-start | bytes 1572868
  59.1 16.8 %copy-start.10 = (bf16[1024,256]{1,0:T(8,128)(2,1)}, bf16[1024,256]{1,0:T(8,128)(2,1)S(1)}, u32[]{:S(2)}) copy-start(bf16[1024,256]{1,0:T(8,128)(2,1)S(1)} %convolution_convert_fusion.7.refs_3_.refs_7_) | copy-start | bytes 1572868
  75.9 21.8 %copy-start.7 = (bf16[1024,256]{1,0:T(8,128)(2,1)}, bf16[1024,256]{1,0:T(8,128)(2,1)S(1)}, u32[]{:S(2)}) copy-start(bf16[1024,256]{1,0:T(8,128)(2,1)S(1)} %get-tuple-element.56.refs_5_) | copy-start | bytes 1572868
  75.9 34.5 %copy-start.15 = (bf16[1024,256]{1,0:T(8,128)(2,1)}, bf16[1024,256]{1,0:T(8,128)(2,1)S(1)}, u32[]{:S(2)}) copy-start(bf16[1024,256]{1,0:T(8,128)(2,1)S(1)} %get-tuple-element.55.refs_0_.refs_4_) | copy-start | bytes 1572868
  75.9 2.4 collective-permute-start.4
  76.4 1.9 collective-permute-start.5
  99.4 11.0 %collective-permute-start.15 = (bf16[256,512]{1,0:T(8,128)(2,1)S(1)}, bf16[256,512]{1,0:T(8,128)(2,1)S(1)}, u32[]{:S(2)}, u32[]{:S(2)}) collective-permute-start(bf16[256,512]{1,0:T(8,128)(2,1)S(1)} %convolution_convert_fusion.9), channel_id=1, source_target_pairs={{0,1},{1,0},{2,3},{3,2},{4,5},{5,4},{6,7},{7,6},{8,9},{9,8},{10,11... | collective-permute-start | bytes 786440 | tf_op jit(solution)/shard_map/ppermute | solution.py:504
  99.8 11.8 %collective-permute-start.8 = (bf16[1024,256]{1,0:T(8,128)(2,1)S(1)}, bf16[1024,256]{1,0:T(8,128)(2,1)S(1)}, u32[]{:S(2)}, u32[]{:S(2)}) collective-permute-start(bf16[1024,256]{1,0:T(8,128)(2,1)S(1)} %get-tuple-element.60), channel_id=1, source_target_pairs={{0,1},{1,0},{2,3},{3,2},{4,5},{5,4},{6,7},{7,6},{8,9},{9,8},{10,11... | collective-permute-start | bytes 1572872 | tf_op jit(solution)/shard_map/ppermute | solution.py:504
  107.6 35.0 %collective-permute-start.17 = (bf16[1024,512]{1,0:T(8,128)(2,1)}, bf16[1024,512]{1,0:T(8,128)(2,1)}, u32[]{:S(2)}, u32[]{:S(2)}) collective-permute-start(bf16[1024,512]{1,0:T(8,128)(2,1)} %convolution_convert_fusion.3), channel_id=1, source_target_pairs={{0,1},{1,0},{2,3},{3,2},{4,5},{5,4},{6,7},{7,6},{8,9},{9,8},{10,11... | collective-permute-start | bytes 3145736 | tf_op jit(solution)/shard_map/ppermute | solution.py:504
  108.0 37.2 %collective-permute-start.16 = (bf16[1024,512]{1,0:T(8,128)(2,1)}, bf16[1024,512]{1,0:T(8,128)(2,1)S(1)}, u32[]{:S(2)}, u32[]{:S(2)}) collective-permute-start(bf16[1024,512]{1,0:T(8,128)(2,1)} %convolution_convert_fusion.5), channel_id=1, source_target_pairs={{0,1},{1,0},{2,3},{3,2},{4,5},{5,4},{6,7},{7,6},{8,9},{9,8},{10,11... | collective-permute-start | bytes 3145736 | tf_op jit(solution)/shard_map/ppermute | solution.py:504
  131.1 2.2 collective-permute-start.9
  141.3 5.1 %collective-permute-start.13 = (bf16[256,512]{1,0:T(8,128)(2,1)S(1)}, bf16[256,512]{1,0:T(8,128)(2,1)S(1)}, u32[]{:S(2)}, u32[]{:S(2)}) collective-permute-start(bf16[256,512]{1,0:T(8,128)(2,1)S(1)} %convolution_convert_fusion.15), channel_id=1, source_target_pairs={{0,1},{1,0},{2,3},{3,2},{4,5},{5,4},{6,7},{7,6},{8,9},{9,8},{10,11... | collective-permute-start | bytes 786440 | tf_op jit(solution)/shard_map/ppermute | solution.py:504
  142.0 5.6 %collective-permute-start.14 = (bf16[512,256]{1,0:T(8,128)(2,1)S(1)}, bf16[512,256]{1,0:T(8,128)(2,1)S(1)}, u32[]{:S(2)}, u32[]{:S(2)}) collective-permute-start(bf16[512,256]{1,0:T(8,128)(2,1)S(1)} %convolution_convert_fusion.13), channel_id=1, source_target_pairs={{0,1},{1,0},{2,3},{3,2},{4,5},{5,4},{6,7},{7,6},{8,9},{9,8},{10,11... | collective-permute-start | bytes 786440 | tf_op jit(solution)/shard_map/ppermute | solution.py:504
  142.5 6.4 %collective-permute-start.10 = (bf16[1024,256]{1,0:T(8,128)(2,1)S(1)}, bf16[1024,256]{1,0:T(8,128)(2,1)S(1)}, u32[]{:S(2)}, u32[]{:S(2)}) collective-permute-start(bf16[1024,256]{1,0:T(8,128)(2,1)S(1)} %get-tuple-element.68), channel_id=1, source_target_pairs={{0,1},{1,0},{2,3},{3,2},{4,5},{5,4},{6,7},{7,6},{8,9},{9,8},{10,11... | collective-permute-start | bytes 1572872 | tf_op jit(solution)/shard_map/ppermute | solution.py:504
  148.8 32.2 %copy-start.21 = (bf16[2048,512]{1,0:T(8,128)(2,1)S(1)}, bf16[2048,512]{1,0:T(8,128)(2,1)}, u32[]{:S(2)}) copy-start(bf16[2048,512]{1,0:T(8,128)(2,1)} %refs_0_.1) | copy-start | bytes 6291460
  188.1 11.2 %collective-permute-start.12 = (bf16[512,512]{1,0:T(8,128)(2,1)S(1)}, bf16[512,512]{1,0:T(8,128)(2,1)S(1)}, u32[]{:S(2)}, u32[]{:S(2)}) collective-permute-start(bf16[512,512]{1,0:T(8,128)(2,1)S(1)} %get-tuple-element.79), channel_id=1, source_target_pairs={{0,1},{1,0},{2,3},{3,2},{4,5},{5,4},{6,7},{7,6},{8,9},{9,8},{10,11... | collective-permute-start | bytes 1572872 | tf_op jit(solution)/shard_map/ppermute | solution.py:504
  198.7 50.3 %collective-permute-start.11 = (bf16[1024,512]{1,0:T(8,128)(2,1)S(1)}, bf16[1024,512]{1,0:T(8,128)(2,1)S(1)}, u32[]{:S(2)}, u32[]{:S(2)}) collective-permute-start(bf16[1024,512]{1,0:T(8,128)(2,1)S(1)} %get-tuple-element.74), channel_id=1, source_target_pairs={{0,1},{1,0},{2,3},{3,2},{4,5},{5,4},{6,7},{7,6},{8,9},{9,8},{10,11... | collective-permute-start | bytes 3145736 | tf_op jit(solution)/shard_map/ppermute | solution.py:504
  198.9 2.5 collective-permute-start.18
  (27 other events, 86.1 us)
Sparse Core Ops, SparseCore 0:
  185.2 177.5 all-reduce.2

commit v2 on v1

--- a/solution.py
+++ b/solution.py
@@ -466,6 +466,135 @@
     return outs
 
 
+MESH = pl.DeviceIdType.MESH
+
+
+def all_sum_kernel(plan, nbits, n, *refs):
+    ins, outs = refs[: n + 1], refs[n + 1 : 2 * n + 2]
+    got = refs[2 * n + 2 : 2 * n + 3 + len(plan)]
+    send_sem, recv_sem = refs[2 * n + 3 + len(plan) :]
+    me, core = lax.axis_index("batch"), lax.axis_index("mp")
+    bit = [(me // (1 << b)) % 2 for b in range(nbits)]
+    partner = [(me + (1 << b) * (1 - 2 * bit[b]), core) for b in range(nbits)]
+    barrier = pltpu.get_barrier_semaphore()
+    for b in range(nbits):
+        pl.semaphore_signal(barrier, inc=1, device_id=partner[b], device_id_type=MESH)
+    pl.semaphore_wait(barrier, nbits)
+
+    def send(c, s, b, src, dst):
+        copy = pltpu.make_async_remote_copy(
+            src_ref=src,
+            dst_ref=dst,
+            send_sem=send_sem.at[c, s],
+            recv_sem=recv_sem.at[c, s],
+            device_id=partner[b],
+            device_id_type=MESH,
+        )
+        copy.start()
+        copies[c].append(copy)
+
+    def rows(off, count):
+        return pl.ds(pl.multiple_of(off, 16), count)
+
+    copies = [[] for _ in range(len(plan) + 1)]
+    spans = [[(first, count)] for _, first, count, _ in plan]
+    slots = [[] for _ in plan]
+
+    def held(c, s, b):
+        a, first, count, _ = plan[c]
+        half = count >> (s + 1)
+        base = first if s == 0 else slots[c][s - 1]
+        ref = ins[a] if s == 0 else got[c]
+        return ref, base + (1 - bit[b]) * half, base + bit[b] * half, half
+
+    def begin(c, s):
+        a, first, count, order = plan[c]
+        if s < nbits:
+            b = order[s]
+            ref, gives, _, half = held(c, s, b)
+            slots[c].append(count - (count >> s))
+            off = spans[c][s][0]
+            spans[c].append((off + bit[b] * half, half))
+            send(c, s, b, ref.at[rows(gives, half), :], got[c].at[pl.ds(slots[c][s], half), :])
+        else:
+            j = 2 * nbits - 1 - s
+            block = outs[a].at[rows(*spans[c][j + 1]), :]
+            send(c, s, order[j], block, block)
+
+    def finish(c, s):
+        copies[c][s].wait_recv()
+        if s < nbits:
+            a, _, _, order = plan[c]
+            ref, _, stays, half = held(c, s, order[s])
+            came = pl.ds(slots[c][s], half)
+            total = ref[rows(stays, half), :].astype(F32) + got[c][came, :].astype(F32)
+            if s < nbits - 1:
+                got[c][came, :] = total.astype(BF16)
+            else:
+                outs[a][rows(*spans[c][s + 1]), :] = total.astype(BF16)
+
+    last = len(plan)
+    size = ins[n].shape[0]
+    outs[n][...] = ins[n][...]
+    for s in range(2 * nbits + 1):
+        if 1 <= s <= nbits:
+            copies[last][s - 1].wait()
+            outs[n][...] = (
+                outs[n][...].astype(F32) + got[last][(s - 1) * size : s * size, :].astype(F32)
+            ).astype(BF16)
+        if s < nbits:
+            send(last, s, s, outs[n], got[last].at[pl.ds(s * size, size), :])
+        for c in range(len(plan)):
+            if s >= 1:
+                finish(c, s - 1)
+            if s < 2 * nbits:
+                begin(c, s)
+    for c in range(len(plan)):
+        for copy in copies[c]:
+            copy.wait_send()
+
+
+def all_sum(arrays, splits, small, devices):
+    nbits = devices.bit_length() - 1
+    if devices != 1 << nbits or nbits < 3:
+        return [lax.psum(a, "batch") for a in (*arrays, small)]
+    x_y, y_x = tuple(range(nbits)), (1, 0, *range(2, nbits))
+    far = (*range(2, nbits), 0, 1)
+    flat = [a.reshape(-1, a.shape[-1]) for a in arrays]
+    plan, used = [], []
+    for a, parts in zip(flat, splits):
+        count = a.shape[0] // parts
+        if a.shape[0] % parts == 0 and count % (16 * devices) == 0:
+            for p in range(parts):
+                order = far if parts == 3 else (x_y, y_x)[len(plan) % 2]
+                plan.append((len(used), p * count, count, order))
+            used.append(a)
+        else:
+            used.append(None)
+    keep = [i for i, a in enumerate(used) if a is not None]
+    plan = [(keep.index(i), *rest) for i, *rest in plan]
+    small = jnp.pad(small, ((0, 16 - small.shape[0]), (0, 0)))
+    operands = [used[i] for i in keep] + [small]
+    vmem = pl.BlockSpec(memory_space=pltpu.VMEM)
+    sums = pl.pallas_call(
+        functools.partial(all_sum_kernel, plan, nbits, len(keep)),
+        in_specs=[vmem] * len(operands),
+        out_specs=[vmem] * len(operands),
+        out_shape=[jax.ShapeDtypeStruct(a.shape, a.dtype) for a in operands],
+        scratch_shapes=[pltpu.VMEM((rows, operands[i].shape[1]), BF16) for i, _, rows, _ in plan]
+        + [pltpu.VMEM((16 * nbits, small.shape[1]), BF16)]
+        + [pltpu.SemaphoreType.DMA((len(plan) + 1, 2 * nbits))] * 2,
+        compiler_params=pltpu.CompilerParams(
+            collective_id=7, has_side_effects=True, vmem_limit_bytes=VMEM_BYTES
+        ),
+    )(*operands)
+    outs = [
+        sums[keep.index(i)].reshape(a.shape) if i in keep else lax.psum(a, "batch")
+        for i, a in enumerate(arrays)
+    ]
+    return outs + [sums[-1]]
+
+
 def shards(
     block_input_slots,
     memory,
@@ -482,6 +611,7 @@
     norm_biases,
     cotangent,
     mp,
+    devices,
 ):
     tokens, d = block_input_slots.shape
     mem_tokens = memory.shape[0]
@@ -591,21 +721,26 @@
         lax.dynamic_slice_in_dim(small, ((me - r) % mp) * part, part, 1).astype(BF16) for r in range(mp)
     ]
     small = collect(pieces)
-    summed = [
-        lax.psum(g.astype(BF16), "batch").astype(F32)
-        for g in (
-            self_qkv_grad,
-            self_out_grad,
-            cross_query_grad,
-            cross_kv_grad,
-            cross_out_grad,
-            up_grad,
-            down_grad,
-            small,
-        )
-    ]
-    small = summed[-1].T
-    return (layer_output, input_grad, memory_grad, *summed[:-1], small[:, :3], small[:, 3:])
+    *summed, small = all_sum(
+        [
+            g.astype(BF16)
+            for g in (
+                self_qkv_grad,
+                self_out_grad,
+                cross_query_grad,
+                cross_kv_grad,
+                cross_out_grad,
+                up_grad,
+                down_grad,
+            )
+        ],
+        (3, 1, 1, 2, 1, 2, 2),
+        small.astype(BF16),
+        devices,
+    )
+    summed = [g.astype(F32) for g in summed]
+    small = small.astype(F32).T
+    return (layer_output, input_grad, memory_grad, *summed, small[:, :3], small[:, 3:6])
 
 
 def solution(mesh):
@@ -614,7 +749,7 @@
     both = P(("batch", "mp"), None)
     first, last, last3 = P("mp", None), P(None, "mp"), P(None, None, "mp")
     return jax.shard_map(
-        functools.partial(shards, mp=mp),
+        functools.partial(shards, mp=mp, devices=mesh.shape["batch"]),
         mesh=mesh,
         in_specs=(rows, rows, rows, rows, last3, first, last, last3, first, first, first, P(), P(), both),
         out_specs=(both, both, both, last3, first, last, last3, first, first, first, first, first),

time: 385 us -> 320 us (0.83)
  waiting for transfers between devices: 115 us -> 3.53 us
  Pallas kernels: 138 us -> 241 us
  blocking collectives: 47.1 us -> 0 us
  between operations: 14.5 us -> 1.19 us
    psum x1 -> x0, waiting for transfers between devices: 110 us -> none  [shards(): lax.psum(g.astype(BF16), 'batch').astype(F32)]
    pallas_call x0 -> x1, Pallas kernels: none -> 90.8 us  [all_sum(): pl.pallas_call(functools.partial(all_sum_kernel, plan, nbits, len(keep)),...]
    psum x1 -> x0, blocking collectives: 47.1 us -> none  [shards(): lax.psum(g.astype(BF16), 'batch').astype(F32)]
    pallas_call x2, Pallas kernels: 46.9 us -> 52.9 us  [attend(): pl.pallas_call(functools.partial(attend_kernel, nblk, per_part, len(q_par...]
    pallas_call x2, Pallas kernels: 50.8 us -> 56.5 us  [attend_back(): pl.pallas_call(functools.partial(attend_back_kernel, nblk, per_part, len(...]
    convert_element_type x5 -> x8, other arithmetic: 8.68 us -> 8.09 us  [the longest x7 8.08 us: shards(): summed = [g.astype(F32) for g in summed]]
    unnamed x82 -> x108, local copies, waits for them, and re-layouts: 11.2 us -> 11.5 us
  transfers between devices with their start and end apart: 20 -> 19, of which waited for: 6 -> 4; matrix products, arithmetic and copies ran while one was open for 7% -> 12% of each run, Pallas kernels for 15% -> 48%
where the time goes in v2:
time: 320 us; the launch traced here: 314 us
  Pallas kernels  241 us (75%)
  matrix products  28.1 us (9%)
  other arithmetic  19.7 us (6%)
  local copies, waits for them, and re-layouts  15.1 us (5%)
  starting transfers between devices  5.26 us (2%)
  waiting for transfers between devices  3.53 us (1%)
    pallas_call x1, Pallas kernels, all_sum(): pl.pallas_call(functools.partial(all_sum_kernel, plan, nbits, len(keep)),...  90.8 us
    pallas_call x2, Pallas kernels, attend_back(): pl.pallas_call(functools.partial(attend_back_kernel, nblk, per_part, len(...  56.5 us
    pallas_call x2, Pallas kernels, attend(): pl.pallas_call(functools.partial(attend_kernel, nblk, per_part, len(q_par...  52.9 us
    dot_general x15, matrix products, mm(): return lax.dot_general(a, b, dims, preferred_element_type=F32)  20.5 us
    pallas_call x1, Pallas kernels, middle(): pl.pallas_call(functools.partial(middle_kernel, mp), grid=(share // bt,),...  19.7 us
    unnamed x108, local copies, waits for them, and re-layouts  11.5 us
    pallas_call x2, Pallas kernels, input_part(): pl.pallas_call(functools.partial(part_kernel, len(grads), mp, per_part),...  9.85 us
    convert_element_type x7, other arithmetic, shards(): summed = [g.astype(F32) for g in summed]  8.08 us
  transfers between devices with their start and end apart: 19, of which 4 were waited for; matrix products, arithmetic and copies ran while one was open for 12% of the time, Pallas kernels for 48%

profile of v2, /device:TPU:0, one launch (start us, length us, event | category | flops | bytes accessed | tf_op | source)
XLA Modules:
  0.0 314.0 jit_solution(11523091649556922118)
XLA Ops:
  0.7 3.4 %convolution_convert_fusion.1.refs_1_.refs_5_ = bf16[2048,256]{1,0:T(8,128)(2,1)} fusion(bf16[2048,512]{1,0:T(8,128)(2,1)} %refs_0_.1, bf16[3,512,256]{2,1,0:T(8,128)(2,1)} %refs_3_.5), kind=kOutput, calls=%fused_computation.1 | convolution fusion | flops 537395200 | bytes 3407872 | tf_op jit(solution)/shard_map/dot_general | solution.py:665
  4.1 1.7 convolution_convert_fusion.2.refs_0_
  5.8 1.7 convolution_convert_fusion.refs_2_.refs_6_
  9.3 1.2 copy-done.24
  10.6 1.2 copy-done.25
  11.8 30.8 %shard_map.229 = (bf16[1024,256]{1,0:T(8,128)(2,1)S(1)}, bf16[1024,256]{1,0:T(8,128)(2,1)S(1)}, f32[8,4,256]{2,1,0:T(4,128)S(1)}) custom-call(s32[24]{0:T(128)S(1)} %get-tuple-element.119.sc, bf16[2048,256]{1,0:T(8,128)(2,1)S(1)} %copy-done.25, bf16[2048,256]{1,0:T(8,128)(2,1)S(1)} %copy-done.24, bf16[2048,256]{1,0:T(8,128)(2,1)} %convolution_convert_fusion.refs_2_.refs_6_, ...), custom_call_target="tpu_custom_call" | custom-call | flops 1073741824 | bytes 4194304 | tf_op jit(solution)/shard_map/pallas_call | solution.py:102
  45.8 5.2 %shard_map.230 = (bf16[1024,512]{1,0:T(8,128)(2,1)}, f32[1024,512]{1,0:T(8,128)}, f32[1024,1]{1,0:T(8,128)S(1)}, bf16[1024,256]{1,0:T(8,128)(2,1)S(1)}, bf16[1024,256]{1,0:T(8,128)(2,1)S(1)}) custom-call(s32[1]{0:T(128)} %bitcast.3.sc, bf16[2048,512]{1,0:T(8,128)(2,1)} %refs_0_.1, bf16[1024,256]{1,0:T(8,128)(2,1)S(1)} %get-tuple-element.59.refs_1_.refs_3_, ...), custom_call_target="tpu_custom_call" | custom-call | flops 1073741824 | bytes 6291456 | tf_op jit(solution)/shard_map/pallas_call | solution.py:265
  53.7 22.1 %shard_map.231 = (bf16[1024,256]{1,0:T(8,128)(2,1)S(1)}, bf16[1024,256]{1,0:T(8,128)(2,1)}, f32[8,4,256]{2,1,0:T(4,128)S(1)}) custom-call(s32[24]{0:T(128)S(1)} %get-tuple-element.120.sc, bf16[1024,256]{1,0:T(8,128)(2,1)S(1)} %get-tuple-element.61.refs_0_, bf16[1024,256]{1,0:T(8,128)(2,1)S(1)} %collective-permute-done.3.refs_1_, ...), custom_call_target="tpu_custom_call" | custom-call | flops 1073741824 | bytes 4194304 | tf_op jit(solution)/shard_map/pallas_call | solution.py:102
  77.3 1.7 collective-permute-done.5.refs_5_
  80.1 19.7 %shard_map.232 = (bf16[1024,512]{1,0:T(8,128)(2,1)}, f32[1024,512]{1,0:T(8,128)}, bf16[1024,512]{1,0:T(8,128)(2,1)S(1)}, bf16[1024,512]{1,0:T(8,128)(2,1)}, bf16...) custom-call(bf16[1024,256]{1,0:T(8,128)(2,1)S(1)} %copy-done.31, ...), custom_call_target="tpu_custom_call" | custom-call | flops 9663676416 | bytes 8388608 | tf_op jit(solution)/shard_map/pallas_call | solution.py:363
  99.8 1.8 convolution_convert_fusion.9
  102.2 4.1 %convolution_convert_fusion.6 = bf16[1024,512]{1,0:T(8,128)(2,1)} fusion(bf16[1024,1024]{1,0:T(8,128)(2,1)} %get-tuple-element.90, bf16[1024,512]{1,0:T(8,128)(2,1)S(1)} %get-tuple-element.91), kind=kOutput, calls=%fused_computation.9 | convolution fusion | flops 1074266112 | bytes 4194304 | tf_op jit(solution)/shard_map/dot_general | solution.py:24
  106.3 2.3 convolution_convert_fusion.5
  108.6 2.3 convolution_convert_fusion.4
  110.8 2.3 convolution_convert_fusion.3
  114.9 24.3 %shard_map.233 = (bf16[1024,256]{1,0:T(8,128)(2,1)S(1)}, bf16[1024,256]{1,0:T(8,128)(2,1)}, bf16[1024,256]{1,0:T(8,128)(2,1)S(1)}, bf16[1024,256]{1,0:T(8,128)(2,1)S(1)}) custom-call(s32[24]{0:T(128)S(1)} %get-tuple-element.120.sc, bf16[1024,256]{1,0:T(8,128)(2,1)S(1)} %copy-done.18, bf16[1024,256]{1,0:T(8,128)(2,1)S(1)} %copy-done.20, ...), custom_call_target="tpu_custom_call" | custom-call | flops 2684354560 | bytes 6291456 | tf_op jit(solution)/shard_map/pallas_call | solution.py:197
  141.3 1.2 copy.37
  145.6 2.0 shard_map.237
  148.1 6.3 %shard_map.234 = (f32[1024,512]{1,0:T(8,128)}, bf16[1024,512]{1,0:T(8,128)(2,1)}, bf16[1024,256]{1,0:T(8,128)(2,1)S(1)}, bf16[1024,256]{1,0:T(8,128)(2,1)S(1)}, f32[2,512]{1,0:T(2,128)S(1)}) custom-call(bf16[1024,256]{1,0:T(8,128)(2,1)S(1)} %copy-done.8, bf16[1024,256]{1,0:T(8,128)(2,1)} %collective-permute-done.9.refs_1_, bf16[512,256]{1,0:T(8,128)(2,1)S(1)} %copy-done.2, ...), custom_call_target="tpu_custom_call" | custom-call | flops 1073741824 | bytes 7340032 | tf_op jit(solution)/shard_map/pallas_call | solution.py:419
  154.7 1.8 convolution_convert_fusion.15
  156.9 1.5 convolution_convert_fusion.13
  158.6 2.6 add_convert_fusion.refs_6_
  161.5 2.5 add_convert_fusion.1.refs_5_
  164.0 1.1 convert_add_fusion
  166.5 32.1 %shard_map.235 = (bf16[2048,256]{1,0:T(8,128)(2,1)S(1)}, bf16[2048,256]{1,0:T(8,128)(2,1)}, bf16[2048,256]{1,0:T(8,128)(2,1)}) custom-call(s32[24]{0:T(128)S(1)} %get-tuple-element.119.sc, bf16[2048,256]{1,0:T(8,128)(2,1)} %convolution_convert_fusion.2.refs_0_, bf16[1024,256]{1,0:T(8,128)(2,1)S(1)} %get-tuple-element.75.refs_1_, ...), custom_call_target="tpu_custom_call" | custom-call | flops 2684354560 | bytes 6291456 | tf_op jit(solution)/shard_map/pallas_call | solution.py:197
  200.1 7.9 %shard_map.236 = (f32[1024,512]{1,0:T(8,128)}, bf16[1024,512]{1,0:T(8,128)(2,1)}) custom-call(s32[8]{0:T(128)S(1)} %get-tuple-element.123.sc, bf16[2048,256]{1,0:T(8,128)(2,1)S(1)} %get-tuple-element.78.refs_0_, bf16[2048,256]{1,0:T(8,128)(2,1)S(1)} %copy-done.33, bf16[2048,256]{1,0:T(8,128)(2,1)} %get-tuple-element.80.refs_2_, ...), custom_call_target="tpu_custom_call" | custom-call | flops 1610612736 | bytes 6291456 | tf_op jit(solution)/shard_map/pallas_call | solution.py:453
  210.0 1.2 copy.36
  211.2 90.8 %shard_map.238 = (bf16[1536,256]{1,0:T(8,128)(2,1)S(1)}, bf16[256,512]{1,0:T(8,128)(2,1)S(1)}, bf16[512,256]{1,0:T(8,128)(2,1)S(1)}, bf16[1024,256]{1,0:T(8,128)...) custom-call(bf16[1536,256]{1,0:T(8,128)(2,1)} %bitcast.118, ...), custom_call_target="tpu_custom_call" | custom-call | tf_op jit(solution)/shard_map/pallas_call | solution.py:579
  304.5 1.3 convert.33
  306.8 1.6 convert_element_type.197
  308.4 1.6 convert_element_type.198
  310.9 3.1 add_add_fusion
  (196 shorter events, 28.6 us)
Async XLA Ops:
  0.6 51.3 %copy-start = (bf16[1024,512]{1,0:T(8,128)(2,1)S(1)}, bf16[1024,512]{1,0:T(8,128)(2,1)}, u32[]{:S(2)}) copy-start(bf16[1024,512]{1,0:T(8,128)(2,1)} %param.15) | copy-start | bytes 3145732
  11.8 32.1 %copy-start.1 = (bf16[256,512]{1,0:T(8,128)(2,1)S(1)}, bf16[256,512]{1,0:T(8,128)(2,1)}, u32[]{:S(2)}) copy-start(bf16[256,512]{1,0:T(8,128)(2,1)} %refs_4_.3) | copy-start | bytes 786436
  11.8 32.2 %copy-start.2 = (bf16[512,256]{1,0:T(8,128)(2,1)S(1)}, bf16[512,256]{1,0:T(8,128)(2,1)}, u32[]{:S(2)}) copy-start(bf16[512,256]{1,0:T(8,128)(2,1)} %refs_2_.2) | copy-start | bytes 786436
  11.8 34.0 %copy-start.9 = (f32[512,3]{0,1:T(4,128)S(1)}, f32[512,3]{0,1:T(4,128)}, u32[]{:S(2)}) copy-start(f32[512,3]{0,1:T(4,128)} %param.25) | copy-start | bytes 18436
  11.8 34.0 %copy-start.10 = (f32[512,3]{0,1:T(4,128)S(1)}, f32[512,3]{0,1:T(4,128)}, u32[]{:S(2)}) copy-start(f32[512,3]{0,1:T(4,128)} %param.26) | copy-start | bytes 18436
  42.6 3.2 %collective-permute-start = (bf16[1024,256]{1,0:T(8,128)(2,1)S(1)}, bf16[1024,256]{1,0:T(8,128)(2,1)S(1)}, u32[]{:S(2)}, u32[]{:S(2)}) collective-permute-start(bf16[1024,256]{1,0:T(8,128)(2,1)S(1)} %get-tuple-element.60.refs_4_), channel_id=1, source_target_pairs={{0,1},{1,0},{2,3},{3,2},{4,5},{5,4},{6,7},{7,6},{8,9},{9,8},{10,11... | collective-permute-start | bytes 1572872 | tf_op jit(solution)/shard_map/ppermute | solution.py:634
  43.9 1.5 collective-permute-start.1
  44.0 1.8 collective-permute-start.2
  44.4 34.7 %collective-permute-start.6 = (bf16[1024,512]{1,0:T(8,128)(2,1)}, bf16[1024,512]{1,0:T(8,128)(2,1)}, u32[]{:S(2)}, u32[]{:S(2)}) collective-permute-start(bf16[1024,512]{1,0:T(8,128)(2,1)} %refs_6_.1), channel_id=1, source_target_pairs={{0,1},{1,0},{2,3},{3,2},{4,5},{5,4},{6,7},{7,6},{8,9},{9,8},{10,11... | collective-permute-start | bytes 3145736 | tf_op jit(solution)/shard_map/ppermute | solution.py:628
  44.5 34.6 %collective-permute-start.7 = (bf16[1024,512]{1,0:T(8,128)(2,1)}, bf16[1024,512]{1,0:T(8,128)(2,1)}, u32[]{:S(2)}, u32[]{:S(2)}) collective-permute-start(bf16[1024,512]{1,0:T(8,128)(2,1)} %refs_8_.1), channel_id=1, source_target_pairs={{0,1},{1,0},{2,3},{3,2},{4,5},{5,4},{6,7},{7,6},{8,9},{9,8},{10,11... | collective-permute-start | bytes 3145736 | tf_op jit(solution)/shard_map/ppermute | solution.py:628
  51.8 24.0 %copy-start.17 = (bf16[1024,256]{1,0:T(8,128)(2,1)}, bf16[1024,256]{1,0:T(8,128)(2,1)S(1)}, u32[]{:S(2)}) copy-start(bf16[1024,256]{1,0:T(8,128)(2,1)S(1)} %get-tuple-element.61.refs_0_) | copy-start | bytes 1572868
  51.8 1.9 collective-permute-start.3
  52.4 23.5 %copy-start.22 = (bf16[1024,256]{1,0:T(8,128)(2,1)}, bf16[1024,256]{1,0:T(8,128)(2,1)S(1)}, u32[]{:S(2)}) copy-start(bf16[1024,256]{1,0:T(8,128)(2,1)S(1)} %convolution_convert_fusion.8.refs_2_.refs_6_) | copy-start | bytes 1572868
  52.8 23.0 %copy-start.23 = (bf16[1024,256]{1,0:T(8,128)(2,1)}, bf16[1024,256]{1,0:T(8,128)(2,1)S(1)}, u32[]{:S(2)}) copy-start(bf16[1024,256]{1,0:T(8,128)(2,1)S(1)} %convolution_convert_fusion.7.refs_3_.refs_7_) | copy-start | bytes 1572868
  53.7 22.1 %copy-start.19 = (bf16[1024,256]{1,0:T(8,128)(2,1)}, bf16[1024,256]{1,0:T(8,128)(2,1)S(1)}, u32[]{:S(2)}) copy-start(bf16[1024,256]{1,0:T(8,128)(2,1)S(1)} %collective-permute-done.3.refs_1_) | copy-start | bytes 1572868
  53.7 23.1 %copy-start.21 = (bf16[256,512]{1,0:T(8,128)(2,1)S(1)}, bf16[256,512]{1,0:T(8,128)(2,1)}, u32[]{:S(2)}) copy-start(bf16[256,512]{1,0:T(8,128)(2,1)} %refs_4_.2) | copy-start | bytes 786436
  76.7 2.4 collective-permute-start.4
  76.8 2.3 collective-permute-start.5
  101.6 12.0 %collective-permute-start.15 = (bf16[256,512]{1,0:T(8,128)(2,1)S(1)}, bf16[256,512]{1,0:T(8,128)(2,1)S(1)}, u32[]{:S(2)}, u32[]{:S(2)}) collective-permute-start(bf16[256,512]{1,0:T(8,128)(2,1)S(1)} %convolution_convert_fusion.9), channel_id=1, source_target_pairs={{0,1},{1,0},{2,3},{3,2},{4,5},{5,4},{6,7},{7,6},{8,9},{9,8},{10,11... | collective-permute-start | bytes 786440 | tf_op jit(solution)/shard_map/ppermute | solution.py:634
  101.8 12.3 %collective-permute-start.8 = (bf16[1024,256]{1,0:T(8,128)(2,1)S(1)}, bf16[1024,256]{1,0:T(8,128)(2,1)S(1)}, u32[]{:S(2)}, u32[]{:S(2)}) collective-permute-start(bf16[1024,256]{1,0:T(8,128)(2,1)S(1)} %get-tuple-element.68), channel_id=1, source_target_pairs={{0,1},{1,0},{2,3},{3,2},{4,5},{5,4},{6,7},{7,6},{8,9},{9,8},{10,11... | collective-permute-start | bytes 1572872 | tf_op jit(solution)/shard_map/ppermute | solution.py:634
  113.1 45.3 %collective-permute-start.17 = (bf16[1024,512]{1,0:T(8,128)(2,1)}, bf16[1024,512]{1,0:T(8,128)(2,1)}, u32[]{:S(2)}, u32[]{:S(2)}) collective-permute-start(bf16[1024,512]{1,0:T(8,128)(2,1)} %convolution_convert_fusion.3), channel_id=1, source_target_pairs={{0,1},{1,0},{2,3},{3,2},{4,5},{5,4},{6,7},{7,6},{8,9},{9,8},{10,11... | collective-permute-start | bytes 3145736 | tf_op jit(solution)/shard_map/ppermute | solution.py:634
  113.3 48.0 %collective-permute-start.16 = (bf16[1024,512]{1,0:T(8,128)(2,1)}, bf16[1024,512]{1,0:T(8,128)(2,1)}, u32[]{:S(2)}, u32[]{:S(2)}) collective-permute-start(bf16[1024,512]{1,0:T(8,128)(2,1)} %convolution_convert_fusion.5), channel_id=1, source_target_pairs={{0,1},{1,0},{2,3},{3,2},{4,5},{5,4},{6,7},{7,6},{8,9},{9,8},{10,11... | collective-permute-start | bytes 3145736 | tf_op jit(solution)/shard_map/ppermute | solution.py:634
  139.2 8.8 %collective-permute-start.9 = (bf16[1024,256]{1,0:T(8,128)(2,1)}, bf16[1024,256]{1,0:T(8,128)(2,1)}, u32[]{:S(2)}, u32[]{:S(2)}) collective-permute-start(bf16[1024,256]{1,0:T(8,128)(2,1)} %get-tuple-element.71), channel_id=1, source_target_pairs={{0,1},{1,0},{2,3},{3,2},{4,5},{5,4},{6,7},{7,6},{8,9},{9,8},{10,11... | collective-permute-start | bytes 1572872 | tf_op jit(solution)/shard_map/ppermute | solution.py:634
  147.6 16.4 %collective-permute-start.12 = (bf16[512,512]{1,0:T(8,128)(2,1)S(1)}, bf16[512,512]{1,0:T(8,128)(2,1)S(1)}, u32[]{:S(2)}, u32[]{:S(2)}) collective-permute-start(bf16[512,512]{1,0:T(8,128)(2,1)S(1)} %get-tuple-element.87), channel_id=1, source_target_pairs={{0,1},{1,0},{2,3},{3,2},{4,5},{5,4},{6,7},{7,6},{8,9},{9,8},{10,11... | collective-permute-start | bytes 1572872 | tf_op jit(solution)/shard_map/ppermute | solution.py:634
  148.1 6.6 %copy-start.4 = (bf16[1024,256]{1,0:T(8,128)(2,1)S(1)}, bf16[1024,256]{1,0:T(8,128)(2,1)}, u32[]{:S(2)}) copy-start(bf16[1024,256]{1,0:T(8,128)(2,1)} %copy-done.3) | copy-start | bytes 1572868
  148.1 8.8 %copy-start.43 = (bf16[1024,512]{1,0:T(8,128)(2,1)S(1)}, bf16[1024,512]{1,0:T(8,128)(2,1)}, u32[]{:S(2)}) copy-start(bf16[1024,512]{1,0:T(8,128)(2,1)} %get-tuple-element.65.refs_2_) | copy-start | bytes 3145732
  154.4 10.7 %collective-permute-start.18 = (bf16[6,256]{1,0:T(8,128)(2,1)S(1)}, bf16[6,256]{1,0:T(8,128)(2,1)S(1)}, u32[]{:S(2)}, u32[]{:S(2)}) collective-permute-start(bf16[6,256]{1,0:T(8,128)(2,1)S(1)} %dynamic-slice_convert_fusion), channel_id=1, source_target_pairs={{0,1},{1,0},{2,3},{3,2},{4,5},{5,4},{6,7},{7,6},{8,9},{9,8},{10,11... | collective-permute-start | bytes 9224 | tf_op jit(solution)/shard_map/ppermute | solution.py:634
  156.4 8.7 %collective-permute-start.13 = (bf16[256,512]{1,0:T(8,128)(2,1)S(1)}, bf16[256,512]{1,0:T(8,128)(2,1)S(1)}, u32[]{:S(2)}, u32[]{:S(2)}) collective-permute-start(bf16[256,512]{1,0:T(8,128)(2,1)S(1)} %convolution_convert_fusion.15), channel_id=1, source_target_pairs={{0,1},{1,0},{2,3},{3,2},{4,5},{5,4},{6,7},{7,6},{8,9},{9,8},{10,11... | collective-permute-start | bytes 786440 | tf_op jit(solution)/shard_map/ppermute | solution.py:634
  158.4 7.5 %collective-permute-start.14 = (bf16[512,256]{1,0:T(8,128)(2,1)S(1)}, bf16[512,256]{1,0:T(8,128)(2,1)S(1)}, u32[]{:S(2)}, u32[]{:S(2)}) collective-permute-start(bf16[512,256]{1,0:T(8,128)(2,1)S(1)} %convolution_convert_fusion.13), channel_id=1, source_target_pairs={{0,1},{1,0},{2,3},{3,2},{4,5},{5,4},{6,7},{7,6},{8,9},{9,8},{10,11... | collective-permute-start | bytes 786440 | tf_op jit(solution)/shard_map/ppermute | solution.py:634
  161.2 5.2 %collective-permute-start.10 = (bf16[1024,256]{1,0:T(8,128)(2,1)S(1)}, bf16[1024,256]{1,0:T(8,128)(2,1)S(1)}, u32[]{:S(2)}, u32[]{:S(2)}) collective-permute-start(bf16[1024,256]{1,0:T(8,128)(2,1)S(1)} %get-tuple-element.76), channel_id=1, source_target_pairs={{0,1},{1,0},{2,3},{3,2},{4,5},{5,4},{6,7},{7,6},{8,9},{9,8},{10,11... | collective-permute-start | bytes 1572872 | tf_op jit(solution)/shard_map/ppermute | solution.py:634
  166.5 32.2 %copy-start.37 = (bf16[2048,512]{1,0:T(8,128)(2,1)S(1)}, bf16[2048,512]{1,0:T(8,128)(2,1)}, u32[]{:S(2)}) copy-start(bf16[2048,512]{1,0:T(8,128)(2,1)} %refs_0_.1) | copy-start | bytes 6291460
  208.0 102.7 %collective-permute-start.11 = (bf16[1024,512]{1,0:T(8,128)(2,1)}, bf16[1024,512]{1,0:T(8,128)(2,1)}, u32[]{:S(2)}, u32[]{:S(2)}) collective-permute-start(bf16[1024,512]{1,0:T(8,128)(2,1)} %get-tuple-element.82), channel_id=1, source_target_pairs={{0,1},{1,0},{2,3},{3,2},{4,5},{5,4},{6,7},{7,6},{8,9},{9,8},{10,11... | collective-permute-start | bytes 3145736 | tf_op jit(solution)/shard_map/ppermute | solution.py:634
  (40 other events, 85.7 us)

commit v3 on v2

--- a/solution.py
+++ b/solution.py
@@ -43,41 +43,67 @@
     return lambda i, sc: (jnp.clip(i - r * per_part, 0, per_part - 1), 0)
 
 
+def per_head(block, heads):
+    head = lax.broadcasted_iota(jnp.int32, block.shape, 1) // DH
+    return jnp.concatenate([jnp.where(head == h, block, jnp.zeros_like(block)) for h in range(heads)], axis=0)
+
+
 def attend_kernel(nblk, per_part, n_q, n_out, heads, bq, bk, sc, *refs):
     q_refs, refs = refs[:n_q], refs[n_q:]
-    k_ref, v_ref, lo_ref, hi_ref = refs[:4]
-    out_refs, (lse_ref, m_ref, l_ref, acc_ref) = refs[4 : 4 + n_out], refs[4 + n_out :]
+    k_ref, vt_ref, lo_ref, hi_ref = refs[:4]
+    out_refs, (lse_ref, acc_ref, q_heads, s_ref, p_ref) = refs[4 : 4 + n_out], refs[4 + n_out :]
     i = pl.program_id(0)
-    q = pick(i, per_part, q_refs)
+    q_heads[...] = per_head(pick(i, per_part, q_refs), heads)
     lo = lo_ref[...]
     hi = hi_ref[...]
-    m_ref[...] = jnp.full_like(m_ref, NEG)
-    l_ref[...] = jnp.zeros_like(l_ref)
     acc_ref[...] = jnp.zeros_like(acc_ref)
     place = lax.broadcasted_iota(jnp.int32, (bk, bq), 0)
-
-    def step(kb, carry):
-        start = pl.multiple_of(kb * bk, bk)
-        k = k_ref[pl.ds(start, bk), :]
-        v = v_ref[pl.ds(start, bk), :]
+    span = [slice(h * bq, (h + 1) * bq) for h in range(heads)]
+    cols = [slice(h * DH, (h + 1) * DH) for h in range(heads)]
+
+    first, end = sc[i], sc[nblk + i]
+
+    def rows(kb):
+        return pl.ds(pl.multiple_of(kb * bk, bk), bk)
+
+    def scores(kb, h):
+        s_ref[:, span[h]] = mm(k_ref[rows(kb), :], q_heads[span[h], :], NT)
+
+    def soften(kb, h, keep, top, total):
+        t = jnp.where(keep, s_ref[:, span[h]] * SCALE2, NEG)
+        new_top = jnp.maximum(top, jnp.max(t, axis=0, keepdims=True))
+        e = jnp.exp2(t - new_top)
+        decay = jnp.exp2(top - new_top)
+        p_ref[:, span[h]] = e.astype(BF16)
+        return new_top, total * decay + jnp.sum(e, axis=0, keepdims=True), decay
+
+    def gather(kb, h, decay):
+        acc_ref[cols[h], :] = acc_ref[cols[h], :] * decay + mm(vt_ref[cols[h], rows(kb)], p_ref[:, span[h]])
+
+    def stage(kb, carry):
+        start = kb * bk
         keep = jnp.logical_and(place >= lo - start, place < hi - start)
+        after = jnp.minimum(kb + 1, end - 1)
+        new = []
         for h in range(heads):
-            cols = slice(h * DH, (h + 1) * DH)
-            s = mm(k[:, cols], q[:, cols], NT) * SCALE2
-            s = jnp.where(keep, s, NEG)
-            m_old = m_ref[h : h + 1, :]
-            m_new = jnp.maximum(m_old, jnp.max(s, axis=0, keepdims=True))
-            p = jnp.exp2(s - m_new)
-            decay = jnp.exp2(m_old - m_new)
-            m_ref[h : h + 1, :] = m_new
-            l_ref[h : h + 1, :] = l_ref[h : h + 1, :] * decay + jnp.sum(p, axis=0, keepdims=True)
-            acc_ref[cols, :] = acc_ref[cols, :] * decay + mm(v[:, cols], p.astype(BF16), TN)
-        return carry
-
-    lax.fori_loop(sc[i], sc[nblk + i], step, 0)
+            top, total, decay = carry[h]
+            if decay is not None:
+                gather(kb - 1, h, decay)
+            new.append(soften(kb, h, keep, top, total))
+            scores(after, h)
+        return new
+
     for h in range(heads):
-        cols = slice(h * DH, (h + 1) * DH)
-        acc_ref[cols, :] = acc_ref[cols, :] / l_ref[h : h + 1, :]
+        scores(first, h)
+    none = jnp.full((1, bq), NEG, F32), jnp.zeros((1, bq), F32), None
+    carry = lax.fori_loop(first + 1, end, stage, stage(first, [none] * heads))
+    for h in range(heads):
+        gather(end - 1, h, carry[h][2])
+    top = [carry[h][0] for h in range(heads)]
+    total = [carry[h][1] for h in range(heads)]
+    for h in range(heads):
+        acc_ref[cols[h], :] = acc_ref[cols[h], :] / total[h]
+        lse_ref[0, h : h + 1, :] = top[h] + jnp.log2(total[h])
     ctx = acc_ref[...].T.astype(BF16)
     for r in range(n_out):
 
@@ -85,10 +111,8 @@
         def _():
             out_refs[r][...] = ctx
 
-    lse_ref[0, :, :] = m_ref[...] + jnp.log2(l_ref[...])
-
-
-def attend(sc, q_parts, keys, values, lo, hi, mp, bq, bk):
+
+def attend(sc, q_parts, keys, values_t, lo, hi, mp, bq, bk):
     tokens, width = sum(q.shape[0] for q in q_parts), keys.shape[1]
     heads = width // DH
     nblk, per_part = tokens // bq, tokens // bq // mp
@@ -96,28 +120,28 @@
         q_specs = [pl.BlockSpec((bq, width), lambda i, sc: (sc[2 * nblk + i], 0))]
     else:
         q_specs = [pl.BlockSpec((bq, width), part_map(r, per_part)) for r in range(mp)]
-    full = pl.BlockSpec(keys.shape, lambda i, sc: (0, 0))
+    full = lambda a: pl.BlockSpec(a.shape, lambda i, sc: (0, 0))
     row = pl.BlockSpec((1, bq), lambda i, sc: (0, i))
-    per_pick = per_part if len(q_parts) > 1 else nblk
     outs = pl.pallas_call(
         functools.partial(attend_kernel, nblk, per_part, len(q_parts), mp, heads, bq, bk),
         grid_spec=pltpu.PrefetchScalarGridSpec(
             num_scalar_prefetch=1,
             grid=(nblk,),
-            in_specs=q_specs + [full, full, row, row],
+            in_specs=q_specs + [full(keys), full(values_t), row, row],
             out_specs=[pl.BlockSpec((bq, width), part_map(r, per_part)) for r in range(mp)]
             + [pl.BlockSpec((1, heads, bq), lambda i, sc: (i, 0, 0))],
             scratch_shapes=[
-                pltpu.VMEM((heads, bq), F32),
-                pltpu.VMEM((heads, bq), F32),
                 pltpu.VMEM((width, bq), F32),
+                pltpu.VMEM((heads * bq, width), BF16),
+                pltpu.VMEM((bk, heads * bq), F32),
+                pltpu.VMEM((bk, heads * bq), BF16),
             ],
         ),
         out_shape=[jax.ShapeDtypeStruct((tokens // mp, width), BF16)] * mp
         + [jax.ShapeDtypeStruct((nblk, heads, bq), F32)],
         compiler_params=params(),
         cost_estimate=cost(4 * tokens * 512 * width, 8 * tokens * width, tokens * 512 * heads),
-    )(sc, *q_parts, keys, values, lo, hi)
+    )(sc, *q_parts, keys, values_t, lo, hi)
     return outs[:mp], outs[mp]
 
 
@@ -125,9 +149,9 @@
     q_refs, refs = refs[:n_q], refs[n_q:]
     do_refs, refs = refs[:n_part], refs[n_part:]
     o_refs, refs = refs[:n_part], refs[n_part:]
-    k_ref, v_ref, lo_ref, hi_ref, lse_ref = refs[:5]
-    dq_refs, refs = refs[5 : 5 + n_q], refs[5 + n_q :]
-    dk_ref, dv_ref, dk_acc, dv_acc, dq_acc, delta_ref = refs
+    k_ref, kt_ref, v_ref, lo_ref, hi_ref, lse_ref = refs[:6]
+    dq_refs, refs = refs[6 : 6 + n_q], refs[6 + n_q :]
+    dk_ref, dv_ref, dk_acc, dv_acc, dq_acc, q_heads, do_heads = refs
     i = pl.program_id(0)
 
     @pl.when(i == 0)
@@ -135,35 +159,33 @@
         dk_acc[...] = jnp.zeros_like(dk_acc)
         dv_acc[...] = jnp.zeros_like(dv_acc)
 
-    q = pick(i, per_part, q_refs)
+    q_heads[...] = per_head(pick(i, per_part, q_refs), heads)
     do = pick(i, per_part, do_refs)
-    o = pick(i, per_part, o_refs)
+    do_heads[...] = per_head(do, heads)
     lo = lo_ref[...]
     hi = hi_ref[...]
-    prod = (do.astype(F32) * o.astype(F32)).T
-    for h in range(heads):
-        delta_ref[h : h + 1, :] = jnp.sum(prod[h * DH : (h + 1) * DH, :], axis=0, keepdims=True)
+    span = [slice(h * bq, (h + 1) * bq) for h in range(heads)]
+    cols = [slice(h * DH, (h + 1) * DH) for h in range(heads)]
+    prod = (do.astype(F32) * pick(i, per_part, o_refs).astype(F32)).T
+    delta = [jnp.sum(prod[cols[h], :], axis=0, keepdims=True) for h in range(heads)]
+    lse = [lse_ref[0, h : h + 1, :] for h in range(heads)]
     dq_acc[...] = jnp.zeros_like(dq_acc)
     place = lax.broadcasted_iota(jnp.int32, (bk, bq), 0)
 
     def step(kb, carry):
         start = pl.multiple_of(kb * bk, bk)
-        k = k_ref[pl.ds(start, bk), :]
-        v = v_ref[pl.ds(start, bk), :]
+        rows = pl.ds(start, bk)
+        kt = kt_ref[:, rows]
         keep = jnp.logical_and(place >= lo - start, place < hi - start)
-        dks, dvs = [], []
+        s = mm(k_ref[rows, :], q_heads[...], NT) * SCALE2
+        dp = mm(v_ref[rows, :], do_heads[...], NT)
+        p = [jnp.where(keep, jnp.exp2(s[:, span[h]] - lse[h]), 0.0) for h in range(heads)]
+        ds = [(p[h] * (dp[:, span[h]] - delta[h])).astype(BF16) for h in range(heads)]
+        p = [p[h].astype(BF16) for h in range(heads)]
+        dv_acc[rows, :] += mm(jnp.concatenate(p, axis=1), do_heads[...])
+        dk_acc[rows, :] += mm(jnp.concatenate(ds, axis=1), q_heads[...])
         for h in range(heads):
-            cols = slice(h * DH, (h + 1) * DH)
-            s = mm(k[:, cols], q[:, cols], NT) * SCALE2 - lse_ref[0, h : h + 1, :]
-            p = jnp.where(keep, jnp.exp2(s), 0.0)
-            dp = mm(v[:, cols], do[:, cols], NT)
-            ds = (p * (dp - delta_ref[h : h + 1, :])).astype(BF16)
-            dvs.append(mm(p.astype(BF16), do[:, cols]))
-            dks.append(mm(ds, q[:, cols]))
-            dq_acc[cols, :] += mm(k[:, cols], ds, TN)
-        rows = pl.ds(start, bk)
-        dk_acc[rows, :] += jnp.concatenate(dks, axis=1)
-        dv_acc[rows, :] += jnp.concatenate(dvs, axis=1)
+            dq_acc[cols[h], :] += mm(kt[cols[h], :], ds[h])
         return carry
 
     lax.fori_loop(sc[i], sc[nblk + i], step, 0)
@@ -183,7 +205,7 @@
         dv_ref[...] = dv_acc[...].astype(BF16)
 
 
-def attend_back(sc, q_parts, do_parts, o_parts, keys, values, lo, hi, lse, mp, bq, bk):
+def attend_back(sc, q_parts, do_parts, o_parts, keys, keys_t, values, lo, hi, lse, mp, bq, bk):
     tokens, width = sum(q.shape[0] for q in q_parts), keys.shape[1]
     heads = width // DH
     nblk, per_part = tokens // bq, tokens // bq // mp
@@ -192,7 +214,7 @@
         q_specs = [pl.BlockSpec((bq, width), lambda i, sc: (sc[2 * nblk + i], 0))]
     else:
         q_specs = parts
-    full = pl.BlockSpec(keys.shape, lambda i, sc: (0, 0))
+    full = lambda a: pl.BlockSpec(a.shape, lambda i, sc: (0, 0))
     row = pl.BlockSpec((1, bq), lambda i, sc: (0, i))
     outs = pl.pallas_call(
         functools.partial(attend_back_kernel, nblk, per_part, len(q_parts), mp, heads, bq, bk),
@@ -202,20 +224,22 @@
             in_specs=q_specs
             + parts
             + parts
-            + [full, full, row, row, pl.BlockSpec((1, heads, bq), lambda i, sc: (i, 0, 0))],
-            out_specs=q_specs + [full, full],
+            + [full(keys), full(keys_t), full(values), row, row]
+            + [pl.BlockSpec((1, heads, bq), lambda i, sc: (i, 0, 0))],
+            out_specs=q_specs + [full(keys), full(keys)],
             scratch_shapes=[
                 pltpu.VMEM(keys.shape, F32),
                 pltpu.VMEM(keys.shape, F32),
                 pltpu.VMEM((width, bq), F32),
-                pltpu.VMEM((heads, bq), F32),
+                pltpu.VMEM((heads * bq, width), BF16),
+                pltpu.VMEM((heads * bq, width), BF16),
             ],
         ),
         out_shape=[jax.ShapeDtypeStruct(q.shape, BF16) for q in q_parts]
         + [jax.ShapeDtypeStruct(keys.shape, BF16)] * 2,
         compiler_params=params(),
         cost_estimate=cost(10 * tokens * 512 * width, 12 * tokens * width, tokens * 512 * heads),
-    )(sc, *q_parts, *do_parts, *o_parts, keys, values, lo, hi, lse)
+    )(sc, *q_parts, *do_parts, *o_parts, keys, keys_t, values, lo, hi, lse)
     return outs[: len(q_parts)], outs[-2], outs[-1]
 
 
@@ -595,6 +619,74 @@
     return outs + [sums[-1]]
 
 
+def across(r, shift, devices):
+    return [(i, i ^ (r << shift)) for i in range(devices)]
+
+
+def cut(blocks, shift, bits, me):
+    place = (me >> shift) % (1 << bits)
+    return [lax.dynamic_index_in_dim(blocks, place ^ r, 0, keepdims=False) for r in range(1 << bits)]
+
+
+def scatter_step(blocks, shift, devices):
+    return blocks[:1] + [lax.ppermute(b, "batch", across(r, shift, devices)) for r, b in enumerate(blocks) if r]
+
+
+def add_up(blocks):
+    total = blocks[0].astype(F32)
+    for b in blocks[1:]:
+        total += b.astype(F32)
+    return total.astype(BF16)
+
+
+def gather_step(block, shift, bits, devices):
+    return [block] + [lax.ppermute(block, "batch", across(r, shift, devices)) for r in range(1, 1 << bits)]
+
+
+def in_order(pieces, place):
+    return jnp.stack(
+        [lax.select_n(place ^ c, *pieces) if len(pieces) > 1 else pieces[0] for c in range(len(pieces))]
+    )
+
+
+def lay_kernel(n, rows, sc, *refs):
+    pieces, outs = refs[:n], refs[n:]
+    c = pl.program_id(0)
+    for r in range(n):
+
+        @pl.when((sc[0] ^ c) == r)
+        def _():
+            at = 0
+            for out, count in zip(outs, rows):
+                out[...] = pieces[r][:, at : at + count, :].astype(F32).reshape(out.shape)
+                at += count
+
+
+def lay_out(pieces, place, shapes, rows):
+    n = len(pieces)
+    d = pieces[0].shape[-1]
+    if any(count % 16 for count in rows):
+        blocks = in_order(pieces, place)
+        flat = blocks.reshape(-1, *blocks.shape[2:]).astype(F32)
+        at, outs = 0, []
+        for shape, count in zip(shapes, rows):
+            outs.append(flat[:, at : at + count].reshape(shape))
+            at += count
+        return outs
+    return pl.pallas_call(
+        functools.partial(lay_kernel, n, rows),
+        grid_spec=pltpu.PrefetchScalarGridSpec(
+            num_scalar_prefetch=1,
+            grid=(n,),
+            in_specs=[whole(p) for p in pieces],
+            out_specs=[pl.BlockSpec((s[0] // n, d), lambda i, sc: (i, 0)) for s in shapes],
+        ),
+        out_shape=[jax.ShapeDtypeStruct(s, F32) for s in shapes],
+        compiler_params=params(),
+        cost_estimate=cost(0, sum(s[0] * d * 6 for s in shapes)),
+    )(place.reshape(1).astype(jnp.int32), *pieces)
+
+
 def shards(
     block_input_slots,
     memory,
@@ -661,19 +753,19 @@
     as_row = lambda v: v.reshape(1, tokens).astype(jnp.int32)
     self_lo, self_hi, cross_lo, cross_hi = map(as_row, (self_lo, self_hi, cross_lo, cross_hi))
 
-    proj = [
-        jnp.dot(block_input_slots, self_qkv[c], preferred_element_type=F32).astype(BF16) for c in range(3)
-    ]
-    pair = [jnp.dot(memory, cross_kv[c], preferred_element_type=F32).astype(BF16) for c in range(2)]
+    proj = [mm(block_input_slots, self_qkv[c]).astype(BF16) for c in range(3)]
+    pair = [mm(memory, cross_kv[c]).astype(BF16) for c in range(2)]
+    self_kt, self_vt = proj[1].T, proj[2].T
+    cross_kt, cross_vt = pair[0].T, pair[1].T
     ctx_parts, self_lse = attend(
-        self_table, proj[:1], proj[1], proj[2], self_lo, self_hi, mp, bq, bk
+        self_table, proj[:1], proj[1], self_vt, self_lo, self_hi, mp, bq, bk
     )
     ctx = exchange(ctx_parts)
     me_row = me.reshape(1).astype(jnp.int32)
     n1, xhat1, rstd1, qc = post_self(me_row, block_input_slots, ctx, wo, cq, gain, shift, share, bt)
     qc_parts = exchange(qc)
     cctx_parts, cross_lse = attend(
-        cross_table, qc_parts, pair[0], pair[1], cross_lo, cross_hi, mp, bq, bk
+        cross_table, qc_parts, pair[0], cross_vt, cross_lo, cross_hi, mp, bq, bk
     )
     cctx = exchange(cctx_parts)
     layer_output, da2, n2, e3, e2, dcctx, hid, dpre, small23 = middle(
@@ -691,13 +783,23 @@
             total += g.astype(F32)
         return total
 
-    down_grad = collect(grads(hid, [e3] * mp))
-    up_grad = collect(grads(dpre, [n2] * mp))
-    cross_out_grad = collect(grads(cctx, [e2] * mp))
+    early = [
+        collect(grads(dpre, [n2] * mp)).astype(BF16),
+        collect(grads(hid, [e3] * mp)).astype(BF16),
+        collect(grads(cctx, [e2] * mp)).astype(BF16),
+    ]
+    row = lax.axis_index("batch")
+    near, far = 2, devices.bit_length() - 3
+    blocks = jnp.concatenate([g.reshape(devices, -1, d) for g in early], axis=1)
+    blocks = blocks.reshape(1 << near, 1 << far, -1, d)
+    dcctx_parts, blocks = lax.optimization_barrier((dcctx_parts, cut(blocks, 0, near, row)))
+    blocks = scatter_step(blocks, 0, devices)
     dqc_parts, dkc, dvc = attend_back(
-        cross_table, qc_parts, dcctx_parts, cctx_parts, pair[0], pair[1], cross_lo, cross_hi, cross_lse, mp, bq, bk
+        cross_table, qc_parts, dcctx_parts, cctx_parts, pair[0], cross_kt, pair[1], cross_lo, cross_hi, cross_lse, mp, bq, bk
     )
     dqc = exchange(dqc_parts)
+    dqc, blocks = lax.optimization_barrier((dqc, cut(add_up(blocks), near, far, row)))
+    blocks = scatter_step(blocks, near, devices)
     da1, e1, dctx, small1 = pre_self(dqc, cq, wo, da2, xhat1, rstd1, gain, bt)
     dctx_parts = exchange(dctx)
     mem_bt = min(256, mem_share)
@@ -708,9 +810,13 @@
     cross_kv_grad = jnp.stack([mm(memory, g, TN) for g in (dkc, dvc)])
     cross_query_grad = collect(grads([n1] * mp, dqc))
     self_out_grad = collect(grads(ctx, [e1] * mp))
+    dctx_parts, block = lax.optimization_barrier((dctx_parts, add_up(blocks)))
+    blocks = gather_step(block, near, far, devices)
     (dq,), dk, dv = attend_back(
-        self_table, proj[:1], dctx_parts, ctx_parts, proj[1], proj[2], self_lo, self_hi, self_lse, mp, bq, bk
-    )
+        self_table, proj[:1], dctx_parts, ctx_parts, proj[1], self_kt, proj[2], self_lo, self_hi, self_lse, mp, bq, bk
+    )
+    dq, block = lax.optimization_barrier((dq, in_order(blocks, row >> near)))
+    spread_out = gather_step(block, 0, near, devices)
     input_parts = input_part(q_block.astype(jnp.int32), [dq, dk, dv], self_qkv, mp, bq)
     input_grad = collect(input_parts) + da1
     self_qkv_grad = jnp.stack([mm(block_input_slots, g, TN) for g in (dq, dk, dv)])
@@ -729,16 +835,16 @@
                 self_out_grad,
                 cross_query_grad,
                 cross_kv_grad,
-                cross_out_grad,
-                up_grad,
-                down_grad,
             )
         ],
-        (3, 1, 1, 2, 1, 2, 2),
+        (3, 1, 1, 2),
         small.astype(BF16),
         devices,
     )
-    summed = [g.astype(F32) for g in summed]
+    up_grad, down_grad, cross_out_grad = lay_out(
+        spread_out, row % (1 << near), [g.shape for g in early], [g.shape[0] // devices for g in early]
+    )
+    summed = [g.astype(F32) for g in summed] + [cross_out_grad, up_grad, down_grad]
     small = small.astype(F32).T
     return (layer_output, input_grad, memory_grad, *summed, small[:, :3], small[:, 3:6])
 

time: 320 us -> 274 us (0.86); the launches traced: 314 us -> 272 us
  Pallas kernels: 241 us -> 172 us
  starting transfers between devices: 5.26 us -> 28.1 us
  waiting for transfers between devices: 3.53 us -> 8.02 us
  local copies, waits for them, and re-layouts: 15.1 us -> 19.5 us
  other arithmetic: 19.7 us -> 15.3 us
    pallas_call x1, Pallas kernels: 90.8 us -> 58.3 us  [all_sum(): pl.pallas_call(functools.partial(all_sum_kernel, plan, nbits, len(keep)),...]
    pallas_call x2, Pallas kernels: 52.9 us -> 28.1 us  [attend(): pl.pallas_call(functools.partial(attend_kernel, nblk, per_part, len(q_par...]
    ppermute x0 -> x12, starting transfers between devices: none -> 22.9 us  [the longest x6 14.8 us: scatter_step(): lax.ppermute(b, 'batch', across(r, shift, devices))]
    pallas_call x2, Pallas kernels: 56.5 us -> 40.4 us  [attend_back(): pl.pallas_call(functools.partial(attend_back_kernel, nblk, per_part, len(...]
    dot_general x5 -> x0, matrix products: 7.66 us -> none  [the longest x3 6.8 us: shards(): jnp.dot(block_input_slots, self_qkv[c], preferred_element_type=F32)]
    convert_element_type x9 -> x8, other arithmetic: 13.2 us -> 6.45 us  [the longest x4 4.01 us: shards(): g.astype(F32)]
    convert_element_type x0 -> x4, local copies, waits for them, and re-layouts: none -> 6.61 us  [the longest x2 4.13 us: shards(): proj = [mm(block_input_slots, self_qkv[c]).astype(BF16) for c in range(3)]]
    dot_general x15 -> x20, matrix products: 20.5 us -> 27 us  [mm(): return lax.dot_general(a, b, dims, preferred_element_type=F32)]
  transfers between devices with their start and end apart: 19 -> 31, of which waited for: 4 -> 7; matrix products, arithmetic and copies ran while one was open for 12% -> 13% of each run, Pallas kernels for 48% -> 47%
where the time goes in v3:
time: 274 us; the launch traced here: 272 us
  Pallas kernels  172 us (63%)
  starting transfers between devices  28.1 us (10%)
  matrix products  27 us (10%)
  local copies, waits for them, and re-layouts  19.5 us (7%)
  other arithmetic  15.3 us (6%)
  waiting for transfers between devices  8.02 us (3%)
    pallas_call x1, Pallas kernels, all_sum(): pl.pallas_call(functools.partial(all_sum_kernel, plan, nbits, len(keep)),...  58.3 us
    pallas_call x2, Pallas kernels, attend_back(): pl.pallas_call(functools.partial(attend_back_kernel, nblk, per_part, len(...  40.4 us
    pallas_call x2, Pallas kernels, attend(): pl.pallas_call(functools.partial(attend_kernel, nblk, per_part, len(q_par...  28.1 us
    dot_general x20, matrix products, mm(): return lax.dot_general(a, b, dims, preferred_element_type=F32)  27 us
    pallas_call x1, Pallas kernels, middle(): pl.pallas_call(functools.partial(middle_kernel, mp), grid=(share // bt,),...  19.5 us
    ppermute x6, starting transfers between devices, scatter_step(): lax.ppermute(b, 'batch', across(r, shift, devices))  14.8 us
    pallas_call x2, Pallas kernels, input_part(): pl.pallas_call(functools.partial(part_kernel, len(grads), mp, per_part),...  10.6 us
    ppermute x6, starting transfers between devices, gather_step(): lax.ppermute(block, 'batch', across(r, shift, devices))  8.17 us
  transfers between devices with their start and end apart: 31, of which 7 were waited for; matrix products, arithmetic and copies ran while one was open for 13% of the time, Pallas kernels for 47%

profile of v3, /device:TPU:0, one launch (start us, length us, event | category | flops | bytes accessed | tf_op | source)
XLA Modules:
  0.0 271.6 jit_solution(5187549005511954487)
XLA Ops:
  0.7 3.5 %convolution_convert_fusion.1 = bf16[2048,256]{0,1:T(8,128)(2,1)} fusion(bf16[2048,512]{1,0:T(8,128)(2,1)} %refs_0_.1, bf16[3,512,256]{2,1,0:T(8,128)(2,1)} %refs_3_.5), kind=kOutput, calls=%fused_computation.1 | convolution fusion | flops 537395200 | bytes 3407872 | tf_op jit(solution)/shard_map/dot_general | solution.py:24
  4.2 1.7 convolution_convert_fusion.refs_7_
  5.9 1.7 convolution_convert_fusion.2.refs_0_
  9.3 1.5 copy.61.refs_1_.refs_5_
  10.8 2.6 copy.62.refs_2_
  14.8 16.6 %shard_map.229 = (bf16[1024,256]{1,0:T(8,128)(2,1)S(1)}, bf16[1024,256]{1,0:T(8,128)(2,1)S(1)}, f32[8,4,256]{2,1,0:T(4,128)S(1)}) custom-call(s32[24]{0:T(128)S(1)} %get-tuple-element.165.sc, bf16[2048,256]{1,0:T(8,128)(2,1)S(1)} %copy-done.25, bf16[2048,256]{1,0:T(8,128)(2,1)S(1)} %copy.61.refs_1_.refs_5_, bf16[256,2048]{1,0:T(8,128)(2,1)} %copy.62.refs_2_, ...), custom_call_target="tpu_custom_call" | custom-call | flops 1073741824 | bytes 4194304 | tf_op jit(solution)/shard_map/pallas_call | solution.py:125
  35.0 5.3 %shard_map.230 = (bf16[1024,512]{1,0:T(8,128)(2,1)}, f32[1024,512]{1,0:T(8,128)}, f32[1024,1]{1,0:T(8,128)S(1)}, bf16[1024,256]{1,0:T(8,128)(2,1)S(1)}, bf16[1024,256]{1,0:T(8,128)(2,1)}) custom-call(s32[1]{0:T(128)} %bitcast.3.sc, bf16[2048,512]{1,0:T(8,128)(2,1)} %refs_0_.1, bf16[1024,256]{1,0:T(8,128)(2,1)S(1)} %get-tuple-element.76.refs_1_.refs_3_, ...), custom_call_target="tpu_custom_call" | custom-call | flops 1073741824 | bytes 6291456 | tf_op jit(solution)/shard_map/pallas_call | solution.py:289
  46.6 11.5 %shard_map.231 = (bf16[1024,256]{1,0:T(8,128)(2,1)S(1)}, bf16[1024,256]{1,0:T(8,128)(2,1)}, f32[8,4,256]{2,1,0:T(4,128)S(1)}) custom-call(s32[24]{0:T(128)S(1)} %get-tuple-element.166.sc, bf16[1024,256]{1,0:T(8,128)(2,1)S(1)} %get-tuple-element.78.refs_0_, bf16[1024,256]{1,0:T(8,128)(2,1)} %collective-permute-done.3.refs_1_, ...), custom_call_target="tpu_custom_call" | custom-call | flops 1073741824 | bytes 4194304 | tf_op jit(solution)/shard_map/pallas_call | solution.py:125
  59.6 1.8 collective-permute-done.5.refs_5_
  62.4 19.5 %shard_map.232 = (bf16[1024,512]{1,0:T(8,128)(2,1)}, f32[1024,512]{1,0:T(8,128)}, bf16[1024,512]{1,0:T(8,128)(2,1)S(1)}, bf16[1024,512]{1,0:T(8,128)(2,1)}, bf16...) custom-call(bf16[1024,256]{1,0:T(8,128)(2,1)S(1)} %copy-done.27, ...), custom_call_target="tpu_custom_call" | custom-call | flops 9663676416 | bytes 8388608 | tf_op jit(solution)/shard_map/pallas_call | solution.py:387
  81.9 3.0 %convolution_convert_fusion.6 = bf16[1024,512]{1,0:T(8,128)(2,1)S(1)} fusion(bf16[1024,1024]{1,0:T(8,128)(2,1)} %get-tuple-element.86, bf16[1024,512]{1,0:T(8,128)(2,1)S(1)} %get-tuple-element.87), kind=kOutput, calls=%fused_computation.10 | convolution fusion | flops 1074266112 | bytes 4194304 | tf_op jit(solution)/shard_map/dot_general | solution.py:24
  94.0 2.6 collective-permute-start.13
  96.6 1.5 collective-permute-start.14
  98.2 15.4 %shard_map.233 = (bf16[1024,256]{1,0:T(8,128)(2,1)S(1)}, bf16[1024,256]{1,0:T(8,128)(2,1)}, bf16[1024,256]{1,0:T(8,128)(2,1)S(1)}, bf16[1024,256]{1,0:T(8,128)(2,1)S(1)}) custom-call(s32[24]{0:T(128)S(1)} %get-tuple-element.166.sc, bf16[1024,256]{1,0:T(8,128)(2,1)S(1)} %get-tuple-element.78.refs_0_, bf16[1024,256]{1,0:T(8,128)(2,1)} %collective-permute-done.3.refs_1_, ...), custom_call_target="tpu_custom_call" | custom-call | flops 2684354560 | bytes 6291456 | tf_op jit(solution)/shard_map/pallas_call | solution.py:219
  113.6 2.7 %shard_map.237 = (f32[512,512]{1,0:T(8,128)S(1)}, bf16[512,512]{1,0:T(8,128)(2,1)}) custom-call(s32[4]{0:T(128)S(1)} %add.258.sc, bf16[1024,256]{1,0:T(8,128)(2,1)S(1)} %get-tuple-element.124.refs_0_, bf16[1024,256]{1,0:T(8,128)(2,1)S(1)} %get-tuple-element.125.refs_1_, bf16[2,512,256]{2,1,0:T(8,128)(2,1)S(1)} %copy-done.18), custom_call_target="tpu_custom_call" | custom-call | flops 536870912 | bytes 3145728 | tf_op jit(solution)/shard_map/pallas_call | solution.py:477
  119.9 2.2 convert_add_fusion
  122.1 2.8 %collective-permute-done.14 = bf16[4,144,512]{2,1,0:T(8,128)(2,1)} collective-permute-done((bf16[4,144,512]{2,1,0:T(8,128)(2,1)}, bf16[4,144,512]{2,1,0:T(8,128)(2,1)}, u32[]{:S(2)}, u32[]{:S(2)}) %collective-permute-start.14) | collective-permute-done | bytes 589856 | tf_op jit(solution)/shard_map/ppermute | solution.py:632
  124.9 1.7 add_convert_fusion.2
  126.7 1.7 collective-permute-start.17
  128.4 8.9 %collective-permute-start.18 = (bf16[144,512]{1,0:T(8,128)(2,1)S(1)}, bf16[144,512]{1,0:T(8,128)(2,1)S(1)}, u32[]{:S(2)}, u32[]{:S(2)}) collective-permute-start(bf16[144,512]{1,0:T(8,128)(2,1)S(1)} %get-tuple-element.111), channel_id=1, source_target_pairs={{0,16},{2,18},{4,20},{6,22},{8,24},{10,26},{12,28},{14,30},{16,0},... | collective-permute-start | bytes 442376 | tf_op jit(solution)/shard_map/ppermute | solution.py:632
  137.3 1.5 convolution_convert_fusion.11
  138.9 6.2 %shard_map.234 = (f32[1024,512]{1,0:T(8,128)}, bf16[1024,512]{1,0:T(8,128)(2,1)}, bf16[1024,256]{1,0:T(8,128)(2,1)S(1)}, bf16[1024,256]{1,0:T(8,128)(2,1)S(1)}, f32[2,512]{1,0:T(2,128)S(1)}) custom-call(bf16[1024,256]{1,0:T(8,128)(2,1)S(1)} %copy-done.14, bf16[1024,256]{1,0:T(8,128)(2,1)} %collective-permute-done.12.refs_1_, bf16[512,256]{1,0:T(8,128)(2,1)S(1)} %copy-done.3, ...), custom_call_target="tpu_custom_call" | custom-call | flops 1073741824 | bytes 7340032 | tf_op jit(solution)/shard_map/pallas_call | solution.py:443
  145.8 1.7 convolution_convert_fusion.13
  151.4 2.1 collective-permute-start.20
  153.6 2.2 collective-permute-start.21
  156.1 25.0 %shard_map.235 = (bf16[2048,256]{1,0:T(8,128)(2,1)S(1)}, bf16[2048,256]{1,0:T(8,128)(2,1)}, bf16[2048,256]{1,0:T(8,128)(2,1)}) custom-call(s32[24]{0:T(128)S(1)} %get-tuple-element.165.sc, bf16[2048,256]{1,0:T(8,128)(2,1)} %convolution_convert_fusion.2.refs_0_, bf16[1024,256]{1,0:T(8,128)(2,1)S(1)} %get-tuple-element.113.refs_1_, ...), custom_call_target="tpu_custom_call" | custom-call | flops 2684354560 | bytes 6291456 | tf_op jit(solution)/shard_map/pallas_call | solution.py:219
  181.1 1.9 fusion.10
  184.5 7.9 %shard_map.236 = (f32[1024,512]{1,0:T(8,128)}, bf16[1024,512]{1,0:T(8,128)(2,1)}) custom-call(s32[8]{0:T(128)S(1)} %get-tuple-element.169.sc, bf16[2048,256]{1,0:T(8,128)(2,1)S(1)} %get-tuple-element.118.refs_0_, bf16[2048,256]{1,0:T(8,128)(2,1)S(1)} %copy-done.28, bf16[2048,256]{1,0:T(8,128)(2,1)} %get-tuple-element.120.refs_2_, ...), custom_call_target="tpu_custom_call" | custom-call | flops 1610612736 | bytes 6291456 | tf_op jit(solution)/shard_map/pallas_call | solution.py:477
  193.3 3.4 %collective-permute-start.30 = (bf16[4,144,512]{2,1,0:T(8,128)(2,1)S(1)}, bf16[4,144,512]{2,1,0:T(8,128)(2,1)}, u32[]{:S(2)}, u32[]{:S(2)}) collective-permute-start(bf16[4,144,512]{2,1,0:T(8,128)(2,1)S(1)} %pad_maximum_fusion.2.refs_0_), channel_id=1, source_target_pairs={{0,6},{2,4},{4,2},{6,0},{8,14},{10,12},{12,10},{14,8},{16,22},{18,... | collective-permute-start | bytes 1769480 | tf_op jit(solution)/shard_map/ppermute | solution.py:643
  201.7 58.3 %shard_map.238 = (bf16[1536,256]{1,0:T(8,128)(2,1)S(1)}, bf16[256,512]{1,0:T(8,128)(2,1)S(1)}, bf16[512,256]{1,0:T(8,128)(2,1)S(1)}, bf16[1024,256]{1,0:T(8,128)(2,1)S(1)}, bf16[16,256]{1,0:T(8,128)(2,1)S(1)}) custom-call(bf16[1536,256]{1,0:T(8,128)(2,1)S(1)} %bitcast.134, bf16[256,512]{1,0:T(8,128)(2,1)S(1)} %copy-done.16, bf16[512,256]{1,0:T(8,128)(2,1)S(1)} %copy-done.15, ...), custom_call_target="tpu_custom_call" | custom-call | tf_op jit(solution)/shard_map/pallas_call | solution.py:603
  264.7 3.9 %shard_map.239 = (f32[1024,512]{1,0:T(8,128)}, f32[1024,512]{1,0:T(8,128)}, f32[256,512]{1,0:T(8,128)}) custom-call(s32[1]{0:T(128)} %bitcast.47.sc, bf16[4,144,512]{2,1,0:T(8,128)(2,1)S(1)} %pad_maximum_fusion.2.refs_0_, bf16[4,144,512]{2,1,0:T(8,128)(2,1)S(1)} %collective-permute-done.28.refs_1_, bf16[4,144,512]{2,1,0:T(8,128)(2,1)} %collective-permute-done.29.refs_2_, ...), custom_call_target="tpu_custom_call" | custom-call | bytes 7077888 | tf_op jit(solution)/shard_map/pallas_call | solution.py:676
  268.5 3.1 %add_add_fusion = f32[1024,512]{1,0:T(8,128)} fusion(f32[1024,512]{1,0:T(8,128)S(1)} %copy-done.32, f32[1024,512]{1,0:T(8,128)S(1)} %copy-done.33, bf16[1024,512]{1,0:T(8,128)(2,1)} %collective-permute-done.23), kind=kLoop, calls=%fused_computation.4 | loop fusion | flops 1572864 | bytes 7340032 | tf_op jit(solution)/shard_map/add | solution.py:821
  (213 shorter events, 44.6 us)
Async XLA Ops:
  0.6 40.9 %copy-start = (bf16[1024,512]{1,0:T(8,128)(2,1)S(1)}, bf16[1024,512]{1,0:T(8,128)(2,1)}, u32[]{:S(2)}) copy-start(bf16[1024,512]{1,0:T(8,128)(2,1)} %param.15) | copy-start | bytes 3145732
  31.4 3.6 %collective-permute-start = (bf16[1024,256]{1,0:T(8,128)(2,1)S(1)}, bf16[1024,256]{1,0:T(8,128)(2,1)S(1)}, u32[]{:S(2)}, u32[]{:S(2)}) collective-permute-start(bf16[1024,256]{1,0:T(8,128)(2,1)S(1)} %get-tuple-element.77.refs_4_), channel_id=1, source_target_pairs={{0,1},{1,0},{2,3},{3,2},{4,5},{5,4},{6,7},{7,6},{8,9},{9,8},{10,11... | collective-permute-start | bytes 1572872 | tf_op jit(solution)/shard_map/ppermute | solution.py:726
  32.0 2.3 collective-permute-start.1
  32.0 2.9 %collective-permute-start.2 = (bf16[512,256]{1,0:T(8,128)(2,1)S(1)}, bf16[512,256]{1,0:T(8,128)(2,1)S(1)}, u32[]{:S(2)}, u32[]{:S(2)}) collective-permute-start(bf16[512,256]{1,0:T(8,128)(2,1)S(1)} %copy-done.3), channel_id=1, source_target_pairs={{0,1},{1,0},{2,3},{3,2},{4,5},{5,4},{6,7},{7,6},{8,9},{9,8},{10,11... | collective-permute-start | bytes 786440 | tf_op jit(solution)/shard_map/ppermute | solution.py:720
  32.5 28.9 %collective-permute-start.6 = (bf16[1024,512]{1,0:T(8,128)(2,1)}, bf16[1024,512]{1,0:T(8,128)(2,1)}, u32[]{:S(2)}, u32[]{:S(2)}) collective-permute-start(bf16[1024,512]{1,0:T(8,128)(2,1)} %refs_6_.1), channel_id=1, source_target_pairs={{0,1},{1,0},{2,3},{3,2},{4,5},{5,4},{6,7},{7,6},{8,9},{9,8},{10,11... | collective-permute-start | bytes 3145736 | tf_op jit(solution)/shard_map/ppermute | solution.py:720
  32.6 28.8 %collective-permute-start.7 = (bf16[1024,512]{1,0:T(8,128)(2,1)}, bf16[1024,512]{1,0:T(8,128)(2,1)}, u32[]{:S(2)}, u32[]{:S(2)}) collective-permute-start(bf16[1024,512]{1,0:T(8,128)(2,1)} %refs_8_.1), channel_id=1, source_target_pairs={{0,1},{1,0},{2,3},{3,2},{4,5},{5,4},{6,7},{7,6},{8,9},{9,8},{10,11... | collective-permute-start | bytes 3145736 | tf_op jit(solution)/shard_map/ppermute | solution.py:720
  41.2 5.4 %collective-permute-start.3 = (bf16[1024,256]{1,0:T(8,128)(2,1)}, bf16[1024,256]{1,0:T(8,128)(2,1)}, u32[]{:S(2)}, u32[]{:S(2)}) collective-permute-start(bf16[1024,256]{1,0:T(8,128)(2,1)} %get-tuple-element.79), channel_id=1, source_target_pairs={{0,1},{1,0},{2,3},{3,2},{4,5},{5,4},{6,7},{7,6},{8,9},{9,8},{10,11... | collective-permute-start | bytes 1572872 | tf_op jit(solution)/shard_map/ppermute | solution.py:726
  58.9 2.5 collective-permute-start.4
  59.0 2.4 collective-permute-start.5
  86.3 5.4 %collective-permute-start.9 = (bf16[1024,512]{1,0:T(8,128)(2,1)S(1)}, bf16[1024,512]{1,0:T(8,128)(2,1)S(1)}, u32[]{:S(2)}, u32[]{:S(2)}) collective-permute-start(bf16[1024,512]{1,0:T(8,128)(2,1)S(1)} %convolution_convert_fusion.5), channel_id=1, source_target_pairs={{0,1},{1,0},{2,3},{3,2},{4,5},{5,4},{6,7},{7,6},{8,9},{9,8},{10,11... | collective-permute-start | bytes 3145736 | tf_op jit(solution)/shard_map/ppermute | solution.py:726
  88.1 3.9 %collective-permute-start.10 = (bf16[1024,512]{1,0:T(8,128)(2,1)S(1)}, bf16[1024,512]{1,0:T(8,128)(2,1)S(1)}, u32[]{:S(2)}, u32[]{:S(2)}) collective-permute-start(bf16[1024,512]{1,0:T(8,128)(2,1)S(1)} %convolution_convert_fusion.3), channel_id=1, source_target_pairs={{0,1},{1,0},{2,3},{3,2},{4,5},{5,4},{6,7},{7,6},{8,9},{9,8},{10,11... | collective-permute-start | bytes 3145736 | tf_op jit(solution)/shard_map/ppermute | solution.py:726
  88.8 2.4 collective-permute-start.11
  90.5 3.5 %collective-permute-start.8 = (bf16[1024,256]{1,0:T(8,128)(2,1)S(1)}, bf16[1024,256]{1,0:T(8,128)(2,1)S(1)}, u32[]{:S(2)}, u32[]{:S(2)}) collective-permute-start(bf16[1024,256]{1,0:T(8,128)(2,1)S(1)} %get-tuple-element.85), channel_id=1, source_target_pairs={{0,1},{1,0},{2,3},{3,2},{4,5},{5,4},{6,7},{7,6},{8,9},{9,8},{10,11... | collective-permute-start | bytes 1572872 | tf_op jit(solution)/shard_map/ppermute | solution.py:726
  94.0 28.1 %collective-permute-start.13 = (bf16[4,144,512]{2,1,0:T(8,128)(2,1)}, bf16[4,144,512]{2,1,0:T(8,128)(2,1)}, u32[]{:S(2)}, u32[]{:S(2)}) collective-permute-start(bf16[4,144,512]{2,1,0:T(8,128)(2,1)} %get-tuple-element.99), channel_id=1, source_target_pairs={{0,2},{2,0},{4,6},{6,4},{8,10},{10,8},{12,14},{14,12},{16,18},{18,... | collective-permute-start | bytes 1769480 | tf_op jit(solution)/shard_map/ppermute | solution.py:632
  96.6 28.3 %collective-permute-start.14 = (bf16[4,144,512]{2,1,0:T(8,128)(2,1)}, bf16[4,144,512]{2,1,0:T(8,128)(2,1)}, u32[]{:S(2)}, u32[]{:S(2)}) collective-permute-start(bf16[4,144,512]{2,1,0:T(8,128)(2,1)} %get-tuple-element.100), channel_id=1, source_target_pairs={{0,4},{2,6},{4,0},{6,2},{8,12},{10,14},{12,8},{14,10},{16,20},{18,... | collective-permute-start | bytes 1769480 | tf_op jit(solution)/shard_map/ppermute | solution.py:632
  98.1 26.7 %collective-permute-start.15 = (bf16[4,144,512]{2,1,0:T(8,128)(2,1)}, bf16[4,144,512]{2,1,0:T(8,128)(2,1)}, u32[]{:S(2)}, u32[]{:S(2)}) collective-permute-start(bf16[4,144,512]{2,1,0:T(8,128)(2,1)} %get-tuple-element.101), channel_id=1, source_target_pairs={{0,6},{2,4},{4,2},{6,0},{8,14},{10,12},{12,10},{14,8},{16,22},{18,... | collective-permute-start | bytes 1769480 | tf_op jit(solution)/shard_map/ppermute | solution.py:632
  113.6 13.1 %collective-permute-start.12 = (bf16[1024,256]{1,0:T(8,128)(2,1)}, bf16[1024,256]{1,0:T(8,128)(2,1)}, u32[]{:S(2)}, u32[]{:S(2)}) collective-permute-start(bf16[1024,256]{1,0:T(8,128)(2,1)} %get-tuple-element.97), channel_id=1, source_target_pairs={{0,1},{1,0},{2,3},{3,2},{4,5},{5,4},{6,7},{7,6},{8,9},{9,8},{10,11... | collective-permute-start | bytes 1572872 | tf_op jit(solution)/shard_map/ppermute | solution.py:726
  116.3 3.5 %collective-permute-start.24 = (bf16[512,512]{1,0:T(8,128)(2,1)}, bf16[512,512]{1,0:T(8,128)(2,1)}, u32[]{:S(2)}, u32[]{:S(2)}) collective-permute-start(bf16[512,512]{1,0:T(8,128)(2,1)} %get-tuple-element.127), channel_id=1, source_target_pairs={{0,1},{1,0},{2,3},{3,2},{4,5},{5,4},{6,7},{7,6},{8,9},{9,8},{10,11... | collective-permute-start | bytes 1572872 | tf_op jit(solution)/shard_map/ppermute | solution.py:726
  126.7 20.9 %collective-permute-start.17 = (bf16[144,512]{1,0:T(8,128)(2,1)S(1)}, bf16[144,512]{1,0:T(8,128)(2,1)S(1)}, u32[]{:S(2)}, u32[]{:S(2)}) collective-permute-start(bf16[144,512]{1,0:T(8,128)(2,1)S(1)} %get-tuple-element.110), channel_id=1, source_target_pairs={{0,8},{2,10},{4,12},{6,14},{8,0},{10,2},{12,4},{14,6},{16,24},{18,... | collective-permute-start | bytes 442376 | tf_op jit(solution)/shard_map/ppermute | solution.py:632
  128.4 20.0 %collective-permute-start.18 = (bf16[144,512]{1,0:T(8,128)(2,1)S(1)}, bf16[144,512]{1,0:T(8,128)(2,1)S(1)}, u32[]{:S(2)}, u32[]{:S(2)}) collective-permute-start(bf16[144,512]{1,0:T(8,128)(2,1)S(1)} %get-tuple-element.111), channel_id=1, source_target_pairs={{0,16},{2,18},{4,20},{6,22},{8,24},{10,26},{12,28},{14,30},{16,0},... | collective-permute-start | bytes 442376 | tf_op jit(solution)/shard_map/ppermute | solution.py:632
  137.3 11.0 %collective-permute-start.19 = (bf16[144,512]{1,0:T(8,128)(2,1)S(1)}, bf16[144,512]{1,0:T(8,128)(2,1)S(1)}, u32[]{:S(2)}, u32[]{:S(2)}) collective-permute-start(bf16[144,512]{1,0:T(8,128)(2,1)S(1)} %get-tuple-element.112), channel_id=1, source_target_pairs={{0,24},{2,26},{4,28},{6,30},{8,16},{10,18},{12,20},{14,22},{16,8},... | collective-permute-start | bytes 442376 | tf_op jit(solution)/shard_map/ppermute | solution.py:632
  145.1 6.3 %collective-permute-start.16 = (bf16[1024,256]{1,0:T(8,128)(2,1)S(1)}, bf16[1024,256]{1,0:T(8,128)(2,1)S(1)}, u32[]{:S(2)}, u32[]{:S(2)}) collective-permute-start(bf16[1024,256]{1,0:T(8,128)(2,1)S(1)} %get-tuple-element.108), channel_id=1, source_target_pairs={{0,1},{1,0},{2,3},{3,2},{4,5},{5,4},{6,7},{7,6},{8,9},{9,8},{10,11... | collective-permute-start | bytes 1572872 | tf_op jit(solution)/shard_map/ppermute | solution.py:726
  145.2 2.3 collective-permute-start.27
  147.5 1.6 collective-permute-start.26
  147.6 2.7 collective-permute-start.25
  151.4 31.6 %collective-permute-start.20 = (bf16[144,512]{1,0:T(8,128)(2,1)S(1)}, bf16[144,512]{1,0:T(8,128)(2,1)S(1)}, u32[]{:S(2)}, u32[]{:S(2)}) collective-permute-start(bf16[144,512]{1,0:T(8,128)(2,1)S(1)} %add_convert_fusion.3), channel_id=1, source_target_pairs={{0,8},{2,10},{4,12},{6,14},{8,0},{10,2},{12,4},{14,6},{16,24},{18,... | collective-permute-start | bytes 442376 | tf_op jit(solution)/shard_map/ppermute | solution.py:643
  153.6 29.5 %collective-permute-start.21 = (bf16[144,512]{1,0:T(8,128)(2,1)S(1)}, bf16[144,512]{1,0:T(8,128)(2,1)S(1)}, u32[]{:S(2)}, u32[]{:S(2)}) collective-permute-start(bf16[144,512]{1,0:T(8,128)(2,1)S(1)} %add_convert_fusion.3), channel_id=1, source_target_pairs={{0,16},{2,18},{4,20},{6,22},{8,24},{10,26},{12,28},{14,30},{16,0},... | collective-permute-start | bytes 442376 | tf_op jit(solution)/shard_map/ppermute | solution.py:643
  155.8 27.3 %collective-permute-start.22 = (bf16[144,512]{1,0:T(8,128)(2,1)S(1)}, bf16[144,512]{1,0:T(8,128)(2,1)S(1)}, u32[]{:S(2)}, u32[]{:S(2)}) collective-permute-start(bf16[144,512]{1,0:T(8,128)(2,1)S(1)} %add_convert_fusion.3), channel_id=1, source_target_pairs={{0,24},{2,26},{4,28},{6,30},{8,16},{10,18},{12,20},{14,22},{16,8},... | collective-permute-start | bytes 442376 | tf_op jit(solution)/shard_map/ppermute | solution.py:643
  192.4 76.1 %collective-permute-start.23 = (bf16[1024,512]{1,0:T(8,128)(2,1)}, bf16[1024,512]{1,0:T(8,128)(2,1)}, u32[]{:S(2)}, u32[]{:S(2)}) collective-permute-start(bf16[1024,512]{1,0:T(8,128)(2,1)} %get-tuple-element.122), channel_id=1, source_target_pairs={{0,1},{1,0},{2,3},{3,2},{4,5},{5,4},{6,7},{7,6},{8,9},{9,8},{10,11... | collective-permute-start | bytes 3145736 | tf_op jit(solution)/shard_map/ppermute | solution.py:726
  193.1 71.5 %collective-permute-start.28 = (bf16[4,144,512]{2,1,0:T(8,128)(2,1)S(1)}, bf16[4,144,512]{2,1,0:T(8,128)(2,1)S(1)}, u32[]{:S(2)}, u32[]{:S(2)}) collective-permute-start(bf16[4,144,512]{2,1,0:T(8,128)(2,1)S(1)} %pad_maximum_fusion.2.refs_0_), channel_id=1, source_target_pairs={{0,2},{2,0},{4,6},{6,4},{8,10},{10,8},{12,14},{14,12},{16,18},{18,... | collective-permute-start | bytes 1769480 | tf_op jit(solution)/shard_map/ppermute | solution.py:643
  193.2 71.4 %collective-permute-start.29 = (bf16[4,144,512]{2,1,0:T(8,128)(2,1)S(1)}, bf16[4,144,512]{2,1,0:T(8,128)(2,1)}, u32[]{:S(2)}, u32[]{:S(2)}) collective-permute-start(bf16[4,144,512]{2,1,0:T(8,128)(2,1)S(1)} %pad_maximum_fusion.2.refs_0_), channel_id=1, source_target_pairs={{0,4},{2,6},{4,0},{6,2},{8,12},{10,14},{12,8},{14,10},{16,20},{18,... | collective-permute-start | bytes 1769480 | tf_op jit(solution)/shard_map/ppermute | solution.py:643
  193.3 71.4 %collective-permute-start.30 = (bf16[4,144,512]{2,1,0:T(8,128)(2,1)S(1)}, bf16[4,144,512]{2,1,0:T(8,128)(2,1)}, u32[]{:S(2)}, u32[]{:S(2)}) collective-permute-start(bf16[4,144,512]{2,1,0:T(8,128)(2,1)S(1)} %pad_maximum_fusion.2.refs_0_), channel_id=1, source_target_pairs={{0,6},{2,4},{4,2},{6,0},{8,14},{10,12},{12,10},{14,8},{16,22},{18,... | collective-permute-start | bytes 1769480 | tf_op jit(solution)/shard_map/ppermute | solution.py:643
  (44 other events, 321.6 us)

commit v4 on v3

--- a/solution.py
+++ b/solution.py
@@ -17,15 +17,14 @@
 NT = (((1,), (1,)), ((), ()))
 NN = (((1,), (0,)), ((), ()))
 TN = (((0,), (0,)), ((), ()))
-VMEM_BYTES = 50 << 20
 
 
 def mm(a, b, dims=NN):
     return lax.dot_general(a, b, dims, preferred_element_type=F32)
 
 
-def params(semantics=("arbitrary",)):
-    return pltpu.CompilerParams(dimension_semantics=semantics, vmem_limit_bytes=VMEM_BYTES)
+def params(mib):
+    return pltpu.CompilerParams(dimension_semantics=("arbitrary",), vmem_limit_bytes=mib << 20)
 
 
 def cost(flops, nbytes, exps=0):
@@ -43,9 +42,19 @@
     return lambda i, sc: (jnp.clip(i - r * per_part, 0, per_part - 1), 0)
 
 
+def group_of(heads):
+    return min(heads, 128 // DH)
+
+
 def per_head(block, heads):
-    head = lax.broadcasted_iota(jnp.int32, block.shape, 1) // DH
-    return jnp.concatenate([jnp.where(head == h, block, jnp.zeros_like(block)) for h in range(heads)], axis=0)
+    many = group_of(heads)
+    wide = many * DH
+    head = lax.broadcasted_iota(jnp.int32, (block.shape[0], wide), 1) // DH
+    parts = []
+    for h in range(heads):
+        cols = block[:, h // many * wide : (h // many + 1) * wide]
+        parts.append(jnp.where(head == h % many, cols, jnp.zeros_like(cols)))
+    return jnp.concatenate(parts, axis=0)
 
 
 def attend_kernel(nblk, per_part, n_q, n_out, heads, bq, bk, sc, *refs):
@@ -60,6 +69,8 @@
     place = lax.broadcasted_iota(jnp.int32, (bk, bq), 0)
     span = [slice(h * bq, (h + 1) * bq) for h in range(heads)]
     cols = [slice(h * DH, (h + 1) * DH) for h in range(heads)]
+    many = group_of(heads)
+    wide = [slice(h // many * many * DH, (h // many + 1) * many * DH) for h in range(heads)]
 
     first, end = sc[i], sc[nblk + i]
 
@@ -67,7 +78,7 @@
         return pl.ds(pl.multiple_of(kb * bk, bk), bk)
 
     def scores(kb, h):
-        s_ref[:, span[h]] = mm(k_ref[rows(kb), :], q_heads[span[h], :], NT)
+        s_ref[:, span[h]] = mm(k_ref[rows(kb), wide[h]], q_heads[span[h], :], NT)
 
     def soften(kb, h, keep, top, total):
         t = jnp.where(keep, s_ref[:, span[h]] * SCALE2, NEG)
@@ -132,14 +143,14 @@
             + [pl.BlockSpec((1, heads, bq), lambda i, sc: (i, 0, 0))],
             scratch_shapes=[
                 pltpu.VMEM((width, bq), F32),
-                pltpu.VMEM((heads * bq, width), BF16),
+                pltpu.VMEM((heads * bq, group_of(heads) * DH), BF16),
                 pltpu.VMEM((bk, heads * bq), F32),
                 pltpu.VMEM((bk, heads * bq), BF16),
             ],
         ),
         out_shape=[jax.ShapeDtypeStruct((tokens // mp, width), BF16)] * mp
         + [jax.ShapeDtypeStruct((nblk, heads, bq), F32)],
-        compiler_params=params(),
+        compiler_params=params(14),
         cost_estimate=cost(4 * tokens * 512 * width, 8 * tokens * width, tokens * 512 * heads),
     )(sc, *q_parts, keys, values_t, lo, hi)
     return outs[:mp], outs[mp]
@@ -166,6 +177,8 @@
     hi = hi_ref[...]
     span = [slice(h * bq, (h + 1) * bq) for h in range(heads)]
     cols = [slice(h * DH, (h + 1) * DH) for h in range(heads)]
+    many = group_of(heads)
+    wide = [slice(h // many * many * DH, (h // many + 1) * many * DH) for h in range(heads)]
     prod = (do.astype(F32) * pick(i, per_part, o_refs).astype(F32)).T
     delta = [jnp.sum(prod[cols[h], :], axis=0, keepdims=True) for h in range(heads)]
     lse = [lse_ref[0, h : h + 1, :] for h in range(heads)]
@@ -177,13 +190,17 @@
         rows = pl.ds(start, bk)
         kt = kt_ref[:, rows]
         keep = jnp.logical_and(place >= lo - start, place < hi - start)
-        s = mm(k_ref[rows, :], q_heads[...], NT) * SCALE2
-        dp = mm(v_ref[rows, :], do_heads[...], NT)
-        p = [jnp.where(keep, jnp.exp2(s[:, span[h]] - lse[h]), 0.0) for h in range(heads)]
-        ds = [(p[h] * (dp[:, span[h]] - delta[h])).astype(BF16) for h in range(heads)]
+        groups = [(slice(h * bq, (h + many) * bq), wide[h]) for h in range(0, heads, many)]
+        s = [mm(k_ref[rows, w], q_heads[g, :], NT) * SCALE2 for g, w in groups]
+        dp = [mm(v_ref[rows, w], do_heads[g, :], NT) for g, w in groups]
+        at = [(h // many, slice(h % many * bq, (h % many + 1) * bq)) for h in range(heads)]
+        p = [jnp.where(keep, jnp.exp2(s[g][:, c] - lse[h]), 0.0) for h, (g, c) in enumerate(at)]
+        ds = [(p[h] * (dp[g][:, c] - delta[h])).astype(BF16) for h, (g, c) in enumerate(at)]
         p = [p[h].astype(BF16) for h in range(heads)]
-        dv_acc[rows, :] += mm(jnp.concatenate(p, axis=1), do_heads[...])
-        dk_acc[rows, :] += mm(jnp.concatenate(ds, axis=1), q_heads[...])
+        for g, (r, w) in enumerate(groups):
+            here = slice(g * many, (g + 1) * many)
+            dv_acc[rows, w] += mm(jnp.concatenate(p[here], axis=1), do_heads[r, :])
+            dk_acc[rows, w] += mm(jnp.concatenate(ds[here], axis=1), q_heads[r, :])
         for h in range(heads):
             dq_acc[cols[h], :] += mm(kt[cols[h], :], ds[h])
         return carry
@@ -231,13 +248,13 @@
                 pltpu.VMEM(keys.shape, F32),
                 pltpu.VMEM(keys.shape, F32),
                 pltpu.VMEM((width, bq), F32),
-                pltpu.VMEM((heads * bq, width), BF16),
-                pltpu.VMEM((heads * bq, width), BF16),
+                pltpu.VMEM((heads * bq, group_of(heads) * DH), BF16),
+                pltpu.VMEM((heads * bq, group_of(heads) * DH), BF16),
             ],
         ),
         out_shape=[jax.ShapeDtypeStruct(q.shape, BF16) for q in q_parts]
         + [jax.ShapeDtypeStruct(keys.shape, BF16)] * 2,
-        compiler_params=params(),
+        compiler_params=params(26),
         cost_estimate=cost(10 * tokens * 512 * width, 12 * tokens * width, tokens * 512 * heads),
     )(sc, *q_parts, *do_parts, *o_parts, keys, keys_t, values, lo, hi, lse)
     return outs[: len(q_parts)], outs[-2], outs[-1]
@@ -254,6 +271,31 @@
     mean_t = jnp.mean(t, axis=-1, keepdims=True)
     mean_tx = jnp.mean(t * xhat, axis=-1, keepdims=True)
     return rstd * (t - mean_t - xhat * mean_tx)
+
+
+def project_kernel(n, turned, x_ref, w_ref, *outs):
+    x = x_ref[...]
+    for c in range(n):
+        y = mm(x, w_ref[c])
+        outs[c][...] = y.astype(BF16)
+        if c in turned:
+            outs[n + turned.index(c)][...] = y.T.astype(BF16)
+
+
+def project(x, w, turned, bt):
+    n, d, width = w.shape
+    tokens = x.shape[0]
+    return pl.pallas_call(
+        functools.partial(project_kernel, n, turned),
+        grid=(tokens // bt,),
+        in_specs=[pl.BlockSpec((bt, d), lambda i: (i, 0)), pl.BlockSpec(w.shape, lambda i: (0, 0, 0))],
+        out_specs=[pl.BlockSpec((bt, width), lambda i: (i, 0))] * n
+        + [pl.BlockSpec((width, bt), lambda i: (0, i))] * len(turned),
+        out_shape=[jax.ShapeDtypeStruct((tokens, width), BF16)] * n
+        + [jax.ShapeDtypeStruct((width, tokens), BF16)] * len(turned),
+        compiler_params=params(14),
+        cost_estimate=cost(2 * tokens * d * width * n, tokens * (d + 2 * n * width) * 2),
+    )(x, w)
 
 
 def post_self_kernel(mp, sc, *refs):
@@ -302,7 +344,7 @@
             jax.ShapeDtypeStruct((share, 1), F32),
         ]
         + [jax.ShapeDtypeStruct((share, width), BF16)] * mp,
-        compiler_params=params(),
+        compiler_params=params(16),
         cost_estimate=cost(4 * share * d * d, share * d * 12),
     )(sc, x, *ctx, *wo, *cq, gain, shift)
     return outs[0], outs[1], outs[2], outs[3:]
@@ -335,7 +377,7 @@
     a3 = n2.astype(F32)
     for r in range(mp):
         u = mm(n2, up[r][...], NT)
-        sg = 1.0 / (1.0 + jnp.exp(-u))
+        sg = 0.5 * jnp.tanh(0.5 * u) + 0.5
         h = u * sg
         hid[r][...] = h.astype(BF16)
         slope_ref[:, r * ff : (r + 1) * ff] = sg + h * (1.0 - sg)
@@ -397,7 +439,7 @@
         + [shape(width, BF16)] * mp
         + [shape(ff, BF16)] * (2 * mp)
         + [jax.ShapeDtypeStruct((4, d), F32)],
-        compiler_params=params(),
+        compiler_params=params(44),
         cost_estimate=cost(8 * share * d * ff * mp + 4 * share * d * d, share * ff * mp * 4, share * ff * mp),
     )(*cctx, n1, cot, *co, *up, *down, gain, shift)
     out, da2, n2, e3, e2 = outs[:5]
@@ -450,7 +492,7 @@
         out_shape=[jax.ShapeDtypeStruct((share, d), F32), jax.ShapeDtypeStruct((share, d), BF16)]
         + [jax.ShapeDtypeStruct((share, width), BF16)] * mp
         + [jax.ShapeDtypeStruct((2, d), F32)],
-        compiler_params=params(),
+        compiler_params=params(16),
         cost_estimate=cost(4 * share * d * d, share * d * 14),
     )(*dqc, *cq, *wo, da2, xhat, rstd, gain)
     return outs[0], outs[1], outs[2 : 2 + mp], outs[-1]
@@ -459,9 +501,7 @@
 def part_kernel(n_in, n_out, per_part, sc, *refs):
     grads, w_ref, outs = refs[:n_in], refs[n_in], refs[n_in + 1 :]
     i = pl.program_id(0)
-    total = mm(grads[0][...], w_ref[0], NT)
-    for c in range(1, n_in):
-        total += mm(grads[c][...], w_ref[c], NT)
+    total = mm(jnp.concatenate([g[...] for g in grads], axis=1), w_ref[...])
     for r in range(n_out):
 
         @pl.when(jnp.logical_and(i >= r * per_part, i < (r + 1) * per_part))
@@ -472,6 +512,7 @@
 def input_part(sc, grads, w, mp, bt):
     tokens, width = grads[0].shape
     d = w.shape[1]
+    w = w.swapaxes(1, 2).reshape(-1, d)
     nblk = tokens // bt
     per_part = nblk // mp
     outs = pl.pallas_call(
@@ -484,7 +525,7 @@
         ),
         out_shape=[jax.ShapeDtypeStruct((tokens // mp, d), F32)]
         + [jax.ShapeDtypeStruct((tokens // mp, d), BF16)] * (mp - 1),
-        compiler_params=params(),
+        compiler_params=params(16),
         cost_estimate=cost(2 * tokens * d * width * len(grads), tokens * d * 6),
     )(sc, *grads, w)
     return outs
@@ -590,7 +631,7 @@
         count = a.shape[0] // parts
         if a.shape[0] % parts == 0 and count % (16 * devices) == 0:
             for p in range(parts):
-                order = far if parts == 3 else (x_y, y_x)[len(plan) % 2]
+                order = (x_y, y_x, far)[len(plan) % 3]
                 plan.append((len(used), p * count, count, order))
             used.append(a)
         else:
@@ -609,7 +650,7 @@
         + [pltpu.VMEM((16 * nbits, small.shape[1]), BF16)]
         + [pltpu.SemaphoreType.DMA((len(plan) + 1, 2 * nbits))] * 2,
         compiler_params=pltpu.CompilerParams(
-            collective_id=7, has_side_effects=True, vmem_limit_bytes=VMEM_BYTES
+            collective_id=7, has_side_effects=True, vmem_limit_bytes=20 << 20
         ),
     )(*operands)
     outs = [
@@ -682,7 +723,7 @@
             out_specs=[pl.BlockSpec((s[0] // n, d), lambda i, sc: (i, 0)) for s in shapes],
         ),
         out_shape=[jax.ShapeDtypeStruct(s, F32) for s in shapes],
-        compiler_params=params(),
+        compiler_params=params(14),
         cost_estimate=cost(0, sum(s[0] * d * 6 for s in shapes)),
     )(place.reshape(1).astype(jnp.int32), *pieces)
 
@@ -753,10 +794,8 @@
     as_row = lambda v: v.reshape(1, tokens).astype(jnp.int32)
     self_lo, self_hi, cross_lo, cross_hi = map(as_row, (self_lo, self_hi, cross_lo, cross_hi))
 
-    proj = [mm(block_input_slots, self_qkv[c]).astype(BF16) for c in range(3)]
-    pair = [mm(memory, cross_kv[c]).astype(BF16) for c in range(2)]
-    self_kt, self_vt = proj[1].T, proj[2].T
-    cross_kt, cross_vt = pair[0].T, pair[1].T
+    *proj, self_kt, self_vt = project(block_input_slots, self_qkv, (1, 2), min(512, mem_tokens))
+    *pair, cross_kt, cross_vt = project(memory, cross_kv, (0, 1), min(512, mem_tokens))
     ctx_parts, self_lse = attend(
         self_table, proj[:1], proj[1], self_vt, self_lo, self_hi, mp, bq, bk
     )
@@ -769,7 +808,7 @@
     )
     cctx = exchange(cctx_parts)
     layer_output, da2, n2, e3, e2, dcctx, hid, dpre, small23 = middle(
-        cctx, n1, cotangent, co, up, down, gain, shift, bt
+        cctx, n1, cotangent, co, up, down, gain, shift, min(512, share)
     )
     dcctx_parts = exchange(dcctx)
 
@@ -789,37 +828,47 @@
         collect(grads(cctx, [e2] * mp)).astype(BF16),
     ]
     row = lax.axis_index("batch")
-    near, far = 2, devices.bit_length() - 3
-    blocks = jnp.concatenate([g.reshape(devices, -1, d) for g in early], axis=1)
-    blocks = blocks.reshape(1 << near, 1 << far, -1, d)
-    dcctx_parts, blocks = lax.optimization_barrier((dcctx_parts, cut(blocks, 0, near, row)))
-    blocks = scatter_step(blocks, 0, devices)
+    far = devices.bit_length() - 3
+    one = early[0].reshape(2, 2, 1 << far, -1, d)
+    two = jnp.concatenate([g.reshape(devices, -1, d) for g in early[1:]], axis=1)
+    two = two.reshape(2, 2, 1 << far, -1, d)
+    dcctx_parts, one, two = lax.optimization_barrier((dcctx_parts, cut(one, 0, 1, row), cut(two, 1, 1, row)))
+    one, two = scatter_step(one, 0, devices), scatter_step(two, 1, devices)
     dqc_parts, dkc, dvc = attend_back(
         cross_table, qc_parts, dcctx_parts, cctx_parts, pair[0], cross_kt, pair[1], cross_lo, cross_hi, cross_lse, mp, bq, bk
     )
     dqc = exchange(dqc_parts)
-    dqc, blocks = lax.optimization_barrier((dqc, cut(add_up(blocks), near, far, row)))
-    blocks = scatter_step(blocks, near, devices)
-    da1, e1, dctx, small1 = pre_self(dqc, cq, wo, da2, xhat1, rstd1, gain, bt)
-    dctx_parts = exchange(dctx)
-    mem_bt = min(256, mem_share)
+    dkc, one, two = lax.optimization_barrier((dkc, cut(add_up(one), 1, 1, row), cut(add_up(two), 0, 1, row)))
+    one, two = scatter_step(one, 1, devices), scatter_step(two, 0, devices)
+    mem_bt = min(512, mem_share)
     mem_nb = mem_share // mem_bt
     mem_blocks = ((((me - jnp.arange(mp)) % mp) * mem_nb)[:, None] + jnp.arange(mem_nb)[None, :]).reshape(-1)
     memory_parts = input_part(mem_blocks.astype(jnp.int32), [dkc, dvc], cross_kv, mp, mem_bt)
     memory_grad = collect(memory_parts)
-    cross_kv_grad = jnp.stack([mm(memory, g, TN) for g in (dkc, dvc)])
+    cross_kv_grad = [mm(memory, g, TN).astype(BF16) for g in (dkc, dvc)]
+    blocks = jnp.concatenate([add_up(one), add_up(two)], axis=1)
+    dqc, cross_kv_grad, memory_grad, blocks = lax.optimization_barrier(
+        (dqc, cross_kv_grad, memory_grad, cut(blocks, 2, far, row))
+    )
+    blocks = scatter_step(blocks, 2, devices)
+    da1, e1, dctx, small1 = pre_self(dqc, cq, wo, da2, xhat1, rstd1, gain, bt)
+    dctx_parts = exchange(dctx)
     cross_query_grad = collect(grads([n1] * mp, dqc))
     self_out_grad = collect(grads(ctx, [e1] * mp))
     dctx_parts, block = lax.optimization_barrier((dctx_parts, add_up(blocks)))
-    blocks = gather_step(block, near, far, devices)
+    blocks = gather_step(block, 2, far, devices)
     (dq,), dk, dv = attend_back(
         self_table, proj[:1], dctx_parts, ctx_parts, proj[1], self_kt, proj[2], self_lo, self_hi, self_lse, mp, bq, bk
     )
-    dq, block = lax.optimization_barrier((dq, in_order(blocks, row >> near)))
-    spread_out = gather_step(block, 0, near, devices)
-    input_parts = input_part(q_block.astype(jnp.int32), [dq, dk, dv], self_qkv, mp, bq)
+    blocks = in_order(blocks, row >> 2)
+    cut_at = one[0].shape[1]
+    dq, one, two = lax.optimization_barrier((dq, blocks[:, :cut_at], blocks[:, cut_at:]))
+    one, two = gather_step(one, 1, 1, devices), gather_step(two, 0, 1, devices)
+    in_bt = min(512, share)
+    in_blocks = place.reshape(-1, in_bt)[:, 0] // in_bt
+    input_parts = input_part(in_blocks.astype(jnp.int32), [dq, dk, dv], self_qkv, mp, in_bt)
     input_grad = collect(input_parts) + da1
-    self_qkv_grad = jnp.stack([mm(block_input_slots, g, TN) for g in (dq, dk, dv)])
+    self_qkv_grad = [mm(block_input_slots, g, TN) for g in (dq, dk, dv)]
 
     small = jnp.concatenate([small1[:1], small23[:2], small1[1:], small23[2:]], axis=0)
     part = d // mp
@@ -827,24 +876,31 @@
         lax.dynamic_slice_in_dim(small, ((me - r) % mp) * part, part, 1).astype(BF16) for r in range(mp)
     ]
     small = collect(pieces)
+    self_qkv_grad, one, two = lax.optimization_barrier(
+        (self_qkv_grad, in_order(one, row // 2 % 2), in_order(two, row % 2))
+    )
+    one = gather_step(one.reshape(-1, *one.shape[2:]), 0, 1, devices)
+    two = gather_step(two.reshape(-1, *two.shape[2:]), 1, 1, devices)
     *summed, small = all_sum(
         [
             g.astype(BF16)
             for g in (
-                self_qkv_grad,
+                *self_qkv_grad,
                 self_out_grad,
                 cross_query_grad,
-                cross_kv_grad,
+                *cross_kv_grad,
             )
         ],
-        (3, 1, 1, 2),
+        (1, 1, 1, 1, 1, 1, 1),
         small.astype(BF16),
         devices,
     )
-    up_grad, down_grad, cross_out_grad = lay_out(
-        spread_out, row % (1 << near), [g.shape for g in early], [g.shape[0] // devices for g in early]
-    )
-    summed = [g.astype(F32) for g in summed] + [cross_out_grad, up_grad, down_grad]
+    rows = [g.shape[0] // devices for g in early]
+    (up_grad,) = lay_out(one, row % 2, [early[0].shape], rows[:1])
+    down_grad, cross_out_grad = lay_out(two, row // 2 % 2, [g.shape for g in early[1:]], rows[1:])
+    dwq, dwk, dwv, self_out_grad, cross_query_grad, dck, dcv = [g.astype(F32) for g in summed]
+    summed = [jnp.stack([dwq, dwk, dwv]), self_out_grad, cross_query_grad, jnp.stack([dck, dcv])]
+    summed += [cross_out_grad, up_grad, down_grad]
     small = small.astype(F32).T
     return (layer_output, input_grad, memory_grad, *summed, small[:, :3], small[:, 3:6])
 

time: 274 us -> 247 us (0.901)
  Pallas kernels: 172 us -> 150 us
  matrix products: 27 us -> 14.5 us
  waiting for transfers between devices: 8.02 us -> 14 us
  local copies, waits for them, and re-layouts: 19.5 us -> 24.6 us
  other arithmetic: 15.3 us -> 12.2 us
    dot_general x20 -> x15, matrix products: 27 us -> 14.5 us  [mm(): return lax.dot_general(a, b, dims, preferred_element_type=F32)]
    unnamed x92 -> x100, local copies, waits for them, and re-layouts: 7.53 us -> 18.2 us
    ppermute x6 -> x7, waiting for transfers between devices: 3 us -> 10.1 us  [scatter_step(): lax.ppermute(b, 'batch', across(r, shift, devices))]
    pallas_call x1, Pallas kernels: 58.3 us -> 51.4 us  [all_sum(): pl.pallas_call(functools.partial(all_sum_kernel, plan, nbits, len(keep)),...]
    convert_element_type x4 -> x0, local copies, waits for them, and re-layouts: 6.61 us -> none  [the longest x2 4.13 us: shards(): proj = [mm(block_input_slots, self_qkv[c]).astype(BF16) for c in range(3)]]
    pallas_call x2, Pallas kernels: 10.6 us -> 4.58 us  [input_part(): pl.pallas_call(functools.partial(part_kernel, len(grads), mp, per_part),...]
    pallas_call x2, Pallas kernels: 40.4 us -> 35 us  [attend_back(): pl.pallas_call(functools.partial(attend_back_kernel, nblk, per_part, len(...]
    transpose x0 -> x2, local copies, waits for them, and re-layouts: none -> 4.41 us  [input_part(): w = w.swapaxes(1, 2).reshape(-1, d)]
  transfers between devices with their start and end apart: 31 -> 33, of which waited for: 7 -> 9; matrix products, arithmetic and copies ran while one was open for 13% -> 10% of each run, Pallas kernels for 47% -> 45%
where the time goes in v4:
time: 247 us; the launch traced here: 244 us
  Pallas kernels  150 us (61%)
  starting transfers between devices  27.2 us (11%)
  local copies, waits for them, and re-layouts  24.6 us (10%)
  matrix products  14.5 us (6%)
  waiting for transfers between devices  14 us (6%)
  other arithmetic  12.2 us (5%)
    pallas_call x1, Pallas kernels, all_sum(): pl.pallas_call(functools.partial(all_sum_kernel, plan, nbits, len(keep)),...  51.4 us
    pallas_call x2, Pallas kernels, attend_back(): pl.pallas_call(functools.partial(attend_back_kernel, nblk, per_part, len(...  35 us
    pallas_call x2, Pallas kernels, attend(): pl.pallas_call(functools.partial(attend_kernel, nblk, per_part, len(q_par...  26.6 us
    pallas_call x1, Pallas kernels, middle(): pl.pallas_call(functools.partial(middle_kernel, mp), grid=(share // bt,),...  18.4 us
    unnamed x100, local copies, waits for them, and re-layouts  18.2 us
    dot_general x15, matrix products, mm(): return lax.dot_general(a, b, dims, preferred_element_type=F32)  14.5 us
    ppermute x7, starting transfers between devices, scatter_step(): lax.ppermute(b, 'batch', across(r, shift, devices))  12.5 us
    ppermute x7, waiting for transfers between devices, scatter_step(): lax.ppermute(b, 'batch', across(r, shift, devices))  10.1 us
  transfers between devices with their start and end apart: 33, of which 9 were waited for; matrix products, arithmetic and copies ran while one was open for 10% of the time, Pallas kernels for 45%

profile of v4, /device:TPU:0, one launch (start us, length us, event | category | flops | bytes accessed | tf_op | source)
XLA Modules:
  0.0 244.3 jit_solution(3888067418045718538)
XLA Ops:
  4.8 1.6 copy-done
  7.5 2.9 %shard_map.229 = (bf16[2048,256]{1,0:T(8,128)(2,1)S(1)}, bf16[2048,256]{1,0:T(8,128)(2,1)S(1)}, bf16[2048,256]{1,0:T(8,128)(2,1)S(1)}, bf16[256,2048]{1,0:T(8,128)(2,1)S(1)}, bf16[256,2048]{1,0:T(8,128)(2,1)S(1)}) custom-call(bf16[2048,512]{1,0:T(8,128)(2,1)S(1)} %copy-done, bf16[3,512,256]{2,1,0:T(8,128)(2,1)S(1)} %copy-done.7), custom_call_target="tpu_custom_call" | custom-call | flops 1610612736 | bytes 8388608 | tf_op jit(solution)/shard_map/pallas_call | solution.py:288
  11.5 15.2 %shard_map.230 = (bf16[1024,256]{1,0:T(8,128)(2,1)S(1)}, bf16[1024,256]{1,0:T(8,128)(2,1)S(1)}, f32[8,4,256]{2,1,0:T(4,128)S(1)}) custom-call(s32[24]{0:T(128)S(1)} %get-tuple-element.223.sc, bf16[2048,256]{1,0:T(8,128)(2,1)S(1)} %get-tuple-element.101.refs_0_, bf16[2048,256]{1,0:T(8,128)(2,1)S(1)} %get-tuple-element.102.refs_1_.refs_5_, ...), custom_call_target="tpu_custom_call" | custom-call | flops 1073741824 | bytes 4194304 | tf_op jit(solution)/shard_map/pallas_call | solution.py:136
  30.1 3.6 %shard_map.231 = (bf16[1024,512]{1,0:T(8,128)(2,1)S(1)}, f32[1024,512]{1,0:T(8,128)S(1)}, f32[1024,1]{1,0:T(8,128)S(1)}, bf16[1024,256]{1,0:T(8,128)(2,1)S(1)}, bf16[1024,256]{1,0:T(8,128)(2,1)}) custom-call(s32[1]{0:T(128)} %bitcast.3.sc, bf16[2048,512]{1,0:T(8,128)(2,1)S(1)} %copy-done.1, bf16[1024,256]{1,0:T(8,128)(2,1)S(1)} %get-tuple-element.104.refs_1_.refs_3_, ...), custom_call_target="tpu_custom_call" | custom-call | flops 1073741824 | bytes 6291456 | tf_op jit(solution)/shard_map/pallas_call | solution.py:331
  33.7 1.3 copy-done.2
  45.1 11.3 %shard_map.233 = (bf16[1024,256]{1,0:T(8,128)(2,1)S(1)}, bf16[1024,256]{1,0:T(8,128)(2,1)}, f32[8,4,256]{2,1,0:T(4,128)S(1)}) custom-call(s32[24]{0:T(128)S(1)} %get-tuple-element.224.sc, bf16[1024,256]{1,0:T(8,128)(2,1)S(1)} %copy-done.27, bf16[1024,256]{1,0:T(8,128)(2,1)} %collective-permute-done.3.refs_1_, ...), custom_call_target="tpu_custom_call" | custom-call | flops 1073741824 | bytes 4194304 | tf_op jit(solution)/shard_map/pallas_call | solution.py:136
  57.7 2.1 copy.53
  59.8 2.4 copy.54
  65.7 18.4 %shard_map.234 = (bf16[1024,512]{1,0:T(8,128)(2,1)}, f32[1024,512]{1,0:T(8,128)}, bf16[1024,512]{1,0:T(8,128)(2,1)S(1)}, bf16[1024,512]{1,0:T(8,128)(2,1)S(1)}, ...) custom-call(bf16[1024,256]{1,0:T(8,128)(2,1)S(1)} %copy-done.31, ...), custom_call_target="tpu_custom_call" | custom-call | flops 9663676416 | bytes 8388608 | tf_op jit(solution)/shard_map/pallas_call | solution.py:429
  84.1 1.5 convolution_convert_fusion.10
  86.1 3.0 %convolution_convert_fusion.2 = bf16[1024,512]{1,0:T(8,128)(2,1)S(1)} fusion(bf16[1024,1024]{1,0:T(8,128)(2,1)} %get-tuple-element.118, bf16[1024,512]{1,0:T(8,128)(2,1)S(1)} %get-tuple-element.117), kind=kOutput, calls=%fused_computation.7 | convolution fusion | flops 1074266112 | bytes 4194304 | tf_op jit(solution)/shard_map/dot_general | solution.py:23
  89.3 1.3 convolution_convert_fusion
  95.4 2.9 %collective-permute-start.13 = (bf16[2,4,64,512]{3,2,1,0:T(8,128)(2,1)S(1)}, bf16[2,4,64,512]{3,2,1,0:T(8,128)(2,1)S(1)}, u32[]{:S(2)}, u32[]{:S(2)}) collective-permute-start(bf16[2,4,64,512]{3,2,1,0:T(8,128)(2,1)S(1)} %get-tuple-element.132), channel_id=1, source_target_pairs={{0,2},{2,0},{4,6},{6,4},{8,10},{10,8},{12,14},{14,12},{16,18},{18,... | collective-permute-start | bytes 1572872 | tf_op jit(solution)/shard_map/ppermute | solution.py:673
  98.4 1.5 collective-permute-start.14
  99.9 13.7 %shard_map.235 = (bf16[1024,256]{1,0:T(8,128)(2,1)S(1)}, bf16[1024,256]{1,0:T(8,128)(2,1)S(1)}, bf16[1024,256]{1,0:T(8,128)(2,1)S(1)}, bf16[1024,256]{1,0:T(8,128)(2,1)S(1)}) custom-call(s32[24]{0:T(128)S(1)} %get-tuple-element.224.sc, bf16[1024,256]{1,0:T(8,128)(2,1)S(1)} %copy-done.28, bf16[1024,256]{1,0:T(8,128)(2,1)} %collective-permute-done.3.refs_1_, ...), custom_call_target="tpu_custom_call" | custom-call | flops 2684354560 | bytes 6291456 | tf_op jit(solution)/shard_map/pallas_call | solution.py:236
  115.1 1.6 collective-permute-start.16
  117.7 1.5 shard_map.236
  119.4 4.2 %collective-permute-done.16 = bf16[4,64,512]{2,1,0:T(8,128)(2,1)S(1)} collective-permute-done((bf16[4,64,512]{2,1,0:T(8,128)(2,1)S(1)}, bf16[4,64,512]{2,1,0:T(8,128)(2,1)S(1)}, u32[]{:S(2)}, u32[]{:S(2)}) %collective-permute-start.16) | collective-permute-done | bytes 262176 | tf_op jit(solution)/shard_map/ppermute | solution.py:673
  123.6 1.5 collective-permute-done.17
  126.5 3.6 %collective-permute-start.19 = (bf16[144,512]{1,0:T(8,128)(2,1)S(1)}, bf16[144,512]{1,0:T(8,128)(2,1)S(1)}, u32[]{:S(2)}, u32[]{:S(2)}) collective-permute-start(bf16[144,512]{1,0:T(8,128)(2,1)S(1)} %get-tuple-element.151), channel_id=1, source_target_pairs={{0,8},{2,10},{4,12},{6,14},{8,0},{10,2},{12,4},{14,6},{16,24},{18,... | collective-permute-start | bytes 442376 | tf_op jit(solution)/shard_map/ppermute | solution.py:673
  130.6 1.8 collective-permute-start.21
  132.9 3.5 %shard_map.237 = (f32[1024,512]{1,0:T(8,128)S(1)}, bf16[1024,512]{1,0:T(8,128)(2,1)S(1)}, bf16[1024,256]{1,0:T(8,128)(2,1)S(1)}, bf16[1024,256]{1,0:T(8,128)(2,1)S(1)}, f32[2,512]{1,0:T(2,128)S(1)}) custom-call(bf16[1024,256]{1,0:T(8,128)(2,1)S(1)} %get-tuple-element.143.refs_0_, bf16[1024,256]{1,0:T(8,128)(2,1)S(1)} %collective-permute-done.12.refs_1_, ...), custom_call_target="tpu_custom_call" | custom-call | flops 1073741824 | bytes 7340032 | tf_op jit(solution)/shard_map/pallas_call | solution.py:485
  139.0 4.0 %collective-permute-done.20 = bf16[144,512]{1,0:T(8,128)(2,1)S(1)} collective-permute-done((bf16[144,512]{1,0:T(8,128)(2,1)S(1)}, bf16[144,512]{1,0:T(8,128)(2,1)S(1)}, u32[]{:S(2)}, u32[]{:S(2)}) %collective-permute-start.20) | collective-permute-done | bytes 147488 | tf_op jit(solution)/shard_map/ppermute | solution.py:673
  144.1 2.8 %collective-permute-start.22 = (bf16[144,512]{1,0:T(8,128)(2,1)S(1)}, bf16[144,512]{1,0:T(8,128)(2,1)S(1)}, u32[]{:S(2)}, u32[]{:S(2)}) collective-permute-start(bf16[144,512]{1,0:T(8,128)(2,1)S(1)} %add_convert_fusion.6), channel_id=1, source_target_pairs={{0,8},{2,10},{4,12},{6,14},{8,0},{10,2},{12,4},{14,6},{16,24},{18,... | collective-permute-start | bytes 442376 | tf_op jit(solution)/shard_map/ppermute | solution.py:684
  146.9 2.4 collective-permute-start.24
  149.3 21.3 %shard_map.238 = (bf16[2048,256]{1,0:T(8,128)(2,1)S(1)}, bf16[2048,256]{1,0:T(8,128)(2,1)S(1)}, bf16[2048,256]{1,0:T(8,128)(2,1)S(1)}) custom-call(s32[24]{0:T(128)S(1)} %get-tuple-element.223.sc, bf16[2048,256]{1,0:T(8,128)(2,1)S(1)} %copy-done.39, bf16[1024,256]{1,0:T(8,128)(2,1)S(1)} %get-tuple-element.154.refs_1_, ...), custom_call_target="tpu_custom_call" | custom-call | flops 2684354560 | bytes 6291456 | tf_op jit(solution)/shard_map/pallas_call | solution.py:236
  173.6 1.4 collective-permute-start.26
  175.0 3.0 %shard_map.239 = (f32[1024,512]{1,0:T(8,128)S(1)}, bf16[1024,512]{1,0:T(8,128)(2,1)S(1)}) custom-call(s32[4]{0:T(128)S(1)} %and_select_fusion.sc, bf16[2048,256]{1,0:T(8,128)(2,1)S(1)} %get-tuple-element.161.refs_0_, bf16[2048,256]{1,0:T(8,128)(2,1)S(1)} %get-tuple-element.162.refs_1_, bf16[2048,256]{1,0:T(8,128)(2,1)S(1)} %get-tuple-element.163.refs_2_, ...), custom_call_target="tpu_custom_call" | custom-call | flops 1610612736 | bytes 6291456 | tf_op jit(solution)/shard_map/pallas_call | solution.py:518
  183.3 51.4 %shard_map.240 = (bf16[512,256]{1,0:T(8,128)(2,1)S(1)}, bf16[512,256]{1,0:T(8,128)(2,1)S(1)}, bf16[512,256]{1,0:T(8,128)(2,1)S(1)}, bf16[256,512]{1,0:T(8,128)(2...) custom-call(bf16[512,256]{1,0:T(8,128)(2,1)S(1)} %convolution_bitcas, ...), custom_call_target="tpu_custom_call" | custom-call | tf_op jit(solution)/shard_map/pallas_call | solution.py:644
  239.3 1.4 shard_map.242
  240.7 1.6 shard_map.241
  242.3 2.0 add_add_fusion
  (232 shorter events, 50.9 us)
Async XLA Ops:
  26.8 3.2 %collective-permute-start = (bf16[1024,256]{1,0:T(8,128)(2,1)S(1)}, bf16[1024,256]{1,0:T(8,128)(2,1)S(1)}, u32[]{:S(2)}, u32[]{:S(2)}) collective-permute-start(bf16[1024,256]{1,0:T(8,128)(2,1)S(1)} %get-tuple-element.105.refs_4_), channel_id=1, source_target_pairs={{0,1},{1,0},{2,3},{3,2},{4,5},{5,4},{6,7},{7,6},{8,9},{9,8},{10,11... | collective-permute-start | bytes 1572872 | tf_op jit(solution)/shard_map/ppermute | solution.py:767
  28.2 1.8 collective-permute-start.2
  37.6 6.2 %collective-permute-start.3 = (bf16[1024,256]{1,0:T(8,128)(2,1)}, bf16[1024,256]{1,0:T(8,128)(2,1)}, u32[]{:S(2)}, u32[]{:S(2)}) collective-permute-start(bf16[1024,256]{1,0:T(8,128)(2,1)} %get-tuple-element.107), channel_id=1, source_target_pairs={{0,1},{1,0},{2,3},{3,2},{4,5},{5,4},{6,7},{7,6},{8,9},{9,8},{10,11... | collective-permute-start | bytes 1572872 | tf_op jit(solution)/shard_map/ppermute | solution.py:767
  37.7 24.4 %collective-permute-start.6 = (bf16[1024,512]{1,0:T(8,128)(2,1)}, bf16[1024,512]{1,0:T(8,128)(2,1)}, u32[]{:S(2)}, u32[]{:S(2)}) collective-permute-start(bf16[1024,512]{1,0:T(8,128)(2,1)} %refs_6_.1), channel_id=1, source_target_pairs={{0,1},{1,0},{2,3},{3,2},{4,5},{5,4},{6,7},{7,6},{8,9},{9,8},{10,11... | collective-permute-start | bytes 3145736 | tf_op jit(solution)/shard_map/ppermute | solution.py:761
  38.1 24.0 %collective-permute-start.7 = (bf16[1024,512]{1,0:T(8,128)(2,1)}, bf16[1024,512]{1,0:T(8,128)(2,1)}, u32[]{:S(2)}, u32[]{:S(2)}) collective-permute-start(bf16[1024,512]{1,0:T(8,128)(2,1)} %refs_8_.1), channel_id=1, source_target_pairs={{0,1},{1,0},{2,3},{3,2},{4,5},{5,4},{6,7},{7,6},{8,9},{9,8},{10,11... | collective-permute-start | bytes 3145736 | tf_op jit(solution)/shard_map/ppermute | solution.py:761
  38.3 23.9 %collective-permute-start.5 = (bf16[256,512]{1,0:T(8,128)(2,1)S(1)}, bf16[256,512]{1,0:T(8,128)(2,1)}, u32[]{:S(2)}, u32[]{:S(2)}) collective-permute-start(bf16[256,512]{1,0:T(8,128)(2,1)S(1)} %copy-done.29), channel_id=1, source_target_pairs={{0,1},{1,0},{2,3},{3,2},{4,5},{5,4},{6,7},{7,6},{8,9},{9,8},{10,11... | collective-permute-start | bytes 786440 | tf_op jit(solution)/shard_map/ppermute | solution.py:761
  57.2 5.0 %collective-permute-start.4 = (bf16[1024,256]{1,0:T(8,128)(2,1)}, bf16[1024,256]{1,0:T(8,128)(2,1)}, u32[]{:S(2)}, u32[]{:S(2)}) collective-permute-start(bf16[1024,256]{1,0:T(8,128)(2,1)} %get-tuple-element.111.refs_5_), channel_id=1, source_target_pairs={{0,1},{1,0},{2,3},{3,2},{4,5},{5,4},{6,7},{7,6},{8,9},{9,8},{10,11... | collective-permute-start | bytes 1572872 | tf_op jit(solution)/shard_map/ppermute | solution.py:767
  85.6 8.4 %collective-permute-start.11 = (bf16[256,512]{1,0:T(8,128)(2,1)S(1)}, bf16[256,512]{1,0:T(8,128)(2,1)S(1)}, u32[]{:S(2)}, u32[]{:S(2)}) collective-permute-start(bf16[256,512]{1,0:T(8,128)(2,1)S(1)} %convolution_convert_fusion.10), channel_id=1, source_target_pairs={{0,1},{1,0},{2,3},{3,2},{4,5},{5,4},{6,7},{7,6},{8,9},{9,8},{10,11... | collective-permute-start | bytes 786440 | tf_op jit(solution)/shard_map/ppermute | solution.py:767
  89.1 5.4 %collective-permute-start.9 = (bf16[1024,512]{1,0:T(8,128)(2,1)S(1)}, bf16[1024,512]{1,0:T(8,128)(2,1)S(1)}, u32[]{:S(2)}, u32[]{:S(2)}) collective-permute-start(bf16[1024,512]{1,0:T(8,128)(2,1)S(1)} %convolution_convert_fusion.2), channel_id=1, source_target_pairs={{0,1},{1,0},{2,3},{3,2},{4,5},{5,4},{6,7},{7,6},{8,9},{9,8},{10,11... | collective-permute-start | bytes 3145736 | tf_op jit(solution)/shard_map/ppermute | solution.py:767
  90.6 4.3 %collective-permute-start.10 = (bf16[1024,512]{1,0:T(8,128)(2,1)S(1)}, bf16[1024,512]{1,0:T(8,128)(2,1)S(1)}, u32[]{:S(2)}, u32[]{:S(2)}) collective-permute-start(bf16[1024,512]{1,0:T(8,128)(2,1)S(1)} %convolution_convert_fusion), channel_id=1, source_target_pairs={{0,1},{1,0},{2,3},{3,2},{4,5},{5,4},{6,7},{7,6},{8,9},{9,8},{10,11... | collective-permute-start | bytes 3145736 | tf_op jit(solution)/shard_map/ppermute | solution.py:767
  91.0 4.4 %collective-permute-start.8 = (bf16[1024,256]{1,0:T(8,128)(2,1)S(1)}, bf16[1024,256]{1,0:T(8,128)(2,1)S(1)}, u32[]{:S(2)}, u32[]{:S(2)}) collective-permute-start(bf16[1024,256]{1,0:T(8,128)(2,1)S(1)} %get-tuple-element.115), channel_id=1, source_target_pairs={{0,1},{1,0},{2,3},{3,2},{4,5},{5,4},{6,7},{7,6},{8,9},{9,8},{10,11... | collective-permute-start | bytes 1572872 | tf_op jit(solution)/shard_map/ppermute | solution.py:767
  95.4 18.9 %collective-permute-start.13 = (bf16[2,4,64,512]{3,2,1,0:T(8,128)(2,1)S(1)}, bf16[2,4,64,512]{3,2,1,0:T(8,128)(2,1)S(1)}, u32[]{:S(2)}, u32[]{:S(2)}) collective-permute-start(bf16[2,4,64,512]{3,2,1,0:T(8,128)(2,1)S(1)} %get-tuple-element.132), channel_id=1, source_target_pairs={{0,2},{2,0},{4,6},{6,4},{8,10},{10,8},{12,14},{14,12},{16,18},{18,... | collective-permute-start | bytes 1572872 | tf_op jit(solution)/shard_map/ppermute | solution.py:673
  98.4 16.5 %collective-permute-start.14 = (bf16[2,4,80,512]{3,2,1,0:T(8,128)(2,1)S(1)}, bf16[2,4,80,512]{3,2,1,0:T(8,128)(2,1)S(1)}, u32[]{:S(2)}, u32[]{:S(2)}) collective-permute-start(bf16[2,4,80,512]{3,2,1,0:T(8,128)(2,1)S(1)} %get-tuple-element.134), channel_id=1, source_target_pairs={{0,4},{2,6},{4,0},{6,2},{8,12},{10,14},{12,8},{14,10},{16,20},{18,... | collective-permute-start | bytes 1966088 | tf_op jit(solution)/shard_map/ppermute | solution.py:673
  113.7 12.8 %collective-permute-start.12 = (bf16[1024,256]{1,0:T(8,128)(2,1)S(1)}, bf16[1024,256]{1,0:T(8,128)(2,1)S(1)}, u32[]{:S(2)}, u32[]{:S(2)}) collective-permute-start(bf16[1024,256]{1,0:T(8,128)(2,1)S(1)} %get-tuple-element.129), channel_id=1, source_target_pairs={{0,1},{1,0},{2,3},{3,2},{4,5},{5,4},{6,7},{7,6},{8,9},{9,8},{10,11... | collective-permute-start | bytes 1572872 | tf_op jit(solution)/shard_map/ppermute | solution.py:767
  115.1 8.4 %collective-permute-start.16 = (bf16[4,64,512]{2,1,0:T(8,128)(2,1)S(1)}, bf16[4,64,512]{2,1,0:T(8,128)(2,1)S(1)}, u32[]{:S(2)}, u32[]{:S(2)}) collective-permute-start(bf16[4,64,512]{2,1,0:T(8,128)(2,1)S(1)} %get-tuple-element.140), channel_id=1, source_target_pairs={{0,4},{2,6},{4,0},{6,2},{8,12},{10,14},{12,8},{14,10},{16,20},{18,... | collective-permute-start | bytes 786440 | tf_op jit(solution)/shard_map/ppermute | solution.py:673
  116.7 8.5 %collective-permute-start.17 = (bf16[4,80,512]{2,1,0:T(8,128)(2,1)S(1)}, bf16[4,80,512]{2,1,0:T(8,128)(2,1)S(1)}, u32[]{:S(2)}, u32[]{:S(2)}) collective-permute-start(bf16[4,80,512]{2,1,0:T(8,128)(2,1)S(1)} %get-tuple-element.142), channel_id=1, source_target_pairs={{0,2},{2,0},{4,6},{6,4},{8,10},{10,8},{12,14},{14,12},{16,18},{18,... | collective-permute-start | bytes 983048 | tf_op jit(solution)/shard_map/ppermute | solution.py:673
  119.3 6.0 %collective-permute-start.15 = (bf16[512,512]{1,0:T(8,128)(2,1)S(1)}, bf16[512,512]{1,0:T(8,128)(2,1)S(1)}, u32[]{:S(2)}, u32[]{:S(2)}) collective-permute-start(bf16[512,512]{1,0:T(8,128)(2,1)S(1)} %get-tuple-element.138), channel_id=1, source_target_pairs={{0,1},{1,0},{2,3},{3,2},{4,5},{5,4},{6,7},{7,6},{8,9},{9,8},{10,11... | collective-permute-start | bytes 1572872 | tf_op jit(solution)/shard_map/ppermute | solution.py:767
  126.5 12.1 %collective-permute-start.19 = (bf16[144,512]{1,0:T(8,128)(2,1)S(1)}, bf16[144,512]{1,0:T(8,128)(2,1)S(1)}, u32[]{:S(2)}, u32[]{:S(2)}) collective-permute-start(bf16[144,512]{1,0:T(8,128)(2,1)S(1)} %get-tuple-element.151), channel_id=1, source_target_pairs={{0,8},{2,10},{4,12},{6,14},{8,0},{10,2},{12,4},{14,6},{16,24},{18,... | collective-permute-start | bytes 442376 | tf_op jit(solution)/shard_map/ppermute | solution.py:673
  130.0 12.9 %collective-permute-start.20 = (bf16[144,512]{1,0:T(8,128)(2,1)S(1)}, bf16[144,512]{1,0:T(8,128)(2,1)S(1)}, u32[]{:S(2)}, u32[]{:S(2)}) collective-permute-start(bf16[144,512]{1,0:T(8,128)(2,1)S(1)} %get-tuple-element.152), channel_id=1, source_target_pairs={{0,16},{2,18},{4,20},{6,22},{8,24},{10,26},{12,28},{14,30},{16,0},... | collective-permute-start | bytes 442376 | tf_op jit(solution)/shard_map/ppermute | solution.py:673
  130.6 12.3 %collective-permute-start.21 = (bf16[144,512]{1,0:T(8,128)(2,1)S(1)}, bf16[144,512]{1,0:T(8,128)(2,1)S(1)}, u32[]{:S(2)}, u32[]{:S(2)}) collective-permute-start(bf16[144,512]{1,0:T(8,128)(2,1)S(1)} %get-tuple-element.153), channel_id=1, source_target_pairs={{0,24},{2,26},{4,28},{6,30},{8,16},{10,18},{12,20},{14,22},{16,8},... | collective-permute-start | bytes 442376 | tf_op jit(solution)/shard_map/ppermute | solution.py:673
  136.4 7.7 %collective-permute-start.18 = (bf16[1024,256]{1,0:T(8,128)(2,1)S(1)}, bf16[1024,256]{1,0:T(8,128)(2,1)S(1)}, u32[]{:S(2)}, u32[]{:S(2)}) collective-permute-start(bf16[1024,256]{1,0:T(8,128)(2,1)S(1)} %get-tuple-element.149), channel_id=1, source_target_pairs={{0,1},{1,0},{2,3},{3,2},{4,5},{5,4},{6,7},{7,6},{8,9},{9,8},{10,11... | collective-permute-start | bytes 1572872 | tf_op jit(solution)/shard_map/ppermute | solution.py:767
  136.5 1.8 collective-permute-start.30
  138.4 4.7 %collective-permute-start.29 = (bf16[512,256]{1,0:T(8,128)(2,1)S(1)}, bf16[512,256]{1,0:T(8,128)(2,1)S(1)}, u32[]{:S(2)}, u32[]{:S(2)}) collective-permute-start(bf16[512,256]{1,0:T(8,128)(2,1)S(1)} %convolution_convert_fusion.4), channel_id=1, source_target_pairs={{0,1},{1,0},{2,3},{3,2},{4,5},{5,4},{6,7},{7,6},{8,9},{9,8},{10,11... | collective-permute-start | bytes 786440 | tf_op jit(solution)/shard_map/ppermute | solution.py:767
  138.5 5.1 %collective-permute-start.28 = (bf16[256,512]{1,0:T(8,128)(2,1)S(1)}, bf16[256,512]{1,0:T(8,128)(2,1)S(1)}, u32[]{:S(2)}, u32[]{:S(2)}) collective-permute-start(bf16[256,512]{1,0:T(8,128)(2,1)S(1)} %convolution_convert_fusion.6), channel_id=1, source_target_pairs={{0,1},{1,0},{2,3},{3,2},{4,5},{5,4},{6,7},{7,6},{8,9},{9,8},{10,11... | collective-permute-start | bytes 786440 | tf_op jit(solution)/shard_map/ppermute | solution.py:767
  144.1 28.4 %collective-permute-start.22 = (bf16[144,512]{1,0:T(8,128)(2,1)S(1)}, bf16[144,512]{1,0:T(8,128)(2,1)S(1)}, u32[]{:S(2)}, u32[]{:S(2)}) collective-permute-start(bf16[144,512]{1,0:T(8,128)(2,1)S(1)} %add_convert_fusion.6), channel_id=1, source_target_pairs={{0,8},{2,10},{4,12},{6,14},{8,0},{10,2},{12,4},{14,6},{16,24},{18,... | collective-permute-start | bytes 442376 | tf_op jit(solution)/shard_map/ppermute | solution.py:684
  146.9 25.6 %collective-permute-start.23 = (bf16[144,512]{1,0:T(8,128)(2,1)S(1)}, bf16[144,512]{1,0:T(8,128)(2,1)S(1)}, u32[]{:S(2)}, u32[]{:S(2)}) collective-permute-start(bf16[144,512]{1,0:T(8,128)(2,1)S(1)} %add_convert_fusion.6), channel_id=1, source_target_pairs={{0,16},{2,18},{4,20},{6,22},{8,24},{10,26},{12,28},{14,30},{16,0},... | collective-permute-start | bytes 442376 | tf_op jit(solution)/shard_map/ppermute | solution.py:684
  146.9 25.6 %collective-permute-start.24 = (bf16[144,512]{1,0:T(8,128)(2,1)S(1)}, bf16[144,512]{1,0:T(8,128)(2,1)S(1)}, u32[]{:S(2)}, u32[]{:S(2)}) collective-permute-start(bf16[144,512]{1,0:T(8,128)(2,1)S(1)} %add_convert_fusion.6), channel_id=1, source_target_pairs={{0,24},{2,26},{4,28},{6,30},{8,16},{10,18},{12,20},{14,22},{16,8},... | collective-permute-start | bytes 442376 | tf_op jit(solution)/shard_map/ppermute | solution.py:684
  172.7 8.2 %collective-permute-start.27 = (bf16[4,80,512]{2,1,0:T(8,128)(2,1)S(1)}, bf16[4,80,512]{2,1,0:T(8,128)(2,1)S(1)}, u32[]{:S(2)}, u32[]{:S(2)}) collective-permute-start(bf16[4,80,512]{2,1,0:T(8,128)(2,1)S(1)} %pad_maximum_fusion.2), channel_id=1, source_target_pairs={{0,2},{2,0},{4,6},{6,4},{8,10},{10,8},{12,14},{14,12},{16,18},{18,... | collective-permute-start | bytes 983048 | tf_op jit(solution)/shard_map/ppermute | solution.py:684
  173.6 6.6 %collective-permute-start.26 = (bf16[4,64,512]{2,1,0:T(8,128)(2,1)S(1)}, bf16[4,64,512]{2,1,0:T(8,128)(2,1)S(1)}, u32[]{:S(2)}, u32[]{:S(2)}) collective-permute-start(bf16[4,64,512]{2,1,0:T(8,128)(2,1)S(1)} %pad_maximum_fusion.5), channel_id=1, source_target_pairs={{0,4},{2,6},{4,0},{6,2},{8,12},{10,14},{12,8},{14,10},{16,20},{18,... | collective-permute-start | bytes 786440 | tf_op jit(solution)/shard_map/ppermute | solution.py:684
  178.1 64.2 %collective-permute-start.25 = (bf16[1024,512]{1,0:T(8,128)(2,1)S(1)}, bf16[1024,512]{1,0:T(8,128)(2,1)S(1)}, u32[]{:S(2)}, u32[]{:S(2)}) collective-permute-start(bf16[1024,512]{1,0:T(8,128)(2,1)S(1)} %get-tuple-element.165), channel_id=1, source_target_pairs={{0,1},{1,0},{2,3},{3,2},{4,5},{5,4},{6,7},{7,6},{8,9},{9,8},{10,11... | collective-permute-start | bytes 3145736 | tf_op jit(solution)/shard_map/ppermute | solution.py:767
  181.0 58.3 %collective-permute-start.32 = (bf16[8,64,512]{2,1,0:T(8,128)(2,1)S(1)}, bf16[8,64,512]{2,1,0:T(8,128)(2,1)S(1)}, u32[]{:S(2)}, u32[]{:S(2)}) collective-permute-start(bf16[8,64,512]{2,1,0:T(8,128)(2,1)S(1)} %bitcast.124), channel_id=1, source_target_pairs={{0,2},{2,0},{4,6},{6,4},{8,10},{10,8},{12,14},{14,12},{16,18},{18,... | collective-permute-start | bytes 1572872 | tf_op jit(solution)/shard_map/ppermute | solution.py:684
  182.1 58.6 %collective-permute-start.31 = (bf16[8,80,512]{2,1,0:T(8,128)(2,1)S(1)}, bf16[8,80,512]{2,1,0:T(8,128)(2,1)S(1)}, u32[]{:S(2)}, u32[]{:S(2)}) collective-permute-start(bf16[8,80,512]{2,1,0:T(8,128)(2,1)S(1)} %bitcast.122), channel_id=1, source_target_pairs={{0,4},{2,6},{4,0},{6,2},{8,12},{10,14},{12,8},{14,10},{16,20},{18,... | collective-permute-start | bytes 1966088 | tf_op jit(solution)/shard_map/ppermute | solution.py:684
  (50 other events, 295.1 us)

commit v5 on v4

--- a/solution.py
+++ b/solution.py
@@ -439,7 +439,7 @@
         + [shape(width, BF16)] * mp
         + [shape(ff, BF16)] * (2 * mp)
         + [jax.ShapeDtypeStruct((4, d), F32)],
-        compiler_params=params(44),
+        compiler_params=params(36),
         cost_estimate=cost(8 * share * d * ff * mp + 4 * share * d * d, share * ff * mp * 4, share * ff * mp),
     )(*cctx, n1, cot, *co, *up, *down, gain, shift)
     out, da2, n2, e3, e2 = outs[:5]
@@ -493,7 +493,7 @@
         + [jax.ShapeDtypeStruct((share, width), BF16)] * mp
         + [jax.ShapeDtypeStruct((2, d), F32)],
         compiler_params=params(16),
-        cost_estimate=cost(4 * share * d * d, share * d * 14),
+        cost_estimate=cost(1, 1),
     )(*dqc, *cq, *wo, da2, xhat, rstd, gain)
     return outs[0], outs[1], outs[2 : 2 + mp], outs[-1]
 
@@ -526,7 +526,7 @@
         out_shape=[jax.ShapeDtypeStruct((tokens // mp, d), F32)]
         + [jax.ShapeDtypeStruct((tokens // mp, d), BF16)] * (mp - 1),
         compiler_params=params(16),
-        cost_estimate=cost(2 * tokens * d * width * len(grads), tokens * d * 6),
+        cost_estimate=cost(1, 1),
     )(sc, *grads, w)
     return outs
 
@@ -556,31 +556,32 @@
             device_id_type=MESH,
         )
         copy.start()
-        copies[c].append(copy)
+        copies[c][s] = copy
 
     def rows(off, count):
         return pl.ds(pl.multiple_of(off, 16), count)
 
-    copies = [[] for _ in range(len(plan) + 1)]
-    spans = [[(first, count)] for _, first, count, _ in plan]
-    slots = [[] for _ in plan]
+    copies = [{} for _ in range(len(plan) + 1)]
+    spans = []
+    for _, count, order, _ in plan:
+        span = [(0, count)]
+        for b in order:
+            off, size = span[-1]
+            span.append((off + bit[b] * (size // 2), size // 2))
+        spans.append(span)
 
     def held(c, s, b):
-        a, first, count, _ = plan[c]
+        a, count, _, _ = plan[c]
         half = count >> (s + 1)
-        base = first if s == 0 else slots[c][s - 1]
-        ref = ins[a] if s == 0 else got[c]
-        return ref, base + (1 - bit[b]) * half, base + bit[b] * half, half
+        base = count - (count >> (s - 1)) if s else 0
+        return (got[c] if s else ins[a]), base + (1 - bit[b]) * half, base + bit[b] * half, half
 
     def begin(c, s):
-        a, first, count, order = plan[c]
+        a, count, order, _ = plan[c]
         if s < nbits:
             b = order[s]
             ref, gives, _, half = held(c, s, b)
-            slots[c].append(count - (count >> s))
-            off = spans[c][s][0]
-            spans[c].append((off + bit[b] * half, half))
-            send(c, s, b, ref.at[rows(gives, half), :], got[c].at[pl.ds(slots[c][s], half), :])
+            send(c, s, b, ref.at[rows(gives, half), :], got[c].at[pl.ds(count - (count >> s), half), :])
         else:
             j = 2 * nbits - 1 - s
             block = outs[a].at[rows(*spans[c][j + 1]), :]
@@ -589,9 +590,9 @@
     def finish(c, s):
         copies[c][s].wait_recv()
         if s < nbits:
-            a, _, _, order = plan[c]
+            a, count, order, _ = plan[c]
             ref, _, stays, half = held(c, s, order[s])
-            came = pl.ds(slots[c][s], half)
+            came = pl.ds(count - (count >> s), half)
             total = ref[rows(stays, half), :].astype(F32) + got[c][came, :].astype(F32)
             if s < nbits - 1:
                 got[c][came, :] = total.astype(BF16)
@@ -601,63 +602,66 @@
     last = len(plan)
     size = ins[n].shape[0]
     outs[n][...] = ins[n][...]
-    for s in range(2 * nbits + 1):
-        if 1 <= s <= nbits:
-            copies[last][s - 1].wait()
-            outs[n][...] = (
-                outs[n][...].astype(F32) + got[last][(s - 1) * size : s * size, :].astype(F32)
-            ).astype(BF16)
-        if s < nbits:
-            send(last, s, s, outs[n], got[last].at[pl.ds(s * size, size), :])
-        for c in range(len(plan)):
-            if s >= 1:
+    for c, (a, _, _, done) in enumerate(plan):
+        if done:
+            outs[a][rows(*spans[c][nbits]), :] = ins[a][...]
+    for t in range(2 * nbits + 1):
+        for c, (_, _, _, done) in enumerate(plan):
+            s = t + done
+            if done < s < 2 * nbits or (s == 2 * nbits and not done):
                 finish(c, s - 1)
             if s < 2 * nbits:
                 begin(c, s)
-    for c in range(len(plan)):
-        for copy in copies[c]:
+        if 1 <= t <= nbits:
+            copies[last][t - 1].wait()
+            outs[n][...] = (
+                outs[n][...].astype(F32) + got[last][(t - 1) * size : t * size, :].astype(F32)
+            ).astype(BF16)
+        if t < nbits:
+            send(last, t, t, outs[n], got[last].at[pl.ds(t * size, size), :])
+    for c, (_, _, _, done) in enumerate(plan):
+        if done:
+            finish(c, 2 * nbits - 1)
+        for copy in copies[c].values():
             copy.wait_send()
 
 
-def all_sum(arrays, splits, small, devices):
+def all_sum(arrays, blocks, small, devices):
     nbits = devices.bit_length() - 1
-    if devices != 1 << nbits or nbits < 3:
-        return [lax.psum(a, "batch") for a in (*arrays, small)]
-    x_y, y_x = tuple(range(nbits)), (1, 0, *range(2, nbits))
-    far = (*range(2, nbits), 0, 1)
+    line = tuple(range(nbits - 1, 1, -1))
     flat = [a.reshape(-1, a.shape[-1]) for a in arrays]
-    plan, used = [], []
-    for a, parts in zip(flat, splits):
-        count = a.shape[0] // parts
-        if a.shape[0] % parts == 0 and count % (16 * devices) == 0:
-            for p in range(parts):
-                order = (x_y, y_x, far)[len(plan) % 3]
-                plan.append((len(used), p * count, count, order))
-            used.append(a)
-        else:
-            used.append(None)
-    keep = [i for i, a in enumerate(used) if a is not None]
-    plan = [(keep.index(i), *rest) for i, *rest in plan]
+    fits = [a.shape[0] % (16 * devices) == 0 for a in flat]
+    plan, operands, shapes = [], [], []
+    for a, first in blocks:
+        plan.append((len(operands), a.shape[0] * devices, (*first, *line), nbits))
+        operands.append(a)
+        shapes.append((a.shape[0] * devices, a.shape[1]))
+    for a, fit in zip(flat, fits):
+        if fit:
+            first = ((0, 1), (1, 0))[len(plan) % 2]
+            plan.append((len(operands), a.shape[0], (*first, *range(2, nbits)), 0))
+            operands.append(a)
+            shapes.append(a.shape)
     small = jnp.pad(small, ((0, 16 - small.shape[0]), (0, 0)))
-    operands = [used[i] for i in keep] + [small]
+    operands.append(small)
+    shapes.append(small.shape)
     vmem = pl.BlockSpec(memory_space=pltpu.VMEM)
     sums = pl.pallas_call(
-        functools.partial(all_sum_kernel, plan, nbits, len(keep)),
+        functools.partial(all_sum_kernel, plan, nbits, len(plan)),
         in_specs=[vmem] * len(operands),
         out_specs=[vmem] * len(operands),
-        out_shape=[jax.ShapeDtypeStruct(a.shape, a.dtype) for a in operands],
-        scratch_shapes=[pltpu.VMEM((rows, operands[i].shape[1]), BF16) for i, _, rows, _ in plan]
+        out_shape=[jax.ShapeDtypeStruct(shape, BF16) for shape in shapes],
+        scratch_shapes=[pltpu.VMEM((16 if done else rows, operands[i].shape[1]), BF16) for i, rows, _, done in plan]
         + [pltpu.VMEM((16 * nbits, small.shape[1]), BF16)]
         + [pltpu.SemaphoreType.DMA((len(plan) + 1, 2 * nbits))] * 2,
         compiler_params=pltpu.CompilerParams(
-            collective_id=7, has_side_effects=True, vmem_limit_bytes=20 << 20
+            collective_id=7, has_side_effects=True, vmem_limit_bytes=28 << 20
         ),
     )(*operands)
-    outs = [
-        sums[keep.index(i)].reshape(a.shape) if i in keep else lax.psum(a, "batch")
-        for i, a in enumerate(arrays)
-    ]
-    return outs + [sums[-1]]
+    whole_ones = sums[: len(blocks)]
+    rest = iter(sums[len(blocks) : -1])
+    outs = [next(rest).reshape(a.shape) if fit else lax.psum(a, "batch") for a, fit in zip(arrays, fits)]
+    return outs, whole_ones, sums[-1]
 
 
 def across(r, shift, devices):
@@ -678,54 +682,6 @@
     for b in blocks[1:]:
         total += b.astype(F32)
     return total.astype(BF16)
-
-
-def gather_step(block, shift, bits, devices):
-    return [block] + [lax.ppermute(block, "batch", across(r, shift, devices)) for r in range(1, 1 << bits)]
-
-
-def in_order(pieces, place):
-    return jnp.stack(
-        [lax.select_n(place ^ c, *pieces) if len(pieces) > 1 else pieces[0] for c in range(len(pieces))]
-    )
-
-
-def lay_kernel(n, rows, sc, *refs):
-    pieces, outs = refs[:n], refs[n:]
-    c = pl.program_id(0)
-    for r in range(n):
-
-        @pl.when((sc[0] ^ c) == r)
-        def _():
-            at = 0
-            for out, count in zip(outs, rows):
-                out[...] = pieces[r][:, at : at + count, :].astype(F32).reshape(out.shape)
-                at += count
-
-
-def lay_out(pieces, place, shapes, rows):
-    n = len(pieces)
-    d = pieces[0].shape[-1]
-    if any(count % 16 for count in rows):
-        blocks = in_order(pieces, place)
-        flat = blocks.reshape(-1, *blocks.shape[2:]).astype(F32)
-        at, outs = 0, []
-        for shape, count in zip(shapes, rows):
-            outs.append(flat[:, at : at + count].reshape(shape))
-            at += count
-        return outs
-    return pl.pallas_call(
-        functools.partial(lay_kernel, n, rows),
-        grid_spec=pltpu.PrefetchScalarGridSpec(
-            num_scalar_prefetch=1,
-            grid=(n,),
-            in_specs=[whole(p) for p in pieces],
-            out_specs=[pl.BlockSpec((s[0] // n, d), lambda i, sc: (i, 0)) for s in shapes],
-        ),
-        out_shape=[jax.ShapeDtypeStruct(s, F32) for s in shapes],
-        compiler_params=params(14),
-        cost_estimate=cost(0, sum(s[0] * d * 6 for s in shapes)),
-    )(place.reshape(1).astype(jnp.int32), *pieces)
 
 
 def shards(
@@ -827,43 +783,48 @@
         collect(grads(hid, [e3] * mp)).astype(BF16),
         collect(grads(cctx, [e2] * mp)).astype(BF16),
     ]
+    hidden = all(g.shape[0] % (16 * devices) == 0 for g in early)
     row = lax.axis_index("batch")
     far = devices.bit_length() - 3
-    one = early[0].reshape(2, 2, 1 << far, -1, d)
-    two = jnp.concatenate([g.reshape(devices, -1, d) for g in early[1:]], axis=1)
-    two = two.reshape(2, 2, 1 << far, -1, d)
-    dcctx_parts, one, two = lax.optimization_barrier((dcctx_parts, cut(one, 0, 1, row), cut(two, 1, 1, row)))
-    one, two = scatter_step(one, 0, devices), scatter_step(two, 1, devices)
+    if hidden:
+        one = early[0].reshape(4, 1 << far, -1, d)
+        two = jnp.concatenate([g.reshape(4, 1 << far, -1, d) for g in early[1:]], axis=2)
+        here = row % 4
+        mirrored = here % 2 * 2 + here // 2
+        blocks = [
+            jnp.concatenate(
+                [
+                    lax.dynamic_index_in_dim(one, mirrored ^ (0, 2, 1, 3)[r], 0, keepdims=False),
+                    lax.dynamic_index_in_dim(two, here ^ r, 0, keepdims=False),
+                ],
+                axis=1,
+            )
+            for r in range(4)
+        ]
+        dcctx_parts, blocks = lax.optimization_barrier((dcctx_parts, blocks))
+        blocks = scatter_step(blocks, 0, devices)
     dqc_parts, dkc, dvc = attend_back(
         cross_table, qc_parts, dcctx_parts, cctx_parts, pair[0], cross_kt, pair[1], cross_lo, cross_hi, cross_lse, mp, bq, bk
     )
     dqc = exchange(dqc_parts)
-    dkc, one, two = lax.optimization_barrier((dkc, cut(add_up(one), 1, 1, row), cut(add_up(two), 0, 1, row)))
-    one, two = scatter_step(one, 1, devices), scatter_step(two, 0, devices)
+    if hidden:
+        dqc, block = lax.optimization_barrier((dqc, add_up(blocks)))
+    da1, e1, dctx, small1 = pre_self(dqc, cq, wo, da2, xhat1, rstd1, gain, bt)
+    dctx_parts = exchange(dctx)
     mem_bt = min(512, mem_share)
     mem_nb = mem_share // mem_bt
     mem_blocks = ((((me - jnp.arange(mp)) % mp) * mem_nb)[:, None] + jnp.arange(mem_nb)[None, :]).reshape(-1)
     memory_parts = input_part(mem_blocks.astype(jnp.int32), [dkc, dvc], cross_kv, mp, mem_bt)
     memory_grad = collect(memory_parts)
-    cross_kv_grad = [mm(memory, g, TN).astype(BF16) for g in (dkc, dvc)]
-    blocks = jnp.concatenate([add_up(one), add_up(two)], axis=1)
-    dqc, cross_kv_grad, memory_grad, blocks = lax.optimization_barrier(
-        (dqc, cross_kv_grad, memory_grad, cut(blocks, 2, far, row))
-    )
-    blocks = scatter_step(blocks, 2, devices)
-    da1, e1, dctx, small1 = pre_self(dqc, cq, wo, da2, xhat1, rstd1, gain, bt)
-    dctx_parts = exchange(dctx)
+    cross_kv_grad = [mm(memory, g, TN) for g in (dkc, dvc)]
     cross_query_grad = collect(grads([n1] * mp, dqc))
     self_out_grad = collect(grads(ctx, [e1] * mp))
-    dctx_parts, block = lax.optimization_barrier((dctx_parts, add_up(blocks)))
-    blocks = gather_step(block, 2, far, devices)
+    if hidden:
+        dctx_parts, blocks = lax.optimization_barrier((dctx_parts, cut(block, 2, far, row)))
+        blocks = scatter_step(blocks, 2, devices)
     (dq,), dk, dv = attend_back(
         self_table, proj[:1], dctx_parts, ctx_parts, proj[1], self_kt, proj[2], self_lo, self_hi, self_lse, mp, bq, bk
     )
-    blocks = in_order(blocks, row >> 2)
-    cut_at = one[0].shape[1]
-    dq, one, two = lax.optimization_barrier((dq, blocks[:, :cut_at], blocks[:, cut_at:]))
-    one, two = gather_step(one, 1, 1, devices), gather_step(two, 0, 1, devices)
     in_bt = min(512, share)
     in_blocks = place.reshape(-1, in_bt)[:, 0] // in_bt
     input_parts = input_part(in_blocks.astype(jnp.int32), [dq, dk, dv], self_qkv, mp, in_bt)
@@ -876,28 +837,22 @@
         lax.dynamic_slice_in_dim(small, ((me - r) % mp) * part, part, 1).astype(BF16) for r in range(mp)
     ]
     small = collect(pieces)
-    self_qkv_grad, one, two = lax.optimization_barrier(
-        (self_qkv_grad, in_order(one, row // 2 % 2), in_order(two, row % 2))
-    )
-    one = gather_step(one.reshape(-1, *one.shape[2:]), 0, 1, devices)
-    two = gather_step(two.reshape(-1, *two.shape[2:]), 1, 1, devices)
-    *summed, small = all_sum(
-        [
-            g.astype(BF16)
-            for g in (
-                *self_qkv_grad,
-                self_out_grad,
-                cross_query_grad,
-                *cross_kv_grad,
-            )
-        ],
-        (1, 1, 1, 1, 1, 1, 1),
-        small.astype(BF16),
-        devices,
-    )
-    rows = [g.shape[0] // devices for g in early]
-    (up_grad,) = lay_out(one, row % 2, [early[0].shape], rows[:1])
-    down_grad, cross_out_grad = lay_out(two, row // 2 % 2, [g.shape for g in early[1:]], rows[1:])
+    late = [*self_qkv_grad, self_out_grad, cross_query_grad, *cross_kv_grad]
+    late = [g.astype(BF16) for g in late]
+    if hidden:
+        block = add_up(blocks)
+        count = early[0].shape[0] // devices
+        summed, (up_grad, rest), small = all_sum(
+            late, [(block[:count], (0, 1)), (block[count:], (1, 0))], small.astype(BF16), devices
+        )
+        up_grad = up_grad.astype(F32)
+        rest = rest.reshape(devices, -1, d)
+        count = early[1].shape[0] // devices
+        down_grad = rest[:, :count].reshape(early[1].shape).astype(F32)
+        cross_out_grad = rest[:, count:].reshape(early[2].shape).astype(F32)
+    else:
+        summed, _, small = all_sum(late + early, [], small.astype(BF16), devices)
+        *summed, up_grad, down_grad, cross_out_grad = [g.astype(F32) for g in summed]
     dwq, dwk, dwv, self_out_grad, cross_query_grad, dck, dcv = [g.astype(F32) for g in summed]
     summed = [jnp.stack([dwq, dwk, dwv]), self_out_grad, cross_query_grad, jnp.stack([dck, dcv])]
     summed += [cross_out_grad, up_grad, down_grad]

time: 247 us -> 231 us (0.935); the launches traced: 244 us -> 232 us
  starting transfers between devices: 27.2 us -> 18.7 us
  local copies, waits for them, and re-layouts: 24.6 us -> 19.5 us
  waiting for transfers between devices: 14 us -> 10.2 us
  other arithmetic: 12.2 us -> 15.9 us
    ppermute x7 -> x0, starting transfers between devices: 9.92 us -> none  [gather_step(): lax.ppermute(block, 'batch', across(r, shift, devices))]
    convert_element_type x0 -> x3, other arithmetic: none -> 4.16 us  [the longest x1 1.68 us: shards(): down_grad = rest[:, :count].reshape(early[1].shape).astype(F32)]
    transpose x2, local copies, waits for them, and re-layouts: 4.41 us -> 1.62 us  [input_part(): w = w.swapaxes(1, 2).reshape(-1, d)]
    ppermute x7 -> x6, waiting for transfers between devices: 10.1 us -> 7.65 us  [scatter_step(): lax.ppermute(b, 'batch', across(r, shift, devices))]
    unnamed x100 -> x98, local copies, waits for them, and re-layouts: 18.2 us -> 15.9 us
    pallas_call x3 -> x1, Pallas kernels: 54.4 us -> 56.4 us  [all_sum(): pl.pallas_call(functools.partial(all_sum_kernel, plan, nbits, len(plan)),...]
    ppermute x7 -> x6, starting transfers between devices: 12.5 us -> 13.4 us  [scatter_step(): lax.ppermute(b, 'batch', across(r, shift, devices))]
  transfers between devices with their start and end apart: 33 -> 25, of which waited for: 9 -> 7; matrix products, arithmetic and copies ran while one was open for 10% -> 10% of each run, Pallas kernels for 45% -> 47%
where the time goes in v5:
time: 231 us; the launch traced here: 232 us
  Pallas kernels  151 us (65%)
  local copies, waits for them, and re-layouts  19.5 us (8%)
  starting transfers between devices  18.7 us (8%)
  other arithmetic  15.9 us (7%)
  matrix products  14.5 us (6%)
  waiting for transfers between devices  10.2 us (4%)
    pallas_call x1, Pallas kernels, all_sum(): pl.pallas_call(functools.partial(all_sum_kernel, plan, nbits, len(plan)),...  56.4 us
    pallas_call x2, Pallas kernels, attend_back(): pl.pallas_call(functools.partial(attend_back_kernel, nblk, per_part, len(...  35 us
    pallas_call x2, Pallas kernels, attend(): pl.pallas_call(functools.partial(attend_kernel, nblk, per_part, len(q_par...  26.6 us
    pallas_call x1, Pallas kernels, middle(): pl.pallas_call(functools.partial(middle_kernel, mp), grid=(share // bt,),...  17.5 us
    unnamed x98, local copies, waits for them, and re-layouts  15.9 us
    dot_general x15, matrix products, mm(): return lax.dot_general(a, b, dims, preferred_element_type=F32)  14.5 us
    ppermute x6, starting transfers between devices, scatter_step(): lax.ppermute(b, 'batch', across(r, shift, devices))  13.4 us
    ppermute x6, waiting for transfers between devices, scatter_step(): lax.ppermute(b, 'batch', across(r, shift, devices))  7.65 us
  transfers between devices with their start and end apart: 25, of which 7 were waited for; matrix products, arithmetic and copies ran while one was open for 10% of the time, Pallas kernels for 47%

profile of v5, /device:TPU:0, one launch (start us, length us, event | category | flops | bytes accessed | tf_op | source)
XLA Modules:
  0.0 231.8 jit_solution(6307554639157105892)
XLA Ops:
  4.8 1.6 copy-done
  7.5 2.9 %shard_map.229 = (bf16[2048,256]{1,0:T(8,128)(2,1)S(1)}, bf16[2048,256]{1,0:T(8,128)(2,1)S(1)}, bf16[2048,256]{1,0:T(8,128)(2,1)S(1)}, bf16[256,2048]{1,0:T(8,128)(2,1)S(1)}, bf16[256,2048]{1,0:T(8,128)(2,1)S(1)}) custom-call(bf16[2048,512]{1,0:T(8,128)(2,1)S(1)} %copy-done, bf16[3,512,256]{2,1,0:T(8,128)(2,1)S(1)} %copy-done.12), custom_call_target="tpu_custom_call" | custom-call | flops 1610612736 | bytes 8388608 | tf_op jit(solution)/shard_map/pallas_call | solution.py:288
  12.5 15.2 %shard_map.230 = (bf16[1024,256]{1,0:T(8,128)(2,1)S(1)}, bf16[1024,256]{1,0:T(8,128)(2,1)S(1)}, f32[8,4,256]{2,1,0:T(4,128)S(1)}) custom-call(s32[24]{0:T(128)S(1)} %get-tuple-element.183.sc, bf16[2048,256]{1,0:T(8,128)(2,1)S(1)} %get-tuple-element.85.refs_0_, bf16[2048,256]{1,0:T(8,128)(2,1)S(1)} %get-tuple-element.86.refs_1_.refs_5_, ...), custom_call_target="tpu_custom_call" | custom-call | flops 1073741824 | bytes 4194304 | tf_op jit(solution)/shard_map/pallas_call | solution.py:136
  31.1 3.6 %shard_map.231 = (bf16[1024,512]{1,0:T(8,128)(2,1)S(1)}, f32[1024,512]{1,0:T(8,128)S(1)}, f32[1024,1]{1,0:T(8,128)S(1)}, bf16[1024,256]{1,0:T(8,128)(2,1)S(1)}, bf16[1024,256]{1,0:T(8,128)(2,1)}) custom-call(s32[1]{0:T(128)} %bitcast.3.sc, bf16[2048,512]{1,0:T(8,128)(2,1)S(1)} %copy-done.1, bf16[1024,256]{1,0:T(8,128)(2,1)S(1)} %get-tuple-element.88.refs_1_.refs_3_, ...), custom_call_target="tpu_custom_call" | custom-call | flops 1073741824 | bytes 6291456 | tf_op jit(solution)/shard_map/pallas_call | solution.py:331
  34.8 1.3 copy-done.2
  39.0 1.2 copy-done.23
  40.3 1.2 shard_map.232
  43.1 11.3 %shard_map.233 = (bf16[1024,256]{1,0:T(8,128)(2,1)S(1)}, bf16[1024,256]{1,0:T(8,128)(2,1)}, f32[8,4,256]{2,1,0:T(4,128)S(1)}) custom-call(s32[24]{0:T(128)S(1)} %get-tuple-element.184.sc, bf16[1024,256]{1,0:T(8,128)(2,1)S(1)} %get-tuple-element.90.refs_0_, bf16[1024,256]{1,0:T(8,128)(2,1)} %collective-permute-done.3.refs_1_, ...), custom_call_target="tpu_custom_call" | custom-call | flops 1073741824 | bytes 4194304 | tf_op jit(solution)/shard_map/pallas_call | solution.py:136
  55.9 1.4 copy.51
  57.5 1.2 copy-done.22
  58.7 1.2 copy-done.26
  61.0 17.5 %shard_map.234 = (bf16[1024,512]{1,0:T(8,128)(2,1)}, f32[1024,512]{1,0:T(8,128)S(1)}, bf16[1024,512]{1,0:T(8,128)(2,1)S(1)}, bf16[1024,512]{1,0:T(8,128)(2,1)S(1...) custom-call(bf16[1024,256]{1,0:T(8,128)(2,1)S(1)} %copy-done.32, ...), custom_call_target="tpu_custom_call" | custom-call | flops 9663676416 | bytes 8388608 | tf_op jit(solution)/shard_map/pallas_call | solution.py:429
  78.5 3.0 %convolution_convert_fusion.3 = bf16[1024,512]{1,0:T(8,128)(2,1)S(1)} fusion(bf16[1024,1024]{1,0:T(8,128)(2,1)} %get-tuple-element.100, bf16[1024,512]{1,0:T(8,128)(2,1)S(1)} %get-tuple-element.101), kind=kOutput, calls=%fused_computation.10 | convolution fusion | flops 1074266112 | bytes 4194304 | tf_op jit(solution)/shard_map/dot_general | solution.py:23
  81.5 1.3 convolution_convert_fusion.2
  83.2 1.3 convolution_convert_fusion
  84.7 1.5 convolution_convert_fusion.13
  86.6 1.3 convolution_convert_fusion.1
  89.9 2.7 %collective-permute-start.13 = (bf16[4,144,512]{2,1,0:T(8,128)(2,1)S(1)}, bf16[4,144,512]{2,1,0:T(8,128)(2,1)S(1)}, u32[]{:S(2)}, u32[]{:S(2)}) collective-permute-start(bf16[4,144,512]{2,1,0:T(8,128)(2,1)S(1)} %pad_maximum_fusion.1), channel_id=1, source_target_pairs={{0,2},{2,0},{4,6},{6,4},{8,10},{10,8},{12,14},{14,12},{16,18},{18,... | collective-permute-start | bytes 1769480 | tf_op jit(solution)/shard_map/ppermute | solution.py:677
  92.7 2.6 %collective-permute-start.14 = (bf16[4,144,512]{2,1,0:T(8,128)(2,1)S(1)}, bf16[4,144,512]{2,1,0:T(8,128)(2,1)S(1)}, u32[]{:S(2)}, u32[]{:S(2)}) collective-permute-start(bf16[4,144,512]{2,1,0:T(8,128)(2,1)S(1)} %pad_maximum_fusion.2), channel_id=1, source_target_pairs={{0,4},{2,6},{4,0},{6,2},{8,12},{10,14},{12,8},{14,10},{16,20},{18,... | collective-permute-start | bytes 1769480 | tf_op jit(solution)/shard_map/ppermute | solution.py:677
  95.3 13.7 %shard_map.235 = (bf16[1024,256]{1,0:T(8,128)(2,1)S(1)}, bf16[1024,256]{1,0:T(8,128)(2,1)S(1)}, bf16[1024,256]{1,0:T(8,128)(2,1)S(1)}, bf16[1024,256]{1,0:T(8,128)(2,1)S(1)}) custom-call(s32[24]{0:T(128)S(1)} %get-tuple-element.184.sc, bf16[1024,256]{1,0:T(8,128)(2,1)S(1)} %copy-done.30, bf16[1024,256]{1,0:T(8,128)(2,1)} %collective-permute-done.3.refs_1_, ...), custom_call_target="tpu_custom_call" | custom-call | flops 2684354560 | bytes 6291456 | tf_op jit(solution)/shard_map/pallas_call | solution.py:236
  109.0 1.5 shard_map.239
  113.7 7.6 %collective-permute-done.14 = bf16[4,144,512]{2,1,0:T(8,128)(2,1)S(1)} collective-permute-done((bf16[4,144,512]{2,1,0:T(8,128)(2,1)S(1)}, bf16[4,144,512]{2,1,0:T(8,128)(2,1)S(1)}, u32[]{:S(2)}, u32[]{:S(2)}) %collective-permute-start.14) | collective-permute-done | bytes 589856 | tf_op jit(solution)/shard_map/ppermute | solution.py:677
  122.3 3.5 %shard_map.236 = (f32[1024,512]{1,0:T(8,128)S(1)}, bf16[1024,512]{1,0:T(8,128)(2,1)S(1)}, bf16[1024,256]{1,0:T(8,128)(2,1)S(1)}, bf16[1024,256]{1,0:T(8,128)(2,1)S(1)}, f32[2,512]{1,0:T(2,128)S(1)}) custom-call(bf16[1024,256]{1,0:T(8,128)(2,1)S(1)} %get-tuple-element.118.refs_0_, bf16[1024,256]{1,0:T(8,128)(2,1)S(1)} %collective-permute-done.12.refs_1_, ...), custom_call_target="tpu_custom_call" | custom-call | flops 1 | bytes 1 | tf_op jit(solution)/shard_map/pallas_call | solution.py:485
  129.2 5.7 %collective-permute-start.19 = (bf16[144,512]{1,0:T(8,128)(2,1)S(1)}, bf16[144,512]{1,0:T(8,128)(2,1)S(1)}, u32[]{:S(2)}, u32[]{:S(2)}) collective-permute-start(bf16[144,512]{1,0:T(8,128)(2,1)S(1)} %get-tuple-element.142), channel_id=1, source_target_pairs={{0,8},{2,10},{4,12},{6,14},{8,0},{10,2},{12,4},{14,6},{16,24},{18,... | collective-permute-start | bytes 442376 | tf_op jit(solution)/shard_map/ppermute | solution.py:677
  134.9 2.4 %collective-permute-start.21 = (bf16[144,512]{1,0:T(8,128)(2,1)S(1)}, bf16[144,512]{1,0:T(8,128)(2,1)S(1)}, u32[]{:S(2)}, u32[]{:S(2)}) collective-permute-start(bf16[144,512]{1,0:T(8,128)(2,1)S(1)} %get-tuple-element.144), channel_id=1, source_target_pairs={{0,24},{2,26},{4,28},{6,30},{8,16},{10,18},{12,20},{14,22},{16,8},... | collective-permute-start | bytes 442376 | tf_op jit(solution)/shard_map/ppermute | solution.py:677
  137.3 21.2 %shard_map.237 = (bf16[2048,256]{1,0:T(8,128)(2,1)S(1)}, bf16[2048,256]{1,0:T(8,128)(2,1)S(1)}, bf16[2048,256]{1,0:T(8,128)(2,1)S(1)}) custom-call(s32[24]{0:T(128)S(1)} %get-tuple-element.183.sc, bf16[2048,256]{1,0:T(8,128)(2,1)S(1)} %copy-done.40, bf16[1024,256]{1,0:T(8,128)(2,1)S(1)} %get-tuple-element.126.refs_1_, ...), custom_call_target="tpu_custom_call" | custom-call | flops 2684354560 | bytes 6291456 | tf_op jit(solution)/shard_map/pallas_call | solution.py:236
  161.3 3.0 %shard_map.238 = (f32[1024,512]{1,0:T(8,128)S(1)}, bf16[1024,512]{1,0:T(8,128)(2,1)S(1)}) custom-call(s32[4]{0:T(128)S(1)} %and_select_fusion.sc, bf16[2048,256]{1,0:T(8,128)(2,1)S(1)} %get-tuple-element.131.refs_0_, bf16[2048,256]{1,0:T(8,128)(2,1)S(1)} %get-tuple-element.132.refs_1_, bf16[2048,256]{1,0:T(8,128)(2,1)S(1)} %get-tuple-element.133.refs_2_, ...), custom_call_target="tpu_custom_call" | custom-call | flops 1 | bytes 1 | tf_op jit(solution)/shard_map/pallas_call | solution.py:518
  164.6 56.4 %shard_map.240 = (bf16[1024,512]{1,0:T(8,128)(2,1)S(1)}, bf16[1280,512]{1,0:T(8,128)(2,1)S(1)}, bf16[512,256]{1,0:T(8,128)(2,1)S(1)}, bf16[512,256]{1,0:T(8,128)...) custom-call(bf16[64,512]{1,0:T(8,128)(2,1)S(1)} %slice.70.refs_0_, ...), custom_call_target="tpu_custom_call" | custom-call | tf_op jit(solution)/shard_map/pallas_call | solution.py:649
  221.0 1.3 maximum_convert_fusion
  223.5 1.6 convert_element_type.236
  228.2 1.7 bitcast_convert_fusion
  229.9 1.9 add_add_fusion
  (211 shorter events, 35.1 us)
Async XLA Ops:
  12.5 16.6 %copy-start.4 = (bf16[256,512]{1,0:T(8,128)(2,1)S(1)}, bf16[256,512]{1,0:T(8,128)(2,1)}, u32[]{:S(2)}) copy-start(bf16[256,512]{1,0:T(8,128)(2,1)} %refs_4_.3) | copy-start | bytes 786436
  12.5 16.8 %copy-start.6 = (bf16[512,256]{1,0:T(8,128)(2,1)S(1)}, bf16[512,256]{1,0:T(8,128)(2,1)}, u32[]{:S(2)}) copy-start(bf16[512,256]{1,0:T(8,128)(2,1)} %refs_2_.1) | copy-start | bytes 786436
  12.5 18.6 %copy-start.1 = (bf16[2048,512]{1,0:T(8,128)(2,1)S(1)}, bf16[2048,512]{1,0:T(8,128)(2,1)}, u32[]{:S(2)}) copy-start(bf16[2048,512]{1,0:T(8,128)(2,1)} %refs_0_.1) | copy-start | bytes 6291460
  12.5 18.6 %copy-start.20 = (f32[512,3]{0,1:T(4,128)S(1)}, f32[512,3]{0,1:T(4,128)}, u32[]{:S(2)}) copy-start(f32[512,3]{0,1:T(4,128)} %param.25) | copy-start | bytes 18436
  12.5 18.6 %copy-start.21 = (f32[512,3]{0,1:T(4,128)S(1)}, f32[512,3]{0,1:T(4,128)}, u32[]{:S(2)}) copy-start(f32[512,3]{0,1:T(4,128)} %param.26) | copy-start | bytes 18436
  27.8 3.2 %collective-permute-start = (bf16[1024,256]{1,0:T(8,128)(2,1)S(1)}, bf16[1024,256]{1,0:T(8,128)(2,1)S(1)}, u32[]{:S(2)}, u32[]{:S(2)}) collective-permute-start(bf16[1024,256]{1,0:T(8,128)(2,1)S(1)} %get-tuple-element.89.refs_4_), channel_id=1, source_target_pairs={{0,1},{1,0},{2,3},{3,2},{4,5},{5,4},{6,7},{7,6},{8,9},{9,8},{10,11... | collective-permute-start | bytes 1572872 | tf_op jit(solution)/shard_map/ppermute | solution.py:723
  29.1 1.5 collective-permute-start.1
  29.2 1.8 collective-permute-start.2
  37.9 16.6 %copy-start.29 = (bf16[1024,256]{1,0:T(8,128)(2,1)}, bf16[1024,256]{1,0:T(8,128)(2,1)S(1)}, u32[]{:S(2)}) copy-start(bf16[1024,256]{1,0:T(8,128)(2,1)S(1)} %get-tuple-element.90.refs_0_) | copy-start | bytes 1572868
  37.9 5.2 %collective-permute-start.3 = (bf16[1024,256]{1,0:T(8,128)(2,1)}, bf16[1024,256]{1,0:T(8,128)(2,1)}, u32[]{:S(2)}, u32[]{:S(2)}) collective-permute-start(bf16[1024,256]{1,0:T(8,128)(2,1)} %get-tuple-element.91), channel_id=1, source_target_pairs={{0,1},{1,0},{2,3},{3,2},{4,5},{5,4},{6,7},{7,6},{8,9},{9,8},{10,11... | collective-permute-start | bytes 1572872 | tf_op jit(solution)/shard_map/ppermute | solution.py:723
  38.0 19.5 %collective-permute-start.6 = (bf16[1024,512]{1,0:T(8,128)(2,1)}, bf16[1024,512]{1,0:T(8,128)(2,1)}, u32[]{:S(2)}, u32[]{:S(2)}) collective-permute-start(bf16[1024,512]{1,0:T(8,128)(2,1)} %refs_6_.1), channel_id=1, source_target_pairs={{0,1},{1,0},{2,3},{3,2},{4,5},{5,4},{6,7},{7,6},{8,9},{9,8},{10,11... | collective-permute-start | bytes 3145736 | tf_op jit(solution)/shard_map/ppermute | solution.py:717
  38.4 19.1 %collective-permute-start.7 = (bf16[1024,512]{1,0:T(8,128)(2,1)}, bf16[1024,512]{1,0:T(8,128)(2,1)}, u32[]{:S(2)}, u32[]{:S(2)}) collective-permute-start(bf16[1024,512]{1,0:T(8,128)(2,1)} %refs_8_.1), channel_id=1, source_target_pairs={{0,1},{1,0},{2,3},{3,2},{4,5},{5,4},{6,7},{7,6},{8,9},{9,8},{10,11... | collective-permute-start | bytes 3145736 | tf_op jit(solution)/shard_map/ppermute | solution.py:717
  38.5 18.9 %collective-permute-start.5 = (bf16[256,512]{1,0:T(8,128)(2,1)}, bf16[256,512]{1,0:T(8,128)(2,1)}, u32[]{:S(2)}, u32[]{:S(2)}) collective-permute-start(bf16[256,512]{1,0:T(8,128)(2,1)} %refs_4_.2), channel_id=1, source_target_pairs={{0,1},{1,0},{2,3},{3,2},{4,5},{5,4},{6,7},{7,6},{8,9},{9,8},{10,11... | collective-permute-start | bytes 786440 | tf_op jit(solution)/shard_map/ppermute | solution.py:717
  55.2 2.3 collective-permute-start.4
  82.8 6.3 %collective-permute-start.9 = (bf16[1024,512]{1,0:T(8,128)(2,1)S(1)}, bf16[1024,512]{1,0:T(8,128)(2,1)S(1)}, u32[]{:S(2)}, u32[]{:S(2)}) collective-permute-start(bf16[1024,512]{1,0:T(8,128)(2,1)S(1)} %convolution_convert_fusion.2), channel_id=1, source_target_pairs={{0,1},{1,0},{2,3},{3,2},{4,5},{5,4},{6,7},{7,6},{8,9},{9,8},{10,11... | collective-permute-start | bytes 3145736 | tf_op jit(solution)/shard_map/ppermute | solution.py:723
  84.5 4.1 %collective-permute-start.10 = (bf16[1024,512]{1,0:T(8,128)(2,1)S(1)}, bf16[1024,512]{1,0:T(8,128)(2,1)S(1)}, u32[]{:S(2)}, u32[]{:S(2)}) collective-permute-start(bf16[1024,512]{1,0:T(8,128)(2,1)S(1)} %convolution_convert_fusion), channel_id=1, source_target_pairs={{0,1},{1,0},{2,3},{3,2},{4,5},{5,4},{6,7},{7,6},{8,9},{9,8},{10,11... | collective-permute-start | bytes 3145736 | tf_op jit(solution)/shard_map/ppermute | solution.py:723
  86.2 1.9 collective-permute-start.11
  87.9 2.0 collective-permute-start.8
  89.9 23.8 %collective-permute-start.13 = (bf16[4,144,512]{2,1,0:T(8,128)(2,1)S(1)}, bf16[4,144,512]{2,1,0:T(8,128)(2,1)S(1)}, u32[]{:S(2)}, u32[]{:S(2)}) collective-permute-start(bf16[4,144,512]{2,1,0:T(8,128)(2,1)S(1)} %pad_maximum_fusion.1), channel_id=1, source_target_pairs={{0,2},{2,0},{4,6},{6,4},{8,10},{10,8},{12,14},{14,12},{16,18},{18,... | collective-permute-start | bytes 1769480 | tf_op jit(solution)/shard_map/ppermute | solution.py:677
  92.7 28.7 %collective-permute-start.14 = (bf16[4,144,512]{2,1,0:T(8,128)(2,1)S(1)}, bf16[4,144,512]{2,1,0:T(8,128)(2,1)S(1)}, u32[]{:S(2)}, u32[]{:S(2)}) collective-permute-start(bf16[4,144,512]{2,1,0:T(8,128)(2,1)S(1)} %pad_maximum_fusion.2), channel_id=1, source_target_pairs={{0,4},{2,6},{4,0},{6,2},{8,12},{10,14},{12,8},{14,10},{16,20},{18,... | collective-permute-start | bytes 1769480 | tf_op jit(solution)/shard_map/ppermute | solution.py:677
  95.3 26.1 %collective-permute-start.15 = (bf16[4,144,512]{2,1,0:T(8,128)(2,1)S(1)}, bf16[4,144,512]{2,1,0:T(8,128)(2,1)S(1)}, u32[]{:S(2)}, u32[]{:S(2)}) collective-permute-start(bf16[4,144,512]{2,1,0:T(8,128)(2,1)S(1)} %pad_maximum_fusion.3), channel_id=1, source_target_pairs={{0,6},{2,4},{4,2},{6,0},{8,14},{10,12},{12,10},{14,8},{16,22},{18,... | collective-permute-start | bytes 1769480 | tf_op jit(solution)/shard_map/ppermute | solution.py:677
  95.3 15.4 %copy-start.24 = (bf16[1024,512]{1,0:T(8,128)(2,1)S(1)}, bf16[1024,512]{1,0:T(8,128)(2,1)}, u32[]{:S(2)}) copy-start(bf16[1024,512]{1,0:T(8,128)(2,1)} %x_ref.3) | copy-start | bytes 3145732
  110.6 2.0 collective-permute-start.18
  111.2 10.5 %collective-permute-start.12 = (bf16[1024,256]{1,0:T(8,128)(2,1)S(1)}, bf16[1024,256]{1,0:T(8,128)(2,1)S(1)}, u32[]{:S(2)}, u32[]{:S(2)}) collective-permute-start(bf16[1024,256]{1,0:T(8,128)(2,1)S(1)} %get-tuple-element.113), channel_id=1, source_target_pairs={{0,1},{1,0},{2,3},{3,2},{4,5},{5,4},{6,7},{7,6},{8,9},{9,8},{10,11... | collective-permute-start | bytes 1572872 | tf_op jit(solution)/shard_map/ppermute | solution.py:723
  125.8 1.7 collective-permute-start.24
  125.9 1.7 collective-permute-start.23
  126.8 1.6 collective-permute-start.22
  127.0 2.2 collective-permute-start.16
  129.2 35.3 %collective-permute-start.19 = (bf16[144,512]{1,0:T(8,128)(2,1)S(1)}, bf16[144,512]{1,0:T(8,128)(2,1)S(1)}, u32[]{:S(2)}, u32[]{:S(2)}) collective-permute-start(bf16[144,512]{1,0:T(8,128)(2,1)S(1)} %get-tuple-element.142), channel_id=1, source_target_pairs={{0,8},{2,10},{4,12},{6,14},{8,0},{10,2},{12,4},{14,6},{16,24},{18,... | collective-permute-start | bytes 442376 | tf_op jit(solution)/shard_map/ppermute | solution.py:677
  134.9 29.6 %collective-permute-start.20 = (bf16[144,512]{1,0:T(8,128)(2,1)S(1)}, bf16[144,512]{1,0:T(8,128)(2,1)S(1)}, u32[]{:S(2)}, u32[]{:S(2)}) collective-permute-start(bf16[144,512]{1,0:T(8,128)(2,1)S(1)} %get-tuple-element.143), channel_id=1, source_target_pairs={{0,16},{2,18},{4,20},{6,22},{8,24},{10,26},{12,28},{14,30},{16,0},... | collective-permute-start | bytes 442376 | tf_op jit(solution)/shard_map/ppermute | solution.py:677
  134.9 29.6 %collective-permute-start.21 = (bf16[144,512]{1,0:T(8,128)(2,1)S(1)}, bf16[144,512]{1,0:T(8,128)(2,1)S(1)}, u32[]{:S(2)}, u32[]{:S(2)}) collective-permute-start(bf16[144,512]{1,0:T(8,128)(2,1)S(1)} %get-tuple-element.144), channel_id=1, source_target_pairs={{0,24},{2,26},{4,28},{6,30},{8,16},{10,18},{12,20},{14,22},{16,8},... | collective-permute-start | bytes 442376 | tf_op jit(solution)/shard_map/ppermute | solution.py:677
  164.4 65.5 %collective-permute-start.17 = (bf16[1024,512]{1,0:T(8,128)(2,1)S(1)}, bf16[1024,512]{1,0:T(8,128)(2,1)S(1)}, u32[]{:S(2)}, u32[]{:S(2)}) collective-permute-start(bf16[1024,512]{1,0:T(8,128)(2,1)S(1)} %get-tuple-element.135), channel_id=1, source_target_pairs={{0,1},{1,0},{2,3},{3,2},{4,5},{5,4},{6,7},{7,6},{8,9},{9,8},{10,11... | collective-permute-start | bytes 3145736 | tf_op jit(solution)/shard_map/ppermute | solution.py:723
  (41 other events, 216.1 us)

commit v6 on v5

--- a/solution.py
+++ b/solution.py
@@ -684,6 +684,41 @@
     return total.astype(BF16)
 
 
+def widen_kernel(layout, n, *refs):
+    ins, outs = refs[:n], refs[n:]
+    for out, sources in zip(outs, layout):
+        for c, (i, at, count) in enumerate(sources):
+            block = ins[i][...]
+            if at is not None:
+                block = block[:, at : at + count, :].reshape(-1, block.shape[-1])
+            if len(out.shape) == 3:
+                out[c] = block.astype(F32)
+            else:
+                out[...] = block.astype(F32)
+
+
+def widen(arrays, layout, shapes, steps):
+    def spec(shape):
+        if len(shape) == 2:
+            return pl.BlockSpec((shape[0] // steps, shape[1]), lambda i: (i, 0))
+        return pl.BlockSpec((shape[0], shape[1] // steps, shape[2]), lambda i: (0, i, 0))
+
+    def in_spec(a):
+        if a.ndim == 2:
+            return spec(a.shape)
+        return pl.BlockSpec((a.shape[0] // steps, *a.shape[1:]), lambda i: (i, 0, 0))
+
+    return pl.pallas_call(
+        functools.partial(widen_kernel, layout, len(arrays)),
+        grid=(steps,),
+        in_specs=[in_spec(a) for a in arrays],
+        out_specs=[spec(s) for s in shapes],
+        out_shape=[jax.ShapeDtypeStruct(s, F32) for s in shapes],
+        compiler_params=params(24),
+        cost_estimate=cost(0, sum(math.prod(s) * 6 for s in shapes)),
+    )(*arrays)
+
+
 def shards(
     block_input_slots,
     memory,
@@ -708,7 +743,7 @@
     mem_share = mem_tokens // mp
     width = self_qkv.shape[2]
     me = lax.axis_index("mp")
-    bt = min(256, share)
+    bt = min(512, share)
     bq = min(256, share)
     bk = min(256, mem_tokens)
 
@@ -825,6 +860,8 @@
     (dq,), dk, dv = attend_back(
         self_table, proj[:1], dctx_parts, ctx_parts, proj[1], self_kt, proj[2], self_lo, self_hi, self_lse, mp, bq, bk
     )
+    if hidden:
+        dq, dk, dv, block = lax.optimization_barrier((dq, dk, dv, add_up(blocks)))
     in_bt = min(512, share)
     in_blocks = place.reshape(-1, in_bt)[:, 0] // in_bt
     input_parts = input_part(in_blocks.astype(jnp.int32), [dq, dk, dv], self_qkv, mp, in_bt)
@@ -840,21 +877,38 @@
     late = [*self_qkv_grad, self_out_grad, cross_query_grad, *cross_kv_grad]
     late = [g.astype(BF16) for g in late]
     if hidden:
-        block = add_up(blocks)
         count = early[0].shape[0] // devices
         summed, (up_grad, rest), small = all_sum(
             late, [(block[:count], (0, 1)), (block[count:], (1, 0))], small.astype(BF16), devices
         )
-        up_grad = up_grad.astype(F32)
         rest = rest.reshape(devices, -1, d)
         count = early[1].shape[0] // devices
-        down_grad = rest[:, :count].reshape(early[1].shape).astype(F32)
-        cross_out_grad = rest[:, count:].reshape(early[2].shape).astype(F32)
+        more = early[2].shape[0] // devices
+        late_shapes = [
+            self_qkv.shape,
+            self_out.shape,
+            cross_query.shape,
+            cross_kv.shape,
+        ]
+        *summed, up_grad, down_grad, cross_out_grad = widen(
+            [*summed, up_grad, rest],
+            [
+                [(0, None, 0), (1, None, 0), (2, None, 0)],
+                [(3, None, 0)],
+                [(4, None, 0)],
+                [(5, None, 0), (6, None, 0)],
+                [(7, None, 0)],
+                [(8, 0, count)],
+                [(8, count, more)],
+            ],
+            late_shapes + [g.shape for g in early],
+            8,
+        )
     else:
         summed, _, small = all_sum(late + early, [], small.astype(BF16), devices)
         *summed, up_grad, down_grad, cross_out_grad = [g.astype(F32) for g in summed]
-    dwq, dwk, dwv, self_out_grad, cross_query_grad, dck, dcv = [g.astype(F32) for g in summed]
-    summed = [jnp.stack([dwq, dwk, dwv]), self_out_grad, cross_query_grad, jnp.stack([dck, dcv])]
+        dwq, dwk, dwv, self_out_grad, cross_query_grad, dck, dcv = summed
+        summed = [jnp.stack([dwq, dwk, dwv]), self_out_grad, cross_query_grad, jnp.stack([dck, dcv])]
     summed += [cross_out_grad, up_grad, down_grad]
     small = small.astype(F32).T
     return (layer_output, input_grad, memory_grad, *summed, small[:, :3], small[:, 3:6])

time: 231 us -> 227 us (0.983); the launches traced: 232 us -> 225 us
  Pallas kernels: 151 us -> 160 us
  other arithmetic: 15.9 us -> 7.75 us
  starting transfers between devices: 18.7 us -> 13.5 us
    convert_element_type x5 -> x0, other arithmetic: 5.84 us -> none  [the longest x2 1.68 us: shards(): g.astype(F32)]
    ppermute x6, starting transfers between devices: 13.4 us -> 8.21 us  [scatter_step(): lax.ppermute(b, 'batch', across(r, shift, devices))]
    pallas_call x0 -> x1, Pallas kernels: none -> 4.42 us  [widen(): pl.pallas_call(functools.partial(widen_kernel, layout, len(arrays)), grid...]
    pallas_call x1, Pallas kernels: 56.4 us -> 59.6 us  [all_sum(): pl.pallas_call(functools.partial(all_sum_kernel, plan, nbits, len(plan)),...]
  transfers between devices with their start and end apart: 25 -> 25, of which waited for: 7 -> 8; matrix products, arithmetic and copies ran while one was open for 10% -> 6% of each run, Pallas kernels for 47% -> 51%
where the time goes in v6:
time: 227 us; the launch traced here: 225 us
  Pallas kernels  160 us (70%)
  local copies, waits for them, and re-layouts  19.4 us (9%)
  matrix products  14.5 us (6%)
  starting transfers between devices  13.5 us (6%)
  waiting for transfers between devices  8.12 us (4%)
  other arithmetic  7.75 us (3%)
    pallas_call x1, Pallas kernels, all_sum(): pl.pallas_call(functools.partial(all_sum_kernel, plan, nbits, len(plan)),...  59.6 us
    pallas_call x2, Pallas kernels, attend_back(): pl.pallas_call(functools.partial(attend_back_kernel, nblk, per_part, len(...  36.6 us
    pallas_call x2, Pallas kernels, attend(): pl.pallas_call(functools.partial(attend_kernel, nblk, per_part, len(q_par...  27.7 us
    pallas_call x1, Pallas kernels, middle(): pl.pallas_call(functools.partial(middle_kernel, mp), grid=(share // bt,),...  17.5 us
    unnamed x98, local copies, waits for them, and re-layouts  15.9 us
    dot_general x15, matrix products, mm(): return lax.dot_general(a, b, dims, preferred_element_type=F32)  14.5 us
    ppermute x6, starting transfers between devices, scatter_step(): lax.ppermute(b, 'batch', across(r, shift, devices))  8.21 us
    ppermute x6, waiting for transfers between devices, scatter_step(): lax.ppermute(b, 'batch', across(r, shift, devices))  5.56 us
  transfers between devices with their start and end apart: 25, of which 8 were waited for; matrix products, arithmetic and copies ran while one was open for 6% of the time, Pallas kernels for 51%

profile of v6, /device:TPU:0, one launch (start us, length us, event | category | flops | bytes accessed | tf_op | source)
XLA Modules:
  0.0 225.1 jit_solution(11856011311783059323)
XLA Ops:
  4.8 1.6 copy-done
  6.4 1.1 copy-done.12
  7.5 2.9 %shard_map.229 = (bf16[2048,256]{1,0:T(8,128)(2,1)S(1)}, bf16[2048,256]{1,0:T(8,128)(2,1)S(1)}, bf16[2048,256]{1,0:T(8,128)(2,1)S(1)}, bf16[256,2048]{1,0:T(8,128)(2,1)S(1)}, bf16[256,2048]{1,0:T(8,128)(2,1)S(1)}) custom-call(bf16[2048,512]{1,0:T(8,128)(2,1)S(1)} %copy-done, bf16[3,512,256]{2,1,0:T(8,128)(2,1)S(1)} %copy-done.12), custom_call_target="tpu_custom_call" | custom-call | flops 1610612736 | bytes 8388608 | tf_op jit(solution)/shard_map/pallas_call | solution.py:288
  12.5 15.2 %shard_map.230 = (bf16[1024,256]{1,0:T(8,128)(2,1)S(1)}, bf16[1024,256]{1,0:T(8,128)(2,1)S(1)}, f32[8,4,256]{2,1,0:T(4,128)S(1)}) custom-call(s32[24]{0:T(128)S(1)} %get-tuple-element.205.sc, bf16[2048,256]{1,0:T(8,128)(2,1)S(1)} %get-tuple-element.96.refs_0_, bf16[2048,256]{1,0:T(8,128)(2,1)S(1)} %get-tuple-element.97.refs_1_.refs_5_, ...), custom_call_target="tpu_custom_call" | custom-call | flops 1073741824 | bytes 4194304 | tf_op jit(solution)/shard_map/pallas_call | solution.py:136
  31.1 2.9 %shard_map.231 = (bf16[1024,512]{1,0:T(8,128)(2,1)S(1)}, f32[1024,512]{1,0:T(8,128)S(1)}, f32[1024,1]{1,0:T(8,128)S(1)}, bf16[1024,256]{1,0:T(8,128)(2,1)S(1)}, bf16[1024,256]{1,0:T(8,128)(2,1)}) custom-call(s32[1]{0:T(128)} %bitcast.3.sc, bf16[2048,512]{1,0:T(8,128)(2,1)S(1)} %copy-done.1, bf16[1024,256]{1,0:T(8,128)(2,1)S(1)} %get-tuple-element.99.refs_1_.refs_3_, ...), custom_call_target="tpu_custom_call" | custom-call | flops 1073741824 | bytes 6291456 | tf_op jit(solution)/shard_map/pallas_call | solution.py:331
  34.0 1.3 copy-done.2
  38.2 1.2 copy-done.23
  39.5 1.2 shard_map.232
  42.3 12.5 %shard_map.233 = (bf16[1024,256]{1,0:T(8,128)(2,1)S(1)}, bf16[1024,256]{1,0:T(8,128)(2,1)}, f32[8,4,256]{2,1,0:T(4,128)S(1)}) custom-call(s32[24]{0:T(128)S(1)} %get-tuple-element.206.sc, bf16[1024,256]{1,0:T(8,128)(2,1)S(1)} %get-tuple-element.101.refs_0_, bf16[1024,256]{1,0:T(8,128)(2,1)} %collective-permute-done.3.refs_1_, ...), custom_call_target="tpu_custom_call" | custom-call | flops 1073741824 | bytes 4194304 | tf_op jit(solution)/shard_map/pallas_call | solution.py:136
  56.3 1.4 copy.51
  57.8 1.2 copy-done.22
  59.1 1.2 copy-done.26
  61.3 17.5 %shard_map.234 = (bf16[1024,512]{1,0:T(8,128)(2,1)}, f32[1024,512]{1,0:T(8,128)S(1)}, bf16[1024,512]{1,0:T(8,128)(2,1)S(1)}, bf16[1024,512]{1,0:T(8,128)(2,1)S(1...) custom-call(bf16[1024,256]{1,0:T(8,128)(2,1)S(1)} %copy-done.32, ...), custom_call_target="tpu_custom_call" | custom-call | flops 9663676416 | bytes 8388608 | tf_op jit(solution)/shard_map/pallas_call | solution.py:429
  78.8 3.0 %convolution_convert_fusion.3 = bf16[1024,512]{1,0:T(8,128)(2,1)S(1)} fusion(bf16[1024,1024]{1,0:T(8,128)(2,1)} %get-tuple-element.111, bf16[1024,512]{1,0:T(8,128)(2,1)S(1)} %get-tuple-element.112), kind=kOutput, calls=%fused_computation.10 | convolution fusion | flops 1074266112 | bytes 4194304 | tf_op jit(solution)/shard_map/dot_general | solution.py:23
  81.9 1.3 convolution_convert_fusion.2
  83.6 1.3 convolution_convert_fusion
  85.1 1.5 convolution_convert_fusion.13
  87.0 1.3 convolution_convert_fusion.1
  91.3 1.5 collective-permute-start.14
  93.8 15.4 %shard_map.235 = (bf16[1024,256]{1,0:T(8,128)(2,1)S(1)}, bf16[1024,256]{1,0:T(8,128)(2,1)S(1)}, bf16[1024,256]{1,0:T(8,128)(2,1)S(1)}, bf16[1024,256]{1,0:T(8,128)(2,1)S(1)}) custom-call(s32[24]{0:T(128)S(1)} %get-tuple-element.206.sc, bf16[1024,256]{1,0:T(8,128)(2,1)S(1)} %copy-done.30, bf16[1024,256]{1,0:T(8,128)(2,1)} %collective-permute-done.3.refs_1_, ...), custom_call_target="tpu_custom_call" | custom-call | flops 2684354560 | bytes 6291456 | tf_op jit(solution)/shard_map/pallas_call | solution.py:236
  109.2 1.5 shard_map.239
  112.7 1.1 convert_add_fusion
  113.9 4.3 %collective-permute-done.14 = bf16[4,144,512]{2,1,0:T(8,128)(2,1)S(1)} collective-permute-done((bf16[4,144,512]{2,1,0:T(8,128)(2,1)S(1)}, bf16[4,144,512]{2,1,0:T(8,128)(2,1)S(1)}, u32[]{:S(2)}, u32[]{:S(2)}) %collective-permute-start.14) | collective-permute-done | bytes 589856 | tf_op jit(solution)/shard_map/ppermute | solution.py:677
  118.2 1.3 collective-permute-done.15
  120.3 2.7 %shard_map.236 = (f32[1024,512]{1,0:T(8,128)S(1)}, bf16[1024,512]{1,0:T(8,128)(2,1)S(1)}, bf16[1024,256]{1,0:T(8,128)(2,1)S(1)}, bf16[1024,256]{1,0:T(8,128)(2,1)S(1)}, f32[2,512]{1,0:T(2,128)S(1)}) custom-call(bf16[1024,256]{1,0:T(8,128)(2,1)S(1)} %get-tuple-element.129.refs_0_, bf16[1024,256]{1,0:T(8,128)(2,1)S(1)} %collective-permute-done.12.refs_1_, ...), custom_call_target="tpu_custom_call" | custom-call | flops 1 | bytes 1 | tf_op jit(solution)/shard_map/pallas_call | solution.py:485
  126.5 1.6 collective-permute-start.17
  128.1 3.1 %collective-permute-start.18 = (bf16[144,512]{1,0:T(8,128)(2,1)S(1)}, bf16[144,512]{1,0:T(8,128)(2,1)S(1)}, u32[]{:S(2)}, u32[]{:S(2)}) collective-permute-start(bf16[144,512]{1,0:T(8,128)(2,1)S(1)} %get-tuple-element.147), channel_id=1, source_target_pairs={{0,16},{2,18},{4,20},{6,22},{8,24},{10,26},{12,28},{14,30},{16,0},... | collective-permute-start | bytes 442376 | tf_op jit(solution)/shard_map/ppermute | solution.py:677
  131.3 21.2 %shard_map.237 = (bf16[2048,256]{1,0:T(8,128)(2,1)S(1)}, bf16[2048,256]{1,0:T(8,128)(2,1)S(1)}, bf16[2048,256]{1,0:T(8,128)(2,1)S(1)}) custom-call(s32[24]{0:T(128)S(1)} %get-tuple-element.205.sc, bf16[2048,256]{1,0:T(8,128)(2,1)S(1)} %copy-done.40, bf16[1024,256]{1,0:T(8,128)(2,1)S(1)} %get-tuple-element.137.refs_1_, ...), custom_call_target="tpu_custom_call" | custom-call | flops 2684354560 | bytes 6291456 | tf_op jit(solution)/shard_map/pallas_call | solution.py:236
  153.6 3.0 %shard_map.238 = (f32[1024,512]{1,0:T(8,128)S(1)}, bf16[1024,512]{1,0:T(8,128)(2,1)S(1)}) custom-call(s32[4]{0:T(128)S(1)} %and_select_fusion.sc, bf16[2048,256]{1,0:T(8,128)(2,1)S(1)} %get-tuple-element.149.refs_0_, bf16[2048,256]{1,0:T(8,128)(2,1)S(1)} %get-tuple-element.150.refs_1_, bf16[2048,256]{1,0:T(8,128)(2,1)S(1)} %get-tuple-element.151.refs_2_, ...), custom_call_target="tpu_custom_call" | custom-call | flops 1 | bytes 1 | tf_op jit(solution)/shard_map/pallas_call | solution.py:518
  158.6 59.6 %shard_map.240 = (bf16[1024,512]{1,0:T(8,128)(2,1)S(1)}, bf16[1280,512]{1,0:T(8,128)(2,1)S(1)}, bf16[512,256]{1,0:T(8,128)(2,1)S(1)}, bf16[512,256]{1,0:T(8,128)...) custom-call(bf16[64,512]{1,0:T(8,128)(2,1)S(1)} %slice.48.refs_0_, ...), custom_call_target="tpu_custom_call" | custom-call | tf_op jit(solution)/shard_map/pallas_call | solution.py:649
  218.2 4.4 %shard_map.241 = (f32[3,512,256]{2,1,0:T(8,128)}, f32[256,512]{1,0:T(8,128)}, f32[512,256]{1,0:T(8,128)}, f32[2,512,256]{2,1,0:T(8,128)}, f32[1024,512]{1,0:T(8,...) custom-call(bf16[512,256]{1,0:T(8,128)(2,1)S(1)} %get-tuple-element.163.refs_0_, ...), custom_call_target="tpu_custom_call" | custom-call | bytes 12582912 | tf_op jit(solution)/shard_map/pallas_call | solution.py:711
  223.2 1.9 add_add_fusion
  (203 shorter events, 31.1 us)
Async XLA Ops:
  12.5 16.6 %copy-start.4 = (bf16[256,512]{1,0:T(8,128)(2,1)S(1)}, bf16[256,512]{1,0:T(8,128)(2,1)}, u32[]{:S(2)}) copy-start(bf16[256,512]{1,0:T(8,128)(2,1)} %refs_4_.3) | copy-start | bytes 786436
  12.5 16.7 %copy-start.6 = (bf16[512,256]{1,0:T(8,128)(2,1)S(1)}, bf16[512,256]{1,0:T(8,128)(2,1)}, u32[]{:S(2)}) copy-start(bf16[512,256]{1,0:T(8,128)(2,1)} %refs_2_.1) | copy-start | bytes 786436
  12.5 18.6 %copy-start.1 = (bf16[2048,512]{1,0:T(8,128)(2,1)S(1)}, bf16[2048,512]{1,0:T(8,128)(2,1)}, u32[]{:S(2)}) copy-start(bf16[2048,512]{1,0:T(8,128)(2,1)} %refs_0_.1) | copy-start | bytes 6291460
  12.5 18.6 %copy-start.20 = (f32[512,3]{0,1:T(4,128)S(1)}, f32[512,3]{0,1:T(4,128)}, u32[]{:S(2)}) copy-start(f32[512,3]{0,1:T(4,128)} %param.25) | copy-start | bytes 18436
  12.5 18.6 %copy-start.21 = (f32[512,3]{0,1:T(4,128)S(1)}, f32[512,3]{0,1:T(4,128)}, u32[]{:S(2)}) copy-start(f32[512,3]{0,1:T(4,128)} %param.26) | copy-start | bytes 18436
  27.8 3.3 %collective-permute-start = (bf16[1024,256]{1,0:T(8,128)(2,1)S(1)}, bf16[1024,256]{1,0:T(8,128)(2,1)S(1)}, u32[]{:S(2)}, u32[]{:S(2)}) collective-permute-start(bf16[1024,256]{1,0:T(8,128)(2,1)S(1)} %get-tuple-element.100.refs_4_), channel_id=1, source_target_pairs={{0,1},{1,0},{2,3},{3,2},{4,5},{5,4},{6,7},{7,6},{8,9},{9,8},{10,11... | collective-permute-start | bytes 1572872 | tf_op jit(solution)/shard_map/ppermute | solution.py:758
  29.1 1.5 collective-permute-start.1
  29.2 1.8 collective-permute-start.2
  37.1 17.7 %copy-start.29 = (bf16[1024,256]{1,0:T(8,128)(2,1)}, bf16[1024,256]{1,0:T(8,128)(2,1)S(1)}, u32[]{:S(2)}) copy-start(bf16[1024,256]{1,0:T(8,128)(2,1)S(1)} %get-tuple-element.101.refs_0_) | copy-start | bytes 1572868
  37.1 5.2 %collective-permute-start.3 = (bf16[1024,256]{1,0:T(8,128)(2,1)}, bf16[1024,256]{1,0:T(8,128)(2,1)}, u32[]{:S(2)}, u32[]{:S(2)}) collective-permute-start(bf16[1024,256]{1,0:T(8,128)(2,1)} %get-tuple-element.102), channel_id=1, source_target_pairs={{0,1},{1,0},{2,3},{3,2},{4,5},{5,4},{6,7},{7,6},{8,9},{9,8},{10,11... | collective-permute-start | bytes 1572872 | tf_op jit(solution)/shard_map/ppermute | solution.py:758
  37.2 20.6 %collective-permute-start.6 = (bf16[1024,512]{1,0:T(8,128)(2,1)}, bf16[1024,512]{1,0:T(8,128)(2,1)}, u32[]{:S(2)}, u32[]{:S(2)}) collective-permute-start(bf16[1024,512]{1,0:T(8,128)(2,1)} %refs_6_.1), channel_id=1, source_target_pairs={{0,1},{1,0},{2,3},{3,2},{4,5},{5,4},{6,7},{7,6},{8,9},{9,8},{10,11... | collective-permute-start | bytes 3145736 | tf_op jit(solution)/shard_map/ppermute | solution.py:752
  37.6 20.2 %collective-permute-start.7 = (bf16[1024,512]{1,0:T(8,128)(2,1)}, bf16[1024,512]{1,0:T(8,128)(2,1)}, u32[]{:S(2)}, u32[]{:S(2)}) collective-permute-start(bf16[1024,512]{1,0:T(8,128)(2,1)} %refs_8_.1), channel_id=1, source_target_pairs={{0,1},{1,0},{2,3},{3,2},{4,5},{5,4},{6,7},{7,6},{8,9},{9,8},{10,11... | collective-permute-start | bytes 3145736 | tf_op jit(solution)/shard_map/ppermute | solution.py:752
  37.7 20.1 %collective-permute-start.5 = (bf16[256,512]{1,0:T(8,128)(2,1)}, bf16[256,512]{1,0:T(8,128)(2,1)}, u32[]{:S(2)}, u32[]{:S(2)}) collective-permute-start(bf16[256,512]{1,0:T(8,128)(2,1)} %refs_4_.2), channel_id=1, source_target_pairs={{0,1},{1,0},{2,3},{3,2},{4,5},{5,4},{6,7},{7,6},{8,9},{9,8},{10,11... | collective-permute-start | bytes 786440 | tf_op jit(solution)/shard_map/ppermute | solution.py:752
  55.6 2.3 %collective-permute-start.4 = (bf16[1024,256]{1,0:T(8,128)(2,1)}, bf16[1024,256]{1,0:T(8,128)(2,1)}, u32[]{:S(2)}, u32[]{:S(2)}) collective-permute-start(bf16[1024,256]{1,0:T(8,128)(2,1)} %get-tuple-element.106.refs_5_), channel_id=1, source_target_pairs={{0,1},{1,0},{2,3},{3,2},{4,5},{5,4},{6,7},{7,6},{8,9},{9,8},{10,11... | collective-permute-start | bytes 1572872 | tf_op jit(solution)/shard_map/ppermute | solution.py:758
  83.1 6.3 %collective-permute-start.9 = (bf16[1024,512]{1,0:T(8,128)(2,1)S(1)}, bf16[1024,512]{1,0:T(8,128)(2,1)S(1)}, u32[]{:S(2)}, u32[]{:S(2)}) collective-permute-start(bf16[1024,512]{1,0:T(8,128)(2,1)S(1)} %convolution_convert_fusion.2), channel_id=1, source_target_pairs={{0,1},{1,0},{2,3},{3,2},{4,5},{5,4},{6,7},{7,6},{8,9},{9,8},{10,11... | collective-permute-start | bytes 3145736 | tf_op jit(solution)/shard_map/ppermute | solution.py:758
  84.8 4.1 %collective-permute-start.10 = (bf16[1024,512]{1,0:T(8,128)(2,1)S(1)}, bf16[1024,512]{1,0:T(8,128)(2,1)S(1)}, u32[]{:S(2)}, u32[]{:S(2)}) collective-permute-start(bf16[1024,512]{1,0:T(8,128)(2,1)S(1)} %convolution_convert_fusion), channel_id=1, source_target_pairs={{0,1},{1,0},{2,3},{3,2},{4,5},{5,4},{6,7},{7,6},{8,9},{9,8},{10,11... | collective-permute-start | bytes 3145736 | tf_op jit(solution)/shard_map/ppermute | solution.py:758
  86.6 1.9 collective-permute-start.11
  88.3 2.0 collective-permute-start.8
  90.2 23.6 %collective-permute-start.13 = (bf16[4,144,512]{2,1,0:T(8,128)(2,1)S(1)}, bf16[4,144,512]{2,1,0:T(8,128)(2,1)S(1)}, u32[]{:S(2)}, u32[]{:S(2)}) collective-permute-start(bf16[4,144,512]{2,1,0:T(8,128)(2,1)S(1)} %pad_maximum_fusion.1), channel_id=1, source_target_pairs={{0,2},{2,0},{4,6},{6,4},{8,10},{10,8},{12,14},{14,12},{16,18},{18,... | collective-permute-start | bytes 1769480 | tf_op jit(solution)/shard_map/ppermute | solution.py:677
  91.3 26.9 %collective-permute-start.14 = (bf16[4,144,512]{2,1,0:T(8,128)(2,1)S(1)}, bf16[4,144,512]{2,1,0:T(8,128)(2,1)S(1)}, u32[]{:S(2)}, u32[]{:S(2)}) collective-permute-start(bf16[4,144,512]{2,1,0:T(8,128)(2,1)S(1)} %pad_maximum_fusion.2), channel_id=1, source_target_pairs={{0,4},{2,6},{4,0},{6,2},{8,12},{10,14},{12,8},{14,10},{16,20},{18,... | collective-permute-start | bytes 1769480 | tf_op jit(solution)/shard_map/ppermute | solution.py:677
  92.8 26.6 %collective-permute-start.15 = (bf16[4,144,512]{2,1,0:T(8,128)(2,1)S(1)}, bf16[4,144,512]{2,1,0:T(8,128)(2,1)S(1)}, u32[]{:S(2)}, u32[]{:S(2)}) collective-permute-start(bf16[4,144,512]{2,1,0:T(8,128)(2,1)S(1)} %pad_maximum_fusion.3), channel_id=1, source_target_pairs={{0,6},{2,4},{4,2},{6,0},{8,14},{10,12},{12,10},{14,8},{16,22},{18,... | collective-permute-start | bytes 1769480 | tf_op jit(solution)/shard_map/ppermute | solution.py:677
  93.7 17.1 %copy-start.24 = (bf16[1024,512]{1,0:T(8,128)(2,1)S(1)}, bf16[1024,512]{1,0:T(8,128)(2,1)}, u32[]{:S(2)}) copy-start(bf16[1024,512]{1,0:T(8,128)(2,1)} %x_ref.3) | copy-start | bytes 3145732
  110.7 2.0 collective-permute-start.21
  111.4 8.4 %collective-permute-start.12 = (bf16[1024,256]{1,0:T(8,128)(2,1)S(1)}, bf16[1024,256]{1,0:T(8,128)(2,1)S(1)}, u32[]{:S(2)}, u32[]{:S(2)}) collective-permute-start(bf16[1024,256]{1,0:T(8,128)(2,1)S(1)} %get-tuple-element.124), channel_id=1, source_target_pairs={{0,1},{1,0},{2,3},{3,2},{4,5},{5,4},{6,7},{7,6},{8,9},{9,8},{10,11... | collective-permute-start | bytes 1572872 | tf_op jit(solution)/shard_map/ppermute | solution.py:758
  123.1 1.7 collective-permute-start.24
  123.2 1.7 collective-permute-start.23
  124.1 1.6 collective-permute-start.22
  124.3 2.2 collective-permute-start.16
  126.5 26.0 %collective-permute-start.17 = (bf16[144,512]{1,0:T(8,128)(2,1)S(1)}, bf16[144,512]{1,0:T(8,128)(2,1)S(1)}, u32[]{:S(2)}, u32[]{:S(2)}) collective-permute-start(bf16[144,512]{1,0:T(8,128)(2,1)S(1)} %get-tuple-element.146), channel_id=1, source_target_pairs={{0,8},{2,10},{4,12},{6,14},{8,0},{10,2},{12,4},{14,6},{16,24},{18,... | collective-permute-start | bytes 442376 | tf_op jit(solution)/shard_map/ppermute | solution.py:677
  128.1 24.4 %collective-permute-start.18 = (bf16[144,512]{1,0:T(8,128)(2,1)S(1)}, bf16[144,512]{1,0:T(8,128)(2,1)S(1)}, u32[]{:S(2)}, u32[]{:S(2)}) collective-permute-start(bf16[144,512]{1,0:T(8,128)(2,1)S(1)} %get-tuple-element.147), channel_id=1, source_target_pairs={{0,16},{2,18},{4,20},{6,22},{8,24},{10,26},{12,28},{14,30},{16,0},... | collective-permute-start | bytes 442376 | tf_op jit(solution)/shard_map/ppermute | solution.py:677
  131.2 21.3 %collective-permute-start.19 = (bf16[144,512]{1,0:T(8,128)(2,1)S(1)}, bf16[144,512]{1,0:T(8,128)(2,1)S(1)}, u32[]{:S(2)}, u32[]{:S(2)}) collective-permute-start(bf16[144,512]{1,0:T(8,128)(2,1)S(1)} %get-tuple-element.148), channel_id=1, source_target_pairs={{0,24},{2,26},{4,28},{6,30},{8,16},{10,18},{12,20},{14,22},{16,8},... | collective-permute-start | bytes 442376 | tf_op jit(solution)/shard_map/ppermute | solution.py:677
  156.6 66.6 %collective-permute-start.20 = (bf16[1024,512]{1,0:T(8,128)(2,1)S(1)}, bf16[1024,512]{1,0:T(8,128)(2,1)S(1)}, u32[]{:S(2)}, u32[]{:S(2)}) collective-permute-start(bf16[1024,512]{1,0:T(8,128)(2,1)S(1)} %get-tuple-element.153), channel_id=1, source_target_pairs={{0,1},{1,0},{2,3},{3,2},{4,5},{5,4},{6,7},{7,6},{8,9},{9,8},{10,11... | collective-permute-start | bytes 3145736 | tf_op jit(solution)/shard_map/ppermute | solution.py:758
  (41 other events, 175.6 us)

commit v7 on v6

--- a/solution.py
+++ b/solution.py
@@ -684,8 +684,12 @@
     return total.astype(BF16)
 
 
-def widen_kernel(layout, n, *refs):
-    ins, outs = refs[:n], refs[n:]
+def widen_kernel(layout, n, terms, *refs):
+    ins, adds, outs, total_ref = refs[:n], refs[n : n + terms], refs[n + terms : -1], refs[-1]
+    total = adds[0][...].astype(F32)
+    for r in range(1, terms):
+        total += adds[r][...].astype(F32)
+    total_ref[...] = total
     for out, sources in zip(outs, layout):
         for c, (i, at, count) in enumerate(sources):
             block = ins[i][...]
@@ -697,7 +701,7 @@
                 out[...] = block.astype(F32)
 
 
-def widen(arrays, layout, shapes, steps):
+def widen(arrays, layout, shapes, adds, steps):
     def spec(shape):
         if len(shape) == 2:
             return pl.BlockSpec((shape[0] // steps, shape[1]), lambda i: (i, 0))
@@ -709,14 +713,14 @@
         return pl.BlockSpec((a.shape[0] // steps, *a.shape[1:]), lambda i: (i, 0, 0))
 
     return pl.pallas_call(
-        functools.partial(widen_kernel, layout, len(arrays)),
+        functools.partial(widen_kernel, layout, len(arrays), len(adds)),
         grid=(steps,),
-        in_specs=[in_spec(a) for a in arrays],
-        out_specs=[spec(s) for s in shapes],
-        out_shape=[jax.ShapeDtypeStruct(s, F32) for s in shapes],
+        in_specs=[in_spec(a) for a in (*arrays, *adds)],
+        out_specs=[spec(s) for s in (*shapes, adds[0].shape)],
+        out_shape=[jax.ShapeDtypeStruct(s, F32) for s in (*shapes, adds[0].shape)],
         compiler_params=params(24),
         cost_estimate=cost(0, sum(math.prod(s) * 6 for s in shapes)),
-    )(*arrays)
+    )(*arrays, *adds)
 
 
 def shards(
@@ -865,7 +869,6 @@
     in_bt = min(512, share)
     in_blocks = place.reshape(-1, in_bt)[:, 0] // in_bt
     input_parts = input_part(in_blocks.astype(jnp.int32), [dq, dk, dv], self_qkv, mp, in_bt)
-    input_grad = collect(input_parts) + da1
     self_qkv_grad = [mm(block_input_slots, g, TN) for g in (dq, dk, dv)]
 
     small = jnp.concatenate([small1[:1], small23[:2], small1[1:], small23[2:]], axis=0)
@@ -890,7 +893,7 @@
             cross_query.shape,
             cross_kv.shape,
         ]
-        *summed, up_grad, down_grad, cross_out_grad = widen(
+        *summed, up_grad, down_grad, cross_out_grad, input_grad = widen(
             [*summed, up_grad, rest],
             [
                 [(0, None, 0), (1, None, 0), (2, None, 0)],
@@ -902,9 +905,11 @@
                 [(8, count, more)],
             ],
             late_shapes + [g.shape for g in early],
+            [da1, *exchange(input_parts)],
             8,
         )
     else:
+        input_grad = collect(input_parts) + da1
         summed, _, small = all_sum(late + early, [], small.astype(BF16), devices)
         *summed, up_grad, down_grad, cross_out_grad = [g.astype(F32) for g in summed]
         dwq, dwk, dwv, self_out_grad, cross_query_grad, dck, dcv = summed

time: 227 us -> 244 us (1.075)
  waiting for transfers between devices: 8.12 us -> 26.1 us
  starting transfers between devices: 13.5 us -> 16.7 us
  Pallas kernels: 160 us -> 157 us
    ppermute x6, waiting for transfers between devices: 5.56 us -> 23.9 us  [scatter_step(): lax.ppermute(b, 'batch', across(r, shift, devices))]
    ppermute x6, starting transfers between devices: 8.21 us -> 11.4 us  [scatter_step(): lax.ppermute(b, 'batch', across(r, shift, devices))]
  transfers between devices with their start and end apart: 25 -> 25, of which waited for: 8 -> 7; matrix products, arithmetic and copies ran while one was open for 6% -> 6% of each run, Pallas kernels for 51% -> 38%
where the time goes in v7:
time: 244 us; the launch traced here: 242 us
  Pallas kernels  157 us (64%)
  waiting for transfers between devices  26.1 us (11%)
  local copies, waits for them, and re-layouts  20.5 us (8%)
  starting transfers between devices  16.7 us (7%)
  matrix products  14.5 us (6%)
  other arithmetic  5.86 us (2%)
    pallas_call x1, Pallas kernels, all_sum(): pl.pallas_call(functools.partial(all_sum_kernel, plan, nbits, len(plan)),...  58.6 us
    pallas_call x2, Pallas kernels, attend_back(): pl.pallas_call(functools.partial(attend_back_kernel, nblk, per_part, len(...  34.9 us
    pallas_call x2, Pallas kernels, attend(): pl.pallas_call(functools.partial(attend_kernel, nblk, per_part, len(q_par...  26.6 us
    ppermute x6, waiting for transfers between devices, scatter_step(): lax.ppermute(b, 'batch', across(r, shift, devices))  23.9 us
    pallas_call x1, Pallas kernels, middle(): pl.pallas_call(functools.partial(middle_kernel, mp), grid=(share // bt,),...  17.5 us
    unnamed x98, local copies, waits for them, and re-layouts  17 us
    dot_general x15, matrix products, mm(): return lax.dot_general(a, b, dims, preferred_element_type=F32)  14.5 us
    ppermute x6, starting transfers between devices, scatter_step(): lax.ppermute(b, 'batch', across(r, shift, devices))  11.4 us
  transfers between devices with their start and end apart: 25, of which 7 were waited for; matrix products, arithmetic and copies ran while one was open for 6% of the time, Pallas kernels for 38%

profile of v7, /device:TPU:0, one launch (start us, length us, event | category | flops | bytes accessed | tf_op | source)
XLA Modules:
  0.0 242.1 jit_solution(8235218675249212023)
XLA Ops:
  4.8 1.6 copy-done
  6.4 1.1 copy-done.12
  7.5 2.9 %shard_map.229 = (bf16[2048,256]{1,0:T(8,128)(2,1)S(1)}, bf16[2048,256]{1,0:T(8,128)(2,1)S(1)}, bf16[2048,256]{1,0:T(8,128)(2,1)S(1)}, bf16[256,2048]{1,0:T(8,128)(2,1)S(1)}, bf16[256,2048]{1,0:T(8,128)(2,1)S(1)}) custom-call(bf16[2048,512]{1,0:T(8,128)(2,1)S(1)} %copy-done, bf16[3,512,256]{2,1,0:T(8,128)(2,1)S(1)} %copy-done.12), custom_call_target="tpu_custom_call" | custom-call | flops 1610612736 | bytes 8388608 | tf_op jit(solution)/shard_map/pallas_call | solution.py:288
  12.5 15.2 %shard_map.230 = (bf16[1024,256]{1,0:T(8,128)(2,1)S(1)}, bf16[1024,256]{1,0:T(8,128)(2,1)S(1)}, f32[8,4,256]{2,1,0:T(4,128)S(1)}) custom-call(s32[24]{0:T(128)S(1)} %get-tuple-element.207.sc, bf16[2048,256]{1,0:T(8,128)(2,1)S(1)} %get-tuple-element.97.refs_0_, bf16[2048,256]{1,0:T(8,128)(2,1)S(1)} %get-tuple-element.98.refs_1_.refs_5_, ...), custom_call_target="tpu_custom_call" | custom-call | flops 1073741824 | bytes 4194304 | tf_op jit(solution)/shard_map/pallas_call | solution.py:136
  31.1 2.9 %shard_map.231 = (bf16[1024,512]{1,0:T(8,128)(2,1)S(1)}, f32[1024,512]{1,0:T(8,128)S(1)}, f32[1024,1]{1,0:T(8,128)S(1)}, bf16[1024,256]{1,0:T(8,128)(2,1)S(1)}, bf16[1024,256]{1,0:T(8,128)(2,1)}) custom-call(s32[1]{0:T(128)} %bitcast.3.sc, bf16[2048,512]{1,0:T(8,128)(2,1)S(1)} %copy-done.1, bf16[1024,256]{1,0:T(8,128)(2,1)S(1)} %get-tuple-element.100.refs_1_.refs_3_, ...), custom_call_target="tpu_custom_call" | custom-call | flops 1073741824 | bytes 6291456 | tf_op jit(solution)/shard_map/pallas_call | solution.py:331
  34.0 1.3 copy-done.2
  38.3 1.2 copy-done.23
  39.5 1.2 shard_map.232
  42.3 11.3 %shard_map.233 = (bf16[1024,256]{1,0:T(8,128)(2,1)S(1)}, bf16[1024,256]{1,0:T(8,128)(2,1)}, f32[8,4,256]{2,1,0:T(4,128)S(1)}) custom-call(s32[24]{0:T(128)S(1)} %get-tuple-element.208.sc, bf16[1024,256]{1,0:T(8,128)(2,1)S(1)} %get-tuple-element.102.refs_0_, bf16[1024,256]{1,0:T(8,128)(2,1)} %collective-permute-done.3.refs_1_, ...), custom_call_target="tpu_custom_call" | custom-call | flops 1073741824 | bytes 4194304 | tf_op jit(solution)/shard_map/pallas_call | solution.py:136
  55.1 1.4 copy.56
  56.7 1.2 copy-done.22
  57.9 1.2 copy-done.26
  60.2 17.5 %shard_map.234 = (bf16[1024,512]{1,0:T(8,128)(2,1)}, f32[1024,512]{1,0:T(8,128)S(1)}, bf16[1024,512]{1,0:T(8,128)(2,1)S(1)}, bf16[1024,512]{1,0:T(8,128)(2,1)S(1...) custom-call(bf16[1024,256]{1,0:T(8,128)(2,1)S(1)} %copy-done.32, ...), custom_call_target="tpu_custom_call" | custom-call | flops 9663676416 | bytes 8388608 | tf_op jit(solution)/shard_map/pallas_call | solution.py:429
  77.7 3.0 %convolution_convert_fusion.3 = bf16[1024,512]{1,0:T(8,128)(2,1)S(1)} fusion(bf16[1024,1024]{1,0:T(8,128)(2,1)} %get-tuple-element.112, bf16[1024,512]{1,0:T(8,128)(2,1)S(1)} %get-tuple-element.113), kind=kOutput, calls=%fused_computation.9 | convolution fusion | flops 1074266112 | bytes 4194304 | tf_op jit(solution)/shard_map/dot_general | solution.py:23
  80.7 1.3 convolution_convert_fusion.2
  82.4 1.3 convolution_convert_fusion
  83.9 1.5 convolution_convert_fusion.13
  85.9 1.3 convolution_convert_fusion.1
  90.2 13.7 %shard_map.235 = (bf16[1024,256]{1,0:T(8,128)(2,1)S(1)}, bf16[1024,256]{1,0:T(8,128)(2,1)S(1)}, bf16[1024,256]{1,0:T(8,128)(2,1)S(1)}, bf16[1024,256]{1,0:T(8,128)(2,1)S(1)}) custom-call(s32[24]{0:T(128)S(1)} %get-tuple-element.208.sc, bf16[1024,256]{1,0:T(8,128)(2,1)S(1)} %copy-done.30, bf16[1024,256]{1,0:T(8,128)(2,1)} %collective-permute-done.3.refs_1_, ...), custom_call_target="tpu_custom_call" | custom-call | flops 2684354560 | bytes 6291456 | tf_op jit(solution)/shard_map/pallas_call | solution.py:236
  103.9 1.5 shard_map.241
  105.9 2.0 collective-permute-start.13
  108.0 2.1 collective-permute-start.14
  111.2 1.1 convert_add_fusion
  112.4 9.8 %collective-permute-done.13 = bf16[4,144,512]{2,1,0:T(8,128)(2,1)S(1)} collective-permute-done((bf16[4,144,512]{2,1,0:T(8,128)(2,1)S(1)}, bf16[4,144,512]{2,1,0:T(8,128)(2,1)S(1)}, u32[]{:S(2)}, u32[]{:S(2)}) %collective-permute-start.13) | collective-permute-done | bytes 589856 | tf_op jit(solution)/shard_map/ppermute | solution.py:677
  122.1 14.1 %collective-permute-done.14 = bf16[4,144,512]{2,1,0:T(8,128)(2,1)S(1)} collective-permute-done((bf16[4,144,512]{2,1,0:T(8,128)(2,1)S(1)}, bf16[4,144,512]{2,1,0:T(8,128)(2,1)S(1)}, u32[]{:S(2)}, u32[]{:S(2)}) %collective-permute-start.14) | collective-permute-done | bytes 589856 | tf_op jit(solution)/shard_map/ppermute | solution.py:677
  137.1 2.7 %shard_map.236 = (f32[1024,512]{1,0:T(8,128)S(1)}, bf16[1024,512]{1,0:T(8,128)(2,1)S(1)}, bf16[1024,256]{1,0:T(8,128)(2,1)S(1)}, bf16[1024,256]{1,0:T(8,128)(2,1)S(1)}, f32[2,512]{1,0:T(2,128)S(1)}) custom-call(bf16[1024,256]{1,0:T(8,128)(2,1)S(1)} %get-tuple-element.130.refs_0_, bf16[1024,256]{1,0:T(8,128)(2,1)S(1)} %collective-permute-done.12.refs_1_, ...), custom_call_target="tpu_custom_call" | custom-call | flops 1 | bytes 1 | tf_op jit(solution)/shard_map/pallas_call | solution.py:485
  143.2 3.3 %collective-permute-start.17 = (bf16[144,512]{1,0:T(8,128)(2,1)S(1)}, bf16[144,512]{1,0:T(8,128)(2,1)S(1)}, u32[]{:S(2)}, u32[]{:S(2)}) collective-permute-start(bf16[144,512]{1,0:T(8,128)(2,1)S(1)} %get-tuple-element.147), channel_id=1, source_target_pairs={{0,8},{2,10},{4,12},{6,14},{8,0},{10,2},{12,4},{14,6},{16,24},{18,... | collective-permute-start | bytes 442376 | tf_op jit(solution)/shard_map/ppermute | solution.py:677
  146.5 4.0 %collective-permute-start.18 = (bf16[144,512]{1,0:T(8,128)(2,1)S(1)}, bf16[144,512]{1,0:T(8,128)(2,1)S(1)}, u32[]{:S(2)}, u32[]{:S(2)}) collective-permute-start(bf16[144,512]{1,0:T(8,128)(2,1)S(1)} %get-tuple-element.148), channel_id=1, source_target_pairs={{0,16},{2,18},{4,20},{6,22},{8,24},{10,26},{12,28},{14,30},{16,0},... | collective-permute-start | bytes 442376 | tf_op jit(solution)/shard_map/ppermute | solution.py:677
  150.6 21.2 %shard_map.237 = (bf16[2048,256]{1,0:T(8,128)(2,1)S(1)}, bf16[2048,256]{1,0:T(8,128)(2,1)S(1)}, bf16[2048,256]{1,0:T(8,128)(2,1)S(1)}) custom-call(s32[24]{0:T(128)S(1)} %get-tuple-element.207.sc, bf16[2048,256]{1,0:T(8,128)(2,1)S(1)} %copy-done.40, bf16[1024,256]{1,0:T(8,128)(2,1)S(1)} %get-tuple-element.138.refs_1_, ...), custom_call_target="tpu_custom_call" | custom-call | flops 2684354560 | bytes 6291456 | tf_op jit(solution)/shard_map/pallas_call | solution.py:236
  172.9 3.0 %shard_map.239 = (f32[1024,512]{1,0:T(8,128)S(1)}, bf16[1024,512]{1,0:T(8,128)(2,1)S(1)}) custom-call(s32[4]{0:T(128)S(1)} %and_select_fusion.sc, bf16[2048,256]{1,0:T(8,128)(2,1)S(1)} %get-tuple-element.151.refs_0_, bf16[2048,256]{1,0:T(8,128)(2,1)S(1)} %get-tuple-element.152.refs_1_, bf16[2048,256]{1,0:T(8,128)(2,1)S(1)} %get-tuple-element.153.refs_2_, ...), custom_call_target="tpu_custom_call" | custom-call | flops 1 | bytes 1 | tf_op jit(solution)/shard_map/pallas_call | solution.py:518
  177.9 58.6 %shard_map.238 = (bf16[1024,512]{1,0:T(8,128)(2,1)S(1)}, bf16[1280,512]{1,0:T(8,128)(2,1)S(1)}, bf16[512,256]{1,0:T(8,128)(2,1)S(1)}, bf16[512,256]{1,0:T(8,128)...) custom-call(bf16[64,512]{1,0:T(8,128)(2,1)S(1)} %slice.47.refs_0_, ...), custom_call_target="tpu_custom_call" | custom-call | tf_op jit(solution)/shard_map/pallas_call | solution.py:649
  237.1 5.0 %shard_map.240 = (f32[3,512,256]{2,1,0:T(8,128)}, f32[256,512]{1,0:T(8,128)}, f32[512,256]{1,0:T(8,128)}, f32[2,512,256]{2,1,0:T(8,128)}, f32[1024,512]{1,0:T(8,...) custom-call(bf16[512,256]{1,0:T(8,128)(2,1)S(1)} %get-tuple-element.159.refs_0_, ...), custom_call_target="tpu_custom_call" | custom-call | bytes 12582912 | tf_op jit(solution)/shard_map/pallas_call | solution.py:715
  (202 shorter events, 29.8 us)
Async XLA Ops:
  27.8 3.2 %collective-permute-start = (bf16[1024,256]{1,0:T(8,128)(2,1)S(1)}, bf16[1024,256]{1,0:T(8,128)(2,1)S(1)}, u32[]{:S(2)}, u32[]{:S(2)}) collective-permute-start(bf16[1024,256]{1,0:T(8,128)(2,1)S(1)} %get-tuple-element.101.refs_4_), channel_id=1, source_target_pairs={{0,1},{1,0},{2,3},{3,2},{4,5},{5,4},{6,7},{7,6},{8,9},{9,8},{10,11... | collective-permute-start | bytes 1572872 | tf_op jit(solution)/shard_map/ppermute | solution.py:762
  29.1 1.5 collective-permute-start.1
  29.3 1.8 collective-permute-start.2
  37.1 5.2 %collective-permute-start.3 = (bf16[1024,256]{1,0:T(8,128)(2,1)}, bf16[1024,256]{1,0:T(8,128)(2,1)}, u32[]{:S(2)}, u32[]{:S(2)}) collective-permute-start(bf16[1024,256]{1,0:T(8,128)(2,1)} %get-tuple-element.103), channel_id=1, source_target_pairs={{0,1},{1,0},{2,3},{3,2},{4,5},{5,4},{6,7},{7,6},{8,9},{9,8},{10,11... | collective-permute-start | bytes 1572872 | tf_op jit(solution)/shard_map/ppermute | solution.py:762
  37.2 19.5 %collective-permute-start.6 = (bf16[1024,512]{1,0:T(8,128)(2,1)}, bf16[1024,512]{1,0:T(8,128)(2,1)}, u32[]{:S(2)}, u32[]{:S(2)}) collective-permute-start(bf16[1024,512]{1,0:T(8,128)(2,1)} %refs_6_.1), channel_id=1, source_target_pairs={{0,1},{1,0},{2,3},{3,2},{4,5},{5,4},{6,7},{7,6},{8,9},{9,8},{10,11... | collective-permute-start | bytes 3145736 | tf_op jit(solution)/shard_map/ppermute | solution.py:756
  37.6 19.1 %collective-permute-start.7 = (bf16[1024,512]{1,0:T(8,128)(2,1)}, bf16[1024,512]{1,0:T(8,128)(2,1)}, u32[]{:S(2)}, u32[]{:S(2)}) collective-permute-start(bf16[1024,512]{1,0:T(8,128)(2,1)} %refs_8_.1), channel_id=1, source_target_pairs={{0,1},{1,0},{2,3},{3,2},{4,5},{5,4},{6,7},{7,6},{8,9},{9,8},{10,11... | collective-permute-start | bytes 3145736 | tf_op jit(solution)/shard_map/ppermute | solution.py:756
  37.7 18.9 %collective-permute-start.5 = (bf16[256,512]{1,0:T(8,128)(2,1)}, bf16[256,512]{1,0:T(8,128)(2,1)}, u32[]{:S(2)}, u32[]{:S(2)}) collective-permute-start(bf16[256,512]{1,0:T(8,128)(2,1)} %refs_4_.2), channel_id=1, source_target_pairs={{0,1},{1,0},{2,3},{3,2},{4,5},{5,4},{6,7},{7,6},{8,9},{9,8},{10,11... | collective-permute-start | bytes 786440 | tf_op jit(solution)/shard_map/ppermute | solution.py:756
  54.5 2.3 collective-permute-start.4
  82.0 6.3 %collective-permute-start.9 = (bf16[1024,512]{1,0:T(8,128)(2,1)S(1)}, bf16[1024,512]{1,0:T(8,128)(2,1)S(1)}, u32[]{:S(2)}, u32[]{:S(2)}) collective-permute-start(bf16[1024,512]{1,0:T(8,128)(2,1)S(1)} %convolution_convert_fusion.2), channel_id=1, source_target_pairs={{0,1},{1,0},{2,3},{3,2},{4,5},{5,4},{6,7},{7,6},{8,9},{9,8},{10,11... | collective-permute-start | bytes 3145736 | tf_op jit(solution)/shard_map/ppermute | solution.py:762
  83.7 4.1 %collective-permute-start.10 = (bf16[1024,512]{1,0:T(8,128)(2,1)S(1)}, bf16[1024,512]{1,0:T(8,128)(2,1)S(1)}, u32[]{:S(2)}, u32[]{:S(2)}) collective-permute-start(bf16[1024,512]{1,0:T(8,128)(2,1)S(1)} %convolution_convert_fusion), channel_id=1, source_target_pairs={{0,1},{1,0},{2,3},{3,2},{4,5},{5,4},{6,7},{7,6},{8,9},{9,8},{10,11... | collective-permute-start | bytes 3145736 | tf_op jit(solution)/shard_map/ppermute | solution.py:762
  85.4 1.9 collective-permute-start.11
  87.2 2.0 collective-permute-start.8
  90.2 19.9 %copy-start.24 = (bf16[1024,512]{1,0:T(8,128)(2,1)S(1)}, bf16[1024,512]{1,0:T(8,128)(2,1)}, u32[]{:S(2)}) copy-start(bf16[1024,512]{1,0:T(8,128)(2,1)} %x_ref.3) | copy-start | bytes 3145732
  105.5 5.7 %collective-permute-start.24 = (bf16[512,512]{1,0:T(8,128)(2,1)S(1)}, bf16[512,512]{1,0:T(8,128)(2,1)S(1)}, u32[]{:S(2)}, u32[]{:S(2)}) collective-permute-start(bf16[512,512]{1,0:T(8,128)(2,1)S(1)} %get-tuple-element.173), channel_id=1, source_target_pairs={{0,1},{1,0},{2,3},{3,2},{4,5},{5,4},{6,7},{7,6},{8,9},{9,8},{10,11... | collective-permute-start | bytes 1572872 | tf_op jit(solution)/shard_map/ppermute | solution.py:762
  105.9 16.2 %collective-permute-start.13 = (bf16[4,144,512]{2,1,0:T(8,128)(2,1)S(1)}, bf16[4,144,512]{2,1,0:T(8,128)(2,1)S(1)}, u32[]{:S(2)}, u32[]{:S(2)}) collective-permute-start(bf16[4,144,512]{2,1,0:T(8,128)(2,1)S(1)} %pad_maximum_fusion.1), channel_id=1, source_target_pairs={{0,2},{2,0},{4,6},{6,4},{8,10},{10,8},{12,14},{14,12},{16,18},{18,... | collective-permute-start | bytes 1769480 | tf_op jit(solution)/shard_map/ppermute | solution.py:677
  108.0 28.3 %collective-permute-start.14 = (bf16[4,144,512]{2,1,0:T(8,128)(2,1)S(1)}, bf16[4,144,512]{2,1,0:T(8,128)(2,1)S(1)}, u32[]{:S(2)}, u32[]{:S(2)}) collective-permute-start(bf16[4,144,512]{2,1,0:T(8,128)(2,1)S(1)} %pad_maximum_fusion.2), channel_id=1, source_target_pairs={{0,4},{2,6},{4,0},{6,2},{8,12},{10,14},{12,8},{14,10},{16,20},{18,... | collective-permute-start | bytes 1769480 | tf_op jit(solution)/shard_map/ppermute | solution.py:677
  110.0 26.2 %collective-permute-start.15 = (bf16[4,144,512]{2,1,0:T(8,128)(2,1)S(1)}, bf16[4,144,512]{2,1,0:T(8,128)(2,1)S(1)}, u32[]{:S(2)}, u32[]{:S(2)}) collective-permute-start(bf16[4,144,512]{2,1,0:T(8,128)(2,1)S(1)} %pad_maximum_fusion.3), channel_id=1, source_target_pairs={{0,6},{2,4},{4,2},{6,0},{8,14},{10,12},{12,10},{14,8},{16,22},{18,... | collective-permute-start | bytes 1769480 | tf_op jit(solution)/shard_map/ppermute | solution.py:677
  110.6 26.0 %collective-permute-start.12 = (bf16[1024,256]{1,0:T(8,128)(2,1)S(1)}, bf16[1024,256]{1,0:T(8,128)(2,1)S(1)}, u32[]{:S(2)}, u32[]{:S(2)}) collective-permute-start(bf16[1024,256]{1,0:T(8,128)(2,1)S(1)} %get-tuple-element.125), channel_id=1, source_target_pairs={{0,1},{1,0},{2,3},{3,2},{4,5},{5,4},{6,7},{7,6},{8,9},{9,8},{10,11... | collective-permute-start | bytes 1572872 | tf_op jit(solution)/shard_map/ppermute | solution.py:762
  112.3 24.7 %copy-start.3 = (f32[1024,512]{1,0:T(8,128)S(1)}, f32[1024,512]{1,0:T(8,128)}, u32[]{:S(2)}) copy-start(f32[1024,512]{1,0:T(8,128)} %copy-done.2) | copy-start | bytes 6291460
  112.3 24.7 %copy-start.5 = (bf16[256,512]{1,0:T(8,128)(2,1)S(1)}, bf16[256,512]{1,0:T(8,128)(2,1)}, u32[]{:S(2)}) copy-start(bf16[256,512]{1,0:T(8,128)(2,1)} %refs_4_.3) | copy-start | bytes 786436
  112.3 24.7 %copy-start.7 = (bf16[512,256]{1,0:T(8,128)(2,1)S(1)}, bf16[512,256]{1,0:T(8,128)(2,1)}, u32[]{:S(2)}) copy-start(bf16[512,256]{1,0:T(8,128)(2,1)} %refs_2_.1) | copy-start | bytes 786436
  112.3 24.8 %copy-start.9 = (bf16[256,512]{1,0:T(8,128)(2,1)S(1)}, bf16[256,512]{1,0:T(8,128)(2,1)}, u32[]{:S(2)}) copy-start(bf16[256,512]{1,0:T(8,128)(2,1)} %copy-done.8) | copy-start | bytes 786436
  112.4 24.8 %copy-start.11 = (bf16[512,256]{1,0:T(8,128)(2,1)S(1)}, bf16[512,256]{1,0:T(8,128)(2,1)}, u32[]{:S(2)}) copy-start(bf16[512,256]{1,0:T(8,128)(2,1)} %copy-done.10) | copy-start | bytes 786436
  112.4 24.8 %copy-start.19 = (f32[1024,1]{1,0:T(8,128)S(1)}, f32[1024,1]{1,0:T(8,128)}, u32[]{:S(2)}) copy-start(f32[1024,1]{1,0:T(8,128)} %copy-done.18) | copy-start | bytes 12292
  139.8 3.4 %collective-permute-start.16 = (bf16[1024,256]{1,0:T(8,128)(2,1)S(1)}, bf16[1024,256]{1,0:T(8,128)(2,1)S(1)}, u32[]{:S(2)}, u32[]{:S(2)}) collective-permute-start(bf16[1024,256]{1,0:T(8,128)(2,1)S(1)} %get-tuple-element.136), channel_id=1, source_target_pairs={{0,1},{1,0},{2,3},{3,2},{4,5},{5,4},{6,7},{7,6},{8,9},{9,8},{10,11... | collective-permute-start | bytes 1572872 | tf_op jit(solution)/shard_map/ppermute | solution.py:762
  140.0 1.8 collective-permute-start.22
  140.5 1.7 collective-permute-start.21
  141.1 1.7 collective-permute-start.20
  143.2 28.6 %collective-permute-start.17 = (bf16[144,512]{1,0:T(8,128)(2,1)S(1)}, bf16[144,512]{1,0:T(8,128)(2,1)S(1)}, u32[]{:S(2)}, u32[]{:S(2)}) collective-permute-start(bf16[144,512]{1,0:T(8,128)(2,1)S(1)} %get-tuple-element.147), channel_id=1, source_target_pairs={{0,8},{2,10},{4,12},{6,14},{8,0},{10,2},{12,4},{14,6},{16,24},{18,... | collective-permute-start | bytes 442376 | tf_op jit(solution)/shard_map/ppermute | solution.py:677
  146.5 25.3 %collective-permute-start.18 = (bf16[144,512]{1,0:T(8,128)(2,1)S(1)}, bf16[144,512]{1,0:T(8,128)(2,1)S(1)}, u32[]{:S(2)}, u32[]{:S(2)}) collective-permute-start(bf16[144,512]{1,0:T(8,128)(2,1)S(1)} %get-tuple-element.148), channel_id=1, source_target_pairs={{0,16},{2,18},{4,20},{6,22},{8,24},{10,26},{12,28},{14,30},{16,0},... | collective-permute-start | bytes 442376 | tf_op jit(solution)/shard_map/ppermute | solution.py:677
  150.6 21.3 %collective-permute-start.19 = (bf16[144,512]{1,0:T(8,128)(2,1)S(1)}, bf16[144,512]{1,0:T(8,128)(2,1)S(1)}, u32[]{:S(2)}, u32[]{:S(2)}) collective-permute-start(bf16[144,512]{1,0:T(8,128)(2,1)S(1)} %get-tuple-element.149), channel_id=1, source_target_pairs={{0,24},{2,26},{4,28},{6,30},{8,16},{10,18},{12,20},{14,22},{16,8},... | collective-permute-start | bytes 442376 | tf_op jit(solution)/shard_map/ppermute | solution.py:677
  175.9 61.2 %collective-permute-start.23 = (bf16[1024,512]{1,0:T(8,128)(2,1)S(1)}, bf16[1024,512]{1,0:T(8,128)(2,1)S(1)}, u32[]{:S(2)}, u32[]{:S(2)}) collective-permute-start(bf16[1024,512]{1,0:T(8,128)(2,1)S(1)} %get-tuple-element.170), channel_id=1, source_target_pairs={{0,1},{1,0},{2,3},{3,2},{4,5},{5,4},{6,7},{7,6},{8,9},{9,8},{10,11... | collective-permute-start | bytes 3145736 | tf_op jit(solution)/shard_map/ppermute | solution.py:762
  (41 other events, 242.8 us)
